TPU v7x, 32 devices: a whole 2x2x4 slice. The times are simulated.
32 devices in a mesh: site: 2 (over y), gx: 4 (over z), gy: 2 (over x), comp: 2 (over core).
Axes of the slice: x: 2, y: 2, z: 4, core: 2. Of those that a mesh axis runs over, the one named last changes fastest.
Arguments:
- displacement: float32 [2, 3, 32, 64, 128], P('comp', None, ('site', 'gx'), 'gy'), parts along dimension 2, may hold values from -6 to 6
- previous: float32 [2, 3, 32, 64, 128], P('comp', None, ('site', 'gx'), 'gy'), parts along dimension 2, may hold values from -6 to 6
- first_lame: float32 [32, 64, 128], P(('site', 'gx'), 'gy'), parts along dimension 0, may hold values from 0.5 to 2
- shear_modulus: float32 [32, 64, 128], P(('site', 'gx'), 'gy'), parts along dimension 0, may hold values from 0.5 to 2
- buoyancy: float32 [32, 64, 128], P(('site', 'gx'), 'gy'), parts along dimension 0, may hold values from 0.5 to 2
- tile_column: int32 [2048], P(('site', 'gx', 'gy')), parts along dimension 0, may hold values from 0 to 127
- rupture_tiles: int32 [256, 16], P(('site', 'gx', 'gy')), parts along dimension 0, may hold values from 0 to 1023, as said below
- slip_offsets: int32 [256, 16], P(('site', 'gx', 'gy')), parts along dimension 0, may hold values from 0 to 3
- slip_panels: bfloat16 [256, 16, 6, 128], P(('site', 'gx', 'gy')), parts along dimension 0, may hold values from -0.0546875 to 0.0546875
Outputs:
- final_displacement: float32 [2, 3, 32, 64, 128], P('comp', None, ('site', 'gx'), 'gy'), parts along dimension 2
- synthetics: float32 [2, 256, 4], P('comp', ('site', 'gx', 'gy')), parts along dimension 1
There are 2 independent parts, one for each index of `site`. A program takes and returns all parts, laid end to end along the dimension named above; each array names one. Nothing has to cross between parts.
Inputs may be any that keep to these rules, and one draw needn't show every extreme that they name: `rupture_tiles`: of the 16 x 16 entries of the ruptures r with the same r // 16, between 1 and 64 name tiles t with the same t // 128, for every such device; in each such group some device is named exactly 64 times. Entries may repeat; each group names tile 0 and tile 1024 - 1.
All inputs are finite; a program needn't handle non-finite values.
Results may differ from a plain program's by a relative error of at most 0.0027.
Values may be sent and summed in bfloat16 or wider, within the bound.
No kernel may reach another device: no remote copies, remote signals or barrier semaphores. Data moves between devices by JAX's collectives and lax.ppermute only.
A program may use at most 64 MiB of HBM per device.

v0:
```python
import jax
import jax.numpy as jnp
from jax import lax
from jax.sharding import PartitionSpec as P

STEPS = 4


time_step = 0.12


def padded(value, sides, width):
    for axis, dim in sides:
        devices, length = (lax.axis_size(axis), value.shape[dim])
        up = [(i, (i + 1) % devices) for i in range(devices - 1)]
        down = [(j, i) for i, j in up]
        last = lax.slice_in_dim(value, length - width, length, axis=dim)
        initial = lax.slice_in_dim(value, 0, width, axis=dim)
        before = lax.ppermute(last, axis, up)
        after = lax.ppermute(initial, axis, down)
        value = jnp.concatenate([before, value, after], axis=dim)
    return value


def exchange_faces(block):
    return padded(block, (("gx", 1), ("gy", 2)), 1)


def deliver(payload):
    return lax.all_to_all(payload, ("gx", "gy"), split_axis=0, concat_axis=0, tiled=True)


def strain_region(extended, rows_local, cols_local):
    base = extended[:, : rows_local + 1, : cols_local + 1]
    along_first = extended[:, 1 : rows_local + 2, : cols_local + 1] - base
    along_second = extended[:, : rows_local + 1, 1 : cols_local + 2] - base
    along_depth = jnp.concatenate([base[..., 1:], jnp.zeros_like(base[..., :1])], axis=3) - base
    gradients = [
        [along_first[comp_index], along_second[comp_index], along_depth[comp_index]]
        for comp_index in range(3)
    ]
    return [
        gradients[0][0],
        gradients[1][1],
        gradients[2][2],
        0.5 * (gradients[0][1] + gradients[1][0]),
        0.5 * (gradients[0][2] + gradients[2][0]),
        0.5 * (gradients[1][2] + gradients[2][1]),
    ]


def stress_region(strains, first_lame, shear_modulus):
    trace = strains[0] + strains[1] + strains[2]
    twice = 2.0 * shear_modulus
    return [
        first_lame * trace + twice * strains[0],
        first_lame * trace + twice * strains[1],
        first_lame * trace + twice * strains[2],
        twice * strains[3],
        twice * strains[4],
        twice * strains[5],
    ]


def lower_first(values):
    return values[1:, 1:] - values[:-1, 1:]


def lower_second(values):
    return values[1:, 1:] - values[1:, :-1]


def lower_depth(values):
    inner = values[1:, 1:]
    return inner - jnp.concatenate([jnp.zeros_like(inner[..., :1]), inner[..., :-1]], axis=2)


def force_terms(stresses):
    return [
        lower_first(stresses[0]) + lower_second(stresses[3]) + lower_depth(stresses[4]),
        lower_first(stresses[3]) + lower_second(stresses[1]) + lower_depth(stresses[5]),
        lower_first(stresses[4]) + lower_second(stresses[5]) + lower_depth(stresses[2]),
    ]


def body(
    displacement,
    previous,
    first_lame,
    shear_modulus,
    buoyancy,
    tile_column,
    rupture_tiles,
    slip_offsets,
    slip_panels,
):
    current = displacement[0]
    earlier = previous[0]
    rows_local, cols_local, depth_points = shear_modulus.shape
    tile_slots = tile_column.shape[0]
    rupture_local, list_length = rupture_tiles.shape
    entries = rupture_local * list_length
    owners = lax.axis_size(("gx", "gy"))
    capacity = 2 * entries // owners
    flat_tiles = rupture_tiles.reshape(entries)
    source = flat_tiles // tile_slots
    slot_index = flat_tiles % tile_slots
    one_hot = (source[:, None] == jnp.arange(owners, dtype=jnp.int32)[None, :]).astype(jnp.int32)
    slot_rank = jnp.sum((jnp.cumsum(one_hot, axis=0) - one_hot) * one_hot, axis=1)
    requests = jnp.zeros((owners, capacity), jnp.int32).at[source, slot_rank].set(slot_index)
    wanted = lax.all_to_all(requests, ("gx", "gy"), split_axis=0, concat_axis=0, tiled=True)
    slip_flat = slip_panels.reshape(entries, 6 * depth_points)
    step_scale = time_step * time_step * buoyancy
    coefficients = None
    records = []
    for instant in range(STEPS):
        if instant == 0:
            joined = exchange_faces(
                jnp.concatenate([current, jnp.stack([first_lame, shear_modulus])], axis=0)
            )
            extended = joined[:3]
            coefficients = joined[3:, : rows_local + 1, : cols_local + 1]
        else:
            extended = exchange_faces(current)
        strains = strain_region(extended, rows_local, cols_local)
        stresses = stress_region(strains, coefficients[0], coefficients[1])
        forces = force_terms(stresses)
        updated = jnp.stack(
            [
                2.0 * current[comp_index] - earlier[comp_index] + step_scale * forces[comp_index]
                for comp_index in range(3)
            ]
        )
        own_strains = [strain[1:, 1:] for strain in strains]
        earlier, current = (current, updated)
        tile_strain = jnp.stack(
            [
                strain.reshape(rows_local * cols_local, depth_points)[tile_column]
                for strain in own_strains
            ],
            axis=1,
        )
        tile_strain = tile_strain.astype(jnp.bfloat16)
        records.append(tile_strain)
    stacked = jnp.stack(records, axis=1)
    arrived = deliver(stacked[wanted])
    picked = arrived[source, slot_rank].reshape(entries, STEPS, 6 * depth_points)
    response = jnp.einsum("kmq,kq->km", picked, slip_flat, preferred_element_type=jnp.float32)
    lag_table = (
        jnp.arange(STEPS, dtype=jnp.int32)[None, None, :]
        - jnp.arange(STEPS, dtype=jnp.int32)[None, :, None]
    )
    select = (slip_offsets.reshape(entries)[:, None, None] == lag_table).astype(jnp.float32)
    delayed = jnp.sum(response[:, :, None] * select, axis=1)
    synthetic = delayed.reshape(rupture_local, list_length, STEPS).sum(axis=1)
    return (current[None], synthetic[None])


def solution(mesh):
    in_specs = (
        P("comp", None, ("site", "gx"), "gy", None),
        P("comp", None, ("site", "gx"), "gy", None),
        P(("site", "gx"), "gy", None),
        P(("site", "gx"), "gy", None),
        P(("site", "gx"), "gy", None),
        P(("site", "gx", "gy")),
        P(("site", "gx", "gy"), None),
        P(("site", "gx", "gy"), None),
        P(("site", "gx", "gy"), None, None, None),
    )
    out_specs = (P("comp", None, ("site", "gx"), "gy", None), P("comp", ("site", "gx", "gy"), None))
    return jax.shard_map(body, mesh=mesh, in_specs=in_specs, out_specs=out_specs, check_vma=False)
```

profile of v0, /device:TPU:0, one launch (start us, length us, event | category | flops | bytes accessed | tf_op | source)
XLA Modules:
  0.0 211.2 jit_solution(13981393707768263324)
XLA Ops:
  0.7 1.0 pad_maximum_fusion.23
  1.6 1.3 collective-permute-start.1
  2.9 5.6 %collective-permute-start = (f32[5,1,32,128]{3,2,1,0:T(8,128)S(1)}, f32[5,1,32,128]{3,2,1,0:T(8,128)S(1)}, u32[]{:S(2)}, u32[]{:S(2)}) collective-permute-start(f32[5,1,32,128]{3,2,1,0:T(8,128)S(1)} %get-tuple-element.80), channel_id=1, source_target_pairs={{0,4},{4,8},{8,12},{1,5},{5,9},{9,13},{2,6},{6,10},{10,14},{3,7},{... | collective-permute-start | bytes 245768 | tf_op jit(solution)/shard_map/ppermute | solution.py:19
  8.5 0.8 reshape.708
  9.3 0.8 reshape.707
  10.0 0.8 reshape.706
  11.8 0.6 broadcast.233
  12.4 38.7 %scatter_fusion = s32[8,64]{1,0:T(8,128)} fusion(s32[8,64]{1,0:T(8,128)} %broadcast.233, s32[256]{0:T(256)S(1)} %bitcast.283, s32[256]{0:T(256)S(1)} %get-tuple-element.104), kind=kCustom, calls=%fused_computation.26 | custom fusion | bytes 5120 | tf_op jit(solution)/shard_map/scatter | solution.py:110
  51.1 5.2 %all-to-all-start = ((s32[8,1,64]{2,1,0:T(1,128)}), s32[8,1,64]{2,1,0:T(1,128)S(1)}, u32[]{:S(2)}, u32[]{:S(2)}) async-start(s32[8,1,64]{2,1,0:T(1,128)} %bitcast.102), calls=%async_computation | async-start | bytes 8192 | tf_op jit(solution)/shard_map/all_to_all | solution.py:111
  56.3 0.7 compare_select_fusion.3
  57.0 5.7 %all-to-all-done = s32[8,1,64]{2,1,0:T(1,128)S(1)} async-done(((s32[8,1,64]{2,1,0:T(1,128)}), s32[8,1,64]{2,1,0:T(1,128)S(1)}, u32[]{:S(2)}, u32[]{:S(2)}) %all-to-all-start) | async-done | bytes 2080 | tf_op jit(solution)/shard_map/all_to_all | solution.py:111
  62.8 0.9 pad_maximum_fusion.33
  63.7 2.5 %collective-permute-start.2 = (f32[5,6,1,128]{3,2,1,0:T(1,128)S(1)}, f32[5,6,1,128]{3,2,1,0:T(1,128)S(1)}, u32[]{:S(2)}, u32[]{:S(2)}) collective-permute-start(f32[5,6,1,128]{3,2,1,0:T(1,128)S(1)} %get-tuple-element.62), channel_id=1, source_target_pairs={{0,2},{1,3},{4,6},{5,7},{8,10},{9,11},{12,14},{13,15},{16,18},{17,... | collective-permute-start | bytes 46088 | tf_op jit(solution)/shard_map/ppermute | solution.py:19
  66.2 1.3 collective-permute-start.3
  67.9 4.0 %collective-permute-done.3 = f32[5,6,1,128]{3,2,1,0:T(1,128)S(1)} collective-permute-done((f32[5,6,1,128]{3,2,1,0:T(1,128)S(1)}, f32[5,6,1,128]{3,2,1,0:T(1,128)S(1)}, u32[]{:S(2)}, u32[]{:S(2)}) %collective-permute-start.3) | collective-permute-done | bytes 15392 | tf_op jit(solution)/shard_map/ppermute | solution.py:20
  72.4 1.3 collective-permute-start.5
  73.7 4.5 %collective-permute-start.4 = (f32[3,1,32,128]{3,2,1,0:T(8,128)S(1)}, f32[3,1,32,128]{3,2,1,0:T(8,128)S(1)}, u32[]{:S(2)}, u32[]{:S(2)}) collective-permute-start(f32[3,1,32,128]{3,2,1,0:T(8,128)S(1)} %get-tuple-element.98), channel_id=1, source_target_pairs={{0,4},{4,8},{8,12},{1,5},{5,9},{9,13},{2,6},{6,10},{10,14},{3,7},{... | collective-permute-start | bytes 147464 | tf_op jit(solution)/shard_map/ppermute | solution.py:19
  78.3 0.7 gather_fusion
  79.0 0.7 gather_fusion.1
  79.7 0.7 gather_fusion.2
  80.5 0.7 gather_fusion.3
  81.2 0.7 gather_fusion.4
  82.0 0.7 gather_fusion.5
  82.7 1.6 collective-permute-start.6
  84.4 1.3 collective-permute-start.7
  85.9 4.0 %collective-permute-done.7 = f32[3,6,1,128]{3,2,1,0:T(1,128)S(1)} collective-permute-done((f32[3,6,1,128]{3,2,1,0:T(1,128)S(1)}, f32[3,6,1,128]{3,2,1,0:T(1,128)S(1)}, u32[]{:S(2)}, u32[]{:S(2)}) %collective-permute-start.7) | collective-permute-done | bytes 9248 | tf_op jit(solution)/shard_map/ppermute | solution.py:20
  90.5 1.3 collective-permute-start.9
  91.8 4.5 %collective-permute-start.8 = (f32[3,1,32,128]{3,2,1,0:T(8,128)S(1)}, f32[3,1,32,128]{3,2,1,0:T(8,128)S(1)}, u32[]{:S(2)}, u32[]{:S(2)}) collective-permute-start(f32[3,1,32,128]{3,2,1,0:T(8,128)S(1)} %get-tuple-element.96), channel_id=1, source_target_pairs={{0,4},{4,8},{8,12},{1,5},{5,9},{9,13},{2,6},{6,10},{10,14},{3,7},{... | collective-permute-start | bytes 147464 | tf_op jit(solution)/shard_map/ppermute | solution.py:19
  96.4 0.7 gather_fusion.6
  97.1 0.7 gather_fusion.7
  97.8 0.7 gather_fusion.8
  98.6 0.7 gather_fusion.9
  99.3 0.7 gather_fusion.10
  100.1 0.7 gather_fusion.11
  100.8 1.6 collective-permute-start.10
  102.5 1.3 collective-permute-start.11
  104.0 4.0 %collective-permute-done.11 = f32[3,6,1,128]{3,2,1,0:T(1,128)S(1)} collective-permute-done((f32[3,6,1,128]{3,2,1,0:T(1,128)S(1)}, f32[3,6,1,128]{3,2,1,0:T(1,128)S(1)}, u32[]{:S(2)}, u32[]{:S(2)}) %collective-permute-start.11) | collective-permute-done | bytes 9248 | tf_op jit(solution)/shard_map/ppermute | solution.py:20
  108.6 1.3 collective-permute-start.13
  109.9 4.5 %collective-permute-start.12 = (f32[3,1,32,128]{3,2,1,0:T(8,128)S(1)}, f32[3,1,32,128]{3,2,1,0:T(8,128)S(1)}, u32[]{:S(2)}, u32[]{:S(2)}) collective-permute-start(f32[3,1,32,128]{3,2,1,0:T(8,128)S(1)} %get-tuple-element.94), channel_id=1, source_target_pairs={{0,4},{4,8},{8,12},{1,5},{5,9},{9,13},{2,6},{6,10},{10,14},{3,7},{... | collective-permute-start | bytes 147464 | tf_op jit(solution)/shard_map/ppermute | solution.py:19
  114.4 0.7 gather_fusion.12
  115.2 0.7 gather_fusion.13
  115.9 0.7 gather_fusion.14
  116.6 0.7 gather_fusion.15
  117.4 0.7 gather_fusion.16
  118.1 0.7 gather_fusion.17
  118.9 1.6 collective-permute-start.14
  120.6 1.3 collective-permute-start.15
  122.1 4.0 %collective-permute-done.15 = f32[3,6,1,128]{3,2,1,0:T(1,128)S(1)} collective-permute-done((f32[3,6,1,128]{3,2,1,0:T(1,128)S(1)}, f32[3,6,1,128]{3,2,1,0:T(1,128)S(1)}, u32[]{:S(2)}, u32[]{:S(2)}) %collective-permute-start.15) | collective-permute-done | bytes 9248 | tf_op jit(solution)/shard_map/ppermute | solution.py:20
  126.3 0.7 gather_fusion.18
  127.1 0.7 gather_fusion.19
  127.8 0.7 gather_fusion.20
  128.5 0.7 gather_fusion.21
  129.3 0.7 gather_fusion.22
  130.0 0.7 gather_fusion.23
  130.9 0.6 copy.19
  131.5 4.9 %gather_fusion.24 = bf16[512,4,6,128]{3,1,2,0:T(4,128)(2,1)} fusion(bf16[128,4,6,128]{3,1,2,0:T(4,128)(2,1)S(1)} %copy.19, s32[1024]{0:T(1024)S(1)} %get-tuple-element.114), kind=kCustom, calls=%fused_computation.24 | custom fusion | bytes 6293504 | tf_op jit(solution)/shard_map/gather | solution.py:146
  136.3 4.8 %all-to-all-start.1 = ((bf16[8,64,4,6,128]{4,2,3,1,0:T(4,128)(2,1)}), bf16[8,64,4,6,128]{4,2,3,1,0:T(4,128)(2,1)}, u32[]{:S(2)}, u32[]{:S(2)}) async-start(bf16[8,64,4,6,128]{4,2,3,1,0:T(4,128)(2,1)} %bitcast.281), calls=%async_computation.1 | async-start | bytes 6291456 | tf_op jit(solution)/shard_map/all_to_all | solution.py:30
  141.3 1.1 copy.29
  142.9 0.7 maximum_bitcast_fusion
  143.6 59.9 %all-to-all-done.1 = bf16[8,64,4,6,128]{4,2,3,1,0:T(4,128)(2,1)} async-done(((bf16[8,64,4,6,128]{4,2,3,1,0:T(4,128)(2,1)}), bf16[8,64,4,6,128]{4,2,3,1,0:T(4,128)(2,1)}, u32[]{:S(2)}, u32[]{:S(2)}) %all-to-all-start.1) | async-done | bytes 3145760 | tf_op jit(solution)/shard_map/all_to_all | solution.py:30
  203.4 4.3 %gather_fusion.25 = bf16[256,4,6,128]{3,1,2,0:T(4,128)(2,1)S(1)} fusion(bf16[8,64,4,6,128]{4,2,3,1,0:T(4,128)(2,1)} %all-to-all-done.1, s32[256]{0:T(256)S(1)} %bitcast.282), kind=kCustom, calls=%fused_computation.25 | custom fusion | bytes 3147776 | tf_op jit(solution)/shard_map/gather | solution.py:147
  207.7 1.2 copy.28
  208.9 1.5 multiply_reduce_fusion
  210.5 0.7 reduce_sum.32
  (147 shorter events, 5.1 us)
Async XLA Ops:
  0.6 67.0 %copy-start.2 = (f32[4,32,128]{2,1,0:T(8,128)S(1)}, f32[4,32,128]{2,1,0:T(8,128)}, u32[]{:S(2)}) copy-start(f32[4,32,128]{2,1,0:T(8,128)} %param.12) | copy-start | bytes 196612
  0.6 67.0 %copy-start.3 = (f32[4,32,128]{2,1,0:T(8,128)S(1)}, f32[4,32,128]{2,1,0:T(8,128)}, u32[]{:S(2)}) copy-start(f32[4,32,128]{2,1,0:T(8,128)} %param.11) | copy-start | bytes 196612
  0.7 67.0 %copy-start = (f32[1,3,4,32,128]{4,3,2,1,0:T(8,128)S(1)}, f32[1,3,4,32,128]{4,3,2,1,0:T(8,128)}, u32[]{:S(2)}) copy-start(f32[1,3,4,32,128]{4,3,2,1,0:T(8,128)} %param.9) | copy-start | bytes 589828
  1.6 61.2 %collective-permute-start.1 = (f32[5,1,32,128]{3,2,1,0:T(8,128)S(1)}, f32[5,1,32,128]{3,2,1,0:T(8,128)S(1)}, u32[]{:S(2)}, u32[]{:S(2)}) collective-permute-start(f32[5,1,32,128]{3,2,1,0:T(8,128)S(1)} %get-tuple-element.81), channel_id=1, source_target_pairs={{4,0},{8,4},{12,8},{5,1},{9,5},{13,9},{6,2},{10,6},{14,10},{7,3},{... | collective-permute-start | bytes 245768 | tf_op jit(solution)/shard_map/ppermute | solution.py:20
  2.9 59.9 %collective-permute-start = (f32[5,1,32,128]{3,2,1,0:T(8,128)S(1)}, f32[5,1,32,128]{3,2,1,0:T(8,128)S(1)}, u32[]{:S(2)}, u32[]{:S(2)}) collective-permute-start(f32[5,1,32,128]{3,2,1,0:T(8,128)S(1)} %get-tuple-element.80), channel_id=1, source_target_pairs={{0,4},{4,8},{8,12},{1,5},{5,9},{9,13},{2,6},{6,10},{10,14},{3,7},{... | collective-permute-start | bytes 245768 | tf_op jit(solution)/shard_map/ppermute | solution.py:19
  51.1 11.6 %all-to-all-start = ((s32[8,1,64]{2,1,0:T(1,128)}), s32[8,1,64]{2,1,0:T(1,128)S(1)}, u32[]{:S(2)}, u32[]{:S(2)}) async-start(s32[8,1,64]{2,1,0:T(1,128)} %bitcast.102), calls=%async_computation | async-start | bytes 8192 | tf_op jit(solution)/shard_map/all_to_all | solution.py:111
  63.7 3.9 %collective-permute-start.2 = (f32[5,6,1,128]{3,2,1,0:T(1,128)S(1)}, f32[5,6,1,128]{3,2,1,0:T(1,128)S(1)}, u32[]{:S(2)}, u32[]{:S(2)}) collective-permute-start(f32[5,6,1,128]{3,2,1,0:T(1,128)S(1)} %get-tuple-element.62), channel_id=1, source_target_pairs={{0,2},{1,3},{4,6},{5,7},{8,10},{9,11},{12,14},{13,15},{16,18},{17,... | collective-permute-start | bytes 46088 | tf_op jit(solution)/shard_map/ppermute | solution.py:19
  66.2 5.6 %collective-permute-start.3 = (f32[5,6,1,128]{3,2,1,0:T(1,128)S(1)}, f32[5,6,1,128]{3,2,1,0:T(1,128)S(1)}, u32[]{:S(2)}, u32[]{:S(2)}) collective-permute-start(f32[5,6,1,128]{3,2,1,0:T(1,128)S(1)} %get-tuple-element.61), channel_id=1, source_target_pairs={{2,0},{3,1},{6,4},{7,5},{10,8},{11,9},{14,12},{15,13},{18,16},{19,... | collective-permute-start | bytes 46088 | tf_op jit(solution)/shard_map/ppermute | solution.py:20
  67.7 4.5 %copy-start.1 = (f32[4,32,128]{2,1,0:T(8,128)S(1)}, f32[4,32,128]{2,1,0:T(8,128)}, u32[]{:S(2)}) copy-start(f32[4,32,128]{2,1,0:T(8,128)} %param.13) | copy-start | bytes 196612
  67.7 4.5 %copy-start.5 = (f32[1,3,4,32,128]{4,3,2,1,0:T(8,128)S(1)}, f32[1,3,4,32,128]{4,3,2,1,0:T(8,128)}, u32[]{:S(2)}) copy-start(f32[1,3,4,32,128]{4,3,2,1,0:T(8,128)} %param.10) | copy-start | bytes 589828
  72.4 10.3 %collective-permute-start.5 = (f32[3,1,32,128]{3,2,1,0:T(8,128)S(1)}, f32[3,1,32,128]{3,2,1,0:T(8,128)S(1)}, u32[]{:S(2)}, u32[]{:S(2)}) collective-permute-start(f32[3,1,32,128]{3,2,1,0:T(8,128)S(1)} %get-tuple-element.99), channel_id=1, source_target_pairs={{4,0},{8,4},{12,8},{5,1},{9,5},{13,9},{6,2},{10,6},{14,10},{7,3},{... | collective-permute-start | bytes 147464 | tf_op jit(solution)/shard_map/ppermute | solution.py:20
  73.7 9.0 %collective-permute-start.4 = (f32[3,1,32,128]{3,2,1,0:T(8,128)S(1)}, f32[3,1,32,128]{3,2,1,0:T(8,128)S(1)}, u32[]{:S(2)}, u32[]{:S(2)}) collective-permute-start(f32[3,1,32,128]{3,2,1,0:T(8,128)S(1)} %get-tuple-element.98), channel_id=1, source_target_pairs={{0,4},{4,8},{8,12},{1,5},{5,9},{9,13},{2,6},{6,10},{10,14},{3,7},{... | collective-permute-start | bytes 147464 | tf_op jit(solution)/shard_map/ppermute | solution.py:19
  82.7 3.0 %collective-permute-start.6 = (f32[3,6,1,128]{3,2,1,0:T(1,128)S(1)}, f32[3,6,1,128]{3,2,1,0:T(1,128)S(1)}, u32[]{:S(2)}, u32[]{:S(2)}) collective-permute-start(f32[3,6,1,128]{3,2,1,0:T(1,128)S(1)} %get-tuple-element.87), channel_id=1, source_target_pairs={{0,2},{1,3},{4,6},{5,7},{8,10},{9,11},{12,14},{13,15},{16,18},{17,... | collective-permute-start | bytes 27656 | tf_op jit(solution)/shard_map/ppermute | solution.py:19
  84.4 5.6 %collective-permute-start.7 = (f32[3,6,1,128]{3,2,1,0:T(1,128)S(1)}, f32[3,6,1,128]{3,2,1,0:T(1,128)S(1)}, u32[]{:S(2)}, u32[]{:S(2)}) collective-permute-start(f32[3,6,1,128]{3,2,1,0:T(1,128)S(1)} %get-tuple-element.86), channel_id=1, source_target_pairs={{2,0},{3,1},{6,4},{7,5},{10,8},{11,9},{14,12},{15,13},{18,16},{19,... | collective-permute-start | bytes 27656 | tf_op jit(solution)/shard_map/ppermute | solution.py:20
  90.5 10.3 %collective-permute-start.9 = (f32[3,1,32,128]{3,2,1,0:T(8,128)S(1)}, f32[3,1,32,128]{3,2,1,0:T(8,128)S(1)}, u32[]{:S(2)}, u32[]{:S(2)}) collective-permute-start(f32[3,1,32,128]{3,2,1,0:T(8,128)S(1)} %get-tuple-element.97), channel_id=1, source_target_pairs={{4,0},{8,4},{12,8},{5,1},{9,5},{13,9},{6,2},{10,6},{14,10},{7,3},{... | collective-permute-start | bytes 147464 | tf_op jit(solution)/shard_map/ppermute | solution.py:20
  91.8 9.0 %collective-permute-start.8 = (f32[3,1,32,128]{3,2,1,0:T(8,128)S(1)}, f32[3,1,32,128]{3,2,1,0:T(8,128)S(1)}, u32[]{:S(2)}, u32[]{:S(2)}) collective-permute-start(f32[3,1,32,128]{3,2,1,0:T(8,128)S(1)} %get-tuple-element.96), channel_id=1, source_target_pairs={{0,4},{4,8},{8,12},{1,5},{5,9},{9,13},{2,6},{6,10},{10,14},{3,7},{... | collective-permute-start | bytes 147464 | tf_op jit(solution)/shard_map/ppermute | solution.py:19
  100.8 3.0 %collective-permute-start.10 = (f32[3,6,1,128]{3,2,1,0:T(1,128)S(1)}, f32[3,6,1,128]{3,2,1,0:T(1,128)S(1)}, u32[]{:S(2)}, u32[]{:S(2)}) collective-permute-start(f32[3,6,1,128]{3,2,1,0:T(1,128)S(1)} %get-tuple-element.85), channel_id=1, source_target_pairs={{0,2},{1,3},{4,6},{5,7},{8,10},{9,11},{12,14},{13,15},{16,18},{17,... | collective-permute-start | bytes 27656 | tf_op jit(solution)/shard_map/ppermute | solution.py:19
  102.5 5.6 %collective-permute-start.11 = (f32[3,6,1,128]{3,2,1,0:T(1,128)S(1)}, f32[3,6,1,128]{3,2,1,0:T(1,128)S(1)}, u32[]{:S(2)}, u32[]{:S(2)}) collective-permute-start(f32[3,6,1,128]{3,2,1,0:T(1,128)S(1)} %get-tuple-element.84), channel_id=1, source_target_pairs={{2,0},{3,1},{6,4},{7,5},{10,8},{11,9},{14,12},{15,13},{18,16},{19,... | collective-permute-start | bytes 27656 | tf_op jit(solution)/shard_map/ppermute | solution.py:20
  108.6 10.3 %collective-permute-start.13 = (f32[3,1,32,128]{3,2,1,0:T(8,128)S(1)}, f32[3,1,32,128]{3,2,1,0:T(8,128)S(1)}, u32[]{:S(2)}, u32[]{:S(2)}) collective-permute-start(f32[3,1,32,128]{3,2,1,0:T(8,128)S(1)} %get-tuple-element.95), channel_id=1, source_target_pairs={{4,0},{8,4},{12,8},{5,1},{9,5},{13,9},{6,2},{10,6},{14,10},{7,3},{... | collective-permute-start | bytes 147464 | tf_op jit(solution)/shard_map/ppermute | solution.py:20
  109.9 9.0 %collective-permute-start.12 = (f32[3,1,32,128]{3,2,1,0:T(8,128)S(1)}, f32[3,1,32,128]{3,2,1,0:T(8,128)S(1)}, u32[]{:S(2)}, u32[]{:S(2)}) collective-permute-start(f32[3,1,32,128]{3,2,1,0:T(8,128)S(1)} %get-tuple-element.94), channel_id=1, source_target_pairs={{0,4},{4,8},{8,12},{1,5},{5,9},{9,13},{2,6},{6,10},{10,14},{3,7},{... | collective-permute-start | bytes 147464 | tf_op jit(solution)/shard_map/ppermute | solution.py:19
  118.9 3.0 %collective-permute-start.14 = (f32[3,6,1,128]{3,2,1,0:T(1,128)S(1)}, f32[3,6,1,128]{3,2,1,0:T(1,128)S(1)}, u32[]{:S(2)}, u32[]{:S(2)}) collective-permute-start(f32[3,6,1,128]{3,2,1,0:T(1,128)S(1)} %get-tuple-element.83), channel_id=1, source_target_pairs={{0,2},{1,3},{4,6},{5,7},{8,10},{9,11},{12,14},{13,15},{16,18},{17,... | collective-permute-start | bytes 27656 | tf_op jit(solution)/shard_map/ppermute | solution.py:19
  120.6 5.6 %collective-permute-start.15 = (f32[3,6,1,128]{3,2,1,0:T(1,128)S(1)}, f32[3,6,1,128]{3,2,1,0:T(1,128)S(1)}, u32[]{:S(2)}, u32[]{:S(2)}) collective-permute-start(f32[3,6,1,128]{3,2,1,0:T(1,128)S(1)} %get-tuple-element.82), channel_id=1, source_target_pairs={{2,0},{3,1},{6,4},{7,5},{10,8},{11,9},{14,12},{15,13},{18,16},{19,... | collective-permute-start | bytes 27656 | tf_op jit(solution)/shard_map/ppermute | solution.py:20
  136.3 4.8 %copy-start.4 = (bf16[16,16,6,128]{3,1,2,0:T(8,128)(2,1)S(1)}, bf16[16,16,6,128]{3,1,2,0:T(8,128)(2,1)}, u32[]{:S(2)}) copy-start(bf16[16,16,6,128]{3,1,2,0:T(8,128)(2,1)} %param.17) | copy-start | bytes 1179652
  136.3 67.1 %all-to-all-start.1 = ((bf16[8,64,4,6,128]{4,2,3,1,0:T(4,128)(2,1)}), bf16[8,64,4,6,128]{4,2,3,1,0:T(4,128)(2,1)}, u32[]{:S(2)}, u32[]{:S(2)}) async-start(bf16[8,64,4,6,128]{4,2,3,1,0:T(4,128)(2,1)} %bitcast.281), calls=%async_computation.1 | async-start | bytes 6291456 | tf_op jit(solution)/shard_map/all_to_all | solution.py:30
  141.1 1.4 copy-start.6
where the time goes:
time: 213 us; the launch traced here: 211 us
  waiting for transfers between devices  81.9 us (38%)
  local copies, waits for them, and re-layouts  72.6 us (34%)
  starting transfers between devices  46.9 us (22%)
  other arithmetic  8.31 us (4%)
    all_to_all x1, waiting for transfers between devices, deliver(): lax.all_to_all(payload, ('gx', 'gy'), split_axis=0, concat_axis=0, tiled=...  59.9 us
    scatter x1, local copies, waits for them, and re-layouts, body(): jnp.zeros((owners, capacity), jnp.int32).at[source, slot_rank]  38.7 us
    ppermute x8, starting transfers between devices, padded(): before = lax.ppermute(last, axis, up)  26.6 us
    gather x24, local copies, waits for them, and re-layouts, body(): strain.reshape(rows_local * cols_local, depth_points)[tile_column]  17 us
    ppermute x8, waiting for transfers between devices, padded(): after = lax.ppermute(initial, axis, down)  16.1 us
    ppermute x8, starting transfers between devices, padded(): after = lax.ppermute(initial, axis, down)  10.3 us
    all_to_all x1, waiting for transfers between devices, body(): lax.all_to_all(requests, ('gx', 'gy'), split_axis=0, concat_axis=0, tiled...  5.73 us
    all_to_all x1, starting transfers between devices, body(): lax.all_to_all(requests, ('gx', 'gy'), split_axis=0, concat_axis=0, tiled...  5.23 us
  transfers between devices with their start and end apart: 18, of which 7 were waited for; matrix products, arithmetic and copies ran while one was open for 28% of the time, Pallas kernels for 0%

commit v1 on v0

v1 whole, which is shorter than its diff:
```python
import functools

import jax
import jax.numpy as jnp
from jax import lax
from jax.experimental import pallas as pl
from jax.experimental.pallas import tpu as pltpu
from jax.sharding import PartitionSpec as P

STEPS = 4
TIME_STEP = 0.12
LANES = 128
PAD = 8
OWNERS_AXES = ("gx", "gy")
NT = (((1,), (1,)), ((), ()))


def iota(shape, dim):
    return lax.broadcasted_iota(jnp.int32, shape, dim)


def owner_index():
    return lax.axis_index("gx") * lax.axis_size("gy") + lax.axis_index("gy")


def pack_kernel(owners, slots, ranks, tiles_ref, offsets_ref, panels_ref, out_ref, meta_ref):
    rows, cols = tiles_ref.shape
    entries = rows * cols
    core = lax.axis_index("comp")
    me = owner_index()
    tiles = tiles_ref[...]
    shift = slots.bit_length() - 1
    fields = jnp.concatenate([tiles >> shift, tiles & (slots - 1), offsets_ref[...]], axis=0)
    spread = (iota((cols, entries), 1) % cols == iota((cols, entries), 0)).astype(jnp.bfloat16)
    wide = jnp.dot(fields.astype(jnp.float32).astype(jnp.bfloat16), spread, preferred_element_type=jnp.float32)
    lane_row = iota((rows, entries), 1) // cols
    keep = lane_row == iota((rows, entries), 0)
    source, slot, offset = [
        jnp.sum(jnp.where(keep, wide[i * rows : (i + 1) * rows], 0.0), axis=0, keepdims=True) for i in range(3)
    ]
    record = (iota((1, entries), 1) // cols).astype(jnp.float32) * STEPS + offset
    chosen = source == iota((owners, entries), 0).astype(jnp.float32)
    before = (iota((entries, entries), 0) < iota((entries, entries), 1)).astype(jnp.bfloat16)
    counts = jnp.dot(chosen.astype(jnp.bfloat16), before, preferred_element_type=jnp.float32)
    rank = jnp.sum(jnp.where(chosen, counts, 0.0), axis=0, keepdims=True).astype(jnp.int32) - core * ranks
    mine = (rank >= 0) & (rank < ranks)
    place = jnp.where(mine, source.astype(jnp.int32) * ranks + rank, -1)
    sent = owners * ranks
    select = (iota((sent, entries), 0) == place).astype(jnp.bfloat16)
    blocks = out_ref.shape[0]
    length = sent // blocks
    for i in range(panels_ref.shape[0]):
        part = jnp.dot(select, panels_ref[i], preferred_element_type=jnp.float32).astype(jnp.bfloat16)
        out_ref[:, i * length : (i + 1) * length, :] = part.reshape(blocks, length, LANES)
    group = LANES // ranks
    lane = jnp.where(mine, rank + ranks * (me % group), -1)
    marks = (iota((LANES, entries), 0) == lane).astype(jnp.bfloat16)
    for k, value in enumerate((slot, record)):
        table = jnp.where(chosen, value, 0.0).astype(jnp.bfloat16)
        rows_out = lax.dot_general(table, marks, NT, preferred_element_type=jnp.float32).astype(jnp.bfloat16)
        meta_ref[k] = rows_out


def pack(owners, slots, ranks, tiles, offsets, panels):
    friendly = ranks % 16 == 0
    blocks = owners if friendly else 1
    sent = owners * ranks
    components = panels.shape[0]
    body, meta = pl.pallas_call(
        functools.partial(pack_kernel, owners, slots, ranks),
        out_shape=(
            jax.ShapeDtypeStruct((blocks, components * sent // blocks, LANES), jnp.bfloat16),
            jax.ShapeDtypeStruct((2, owners, LANES), jnp.bfloat16),
        ),
        in_specs=[pl.BlockSpec(memory_space=pltpu.VMEM)] * 3,
        out_specs=(pl.BlockSpec(memory_space=pltpu.VMEM),) * 2,
        name="pack",
    )(tiles, offsets, panels)
    if not friendly:
        body = body.reshape(components, owners, ranks, LANES).transpose(1, 0, 2, 3)
        body = body.reshape(owners, components * ranks, LANES)
    return jnp.concatenate([body, meta.transpose(1, 0, 2)], axis=1)


def unpack(owners, ranks, components, arrived):
    body = arrived[:, : components * ranks]
    meta = arrived[:, components * ranks :].transpose(1, 0, 2)
    if ranks % 16:
        body = body.reshape(owners, components, ranks, LANES).transpose(1, 0, 2, 3)
        body = body.reshape(1, components * owners * ranks, LANES)
    return body, meta


def shifted_up(value, dim):
    return pltpu.roll(value, value.shape[dim] - 1, dim)


def stencil_kernel(halo, merged, *refs):
    disp, prev, lam, mu, buoy, x_low, x_high = refs[:7]
    sides = refs[7:13] if not merged else refs[7:10] * 2
    out_ref, strain_ref = refs[-7:-5]
    wave, first, second, scale = refs[-5:-1]
    nx, ny, nz = lam.shape
    tall = ny + 2 * PAD
    gy = lax.axis_index("gy")
    own_x, own_y = pl.ds(halo, nx), pl.ds(PAD, ny)
    lows, highs = pl.ds(0, halo), pl.ds(halo + nx, halo)

    targets = [wave.at[0, i] for i in range(3)] + [wave.at[1, i] for i in range(3)] + [first, second, scale]
    owns = [disp[0, i] for i in range(3)] + [prev[0, i] for i in range(3)] + [lam[...], mu[...], buoy[...]]
    dt2 = TIME_STEP * TIME_STEP
    for f, (target, own) in enumerate(zip(targets, owns)):
        factor = dt2 if f == 8 else None

        def put(xs, ys, value, factor=factor, target=target):
            target[xs, ys, :] = value if factor is None else value * factor

        put(own_x, own_y, own)
        put(lows, own_y, x_low[f])
        put(highs, own_y, x_high[f])
        for s, ys in ((0, pl.ds(PAD - halo, halo)), (1, pl.ds(PAD + ny, halo))):
            middle, low, high = [r[f] for r in sides[3 * s : 3 * s + 3]]
            if merged:
                here = gy == (1 - s)
                middle, low, high = [jnp.where(here, v, 0.0) for v in (middle, low, high)]
            put(own_x, ys, middle)
            put(lows, ys, low)
            put(highs, ys, high)

    lane = iota((tall, nz), 1)
    not_last, not_first = lane < nz - 1, lane > 0

    def fields(cur, x):
        base = [wave[cur, i, x] for i in range(3)]
        nxt = [wave[cur, i, x + 1] for i in range(3)]
        dx = [n - b for n, b in zip(nxt, base)]
        dy = [shifted_up(b, 0) - b for b in base]
        dz = [jnp.where(not_last, shifted_up(b, 1), 0.0) - b for b in base]
        normal = [dx[0], dy[1], dz[2]]
        twice = [dy[0] + dx[1], dz[0] + dx[2], dz[1] + dy[2]]
        m = second[x]
        volume = first[x] * (normal[0] + normal[1] + normal[2])
        m2 = m + m
        stress = [volume + m2 * e for e in normal] + [m * e for e in twice]
        return base, normal, twice, stress

    def back_y(v):
        return v - pltpu.roll(v, 1, 0)

    def back_z(v):
        return v - jnp.where(not_first, pltpu.roll(v, 1, 1), 0.0)

    def plane(step, cur, own, x, carry):
        base, normal, twice, stress = fields(cur, x)
        if own:
            rows = pl.ds(pl.multiple_of(step * nx * ny + (x - halo) * ny, ny), ny)
            for e, value in enumerate(normal + [0.5 * t for t in twice]):
                strain_ref[rows, e * nz : (e + 1) * nz] = value[PAD : PAD + ny].astype(jnp.bfloat16)
        xx, yy, zz, xy, xz, yz = stress
        forces = [
            (xx - carry[0]) + back_y(xy) + back_z(xz),
            (xy - carry[1]) + back_y(yy) + back_z(yz),
            (xz - carry[2]) + back_y(yz) + back_z(zz),
        ]
        for i in range(3):
            value = 2.0 * base[i] - wave[1 - cur, i, x] + scale[x] * forces[i]
            if step == STEPS - 1:
                out_ref[0, i, x - halo] = value[PAD : PAD + ny]
            else:
                wave[1 - cur, i, x] = value
        return xx, xy, xz

    for step in range(STEPS):
        cur = step % 2
        reach = STEPS - 1 - step
        begin, end = halo - reach, halo + nx + reach
        stress = fields(cur, begin - 1)[3]
        carry = (stress[0], stress[3], stress[4])
        for lo, hi, own in ((begin, halo, False), (halo, halo + nx, True), (halo + nx, end, False)):
            if hi > lo:
                carry = lax.fori_loop(lo, hi, functools.partial(plane, step, cur, own), carry)


def stencil(halo, merged, disp, prev, lam, mu, buoy, x_low, x_high, sides):
    nx, ny, nz = lam.shape
    tall, wide = ny + 2 * PAD, nx + 2 * halo
    vmem = pl.BlockSpec(memory_space=pltpu.VMEM)
    operands = (disp, prev, lam, mu, buoy, x_low, x_high, *sides)
    return pl.pallas_call(
        functools.partial(stencil_kernel, halo, merged),
        out_shape=(
            jax.ShapeDtypeStruct(disp.shape, jnp.float32),
            jax.ShapeDtypeStruct((STEPS * nx * ny, 6 * nz), jnp.bfloat16),
        ),
        in_specs=[vmem] * len(operands),
        out_specs=(vmem, vmem),
        scratch_shapes=[pltpu.VMEM((2, 3, wide, tall, nz), jnp.float32)]
        + [pltpu.VMEM((wide, tall, nz), jnp.float32)] * 3
        + [pltpu.SMEM((1,), jnp.int32)],
        compiler_params=pltpu.CompilerParams(vmem_limit_bytes=40 << 20),
        name="stencil",
    )(*operands)


def response_kernel(owners, ranks, records, strain_ref, column_ref, pan0, meta0, pan1, meta1, out_ref):
    points = column_ref.shape[1]
    sent = owners * ranks
    group = LANES // ranks
    columns = strain_ref.shape[0] // STEPS
    total = None
    for pan, meta in ((pan0, meta0), (pan1, meta1)):
        rows = []
        for k in range(2):
            table = meta[k].astype(jnp.float32)
            parts = [
                jnp.sum(table[g * group : (g + 1) * group], axis=0, keepdims=True) for g in range(owners // group)
            ]
            rows.append(jnp.concatenate(parts, axis=1))
        slot, record = rows
        owner = iota((1, sent), 1) // ranks
        spread = (iota((points, sent), 0) == slot.astype(jnp.int32)).astype(jnp.bfloat16)
        table = jnp.broadcast_to(column_ref[...].astype(jnp.float32), (8, points)).astype(jnp.bfloat16)
        column = jnp.dot(table, spread, preferred_element_type=jnp.float32)[:1].astype(jnp.int32)
        length = pan.shape[1] // 6
        grid = None
        for i in range(3):
            right = jnp.concatenate(
                [pan[:, (2 * i + k) * length : (2 * i + k + 1) * length, :].reshape(sent, LANES) for k in range(2)],
                axis=1,
            )
            left = strain_ref[:, 2 * i * LANES : (2 * i + 2) * LANES]
            term = lax.dot_general(left, right, NT, preferred_element_type=jnp.float32)
            grid = term if grid is None else grid + term
        mark = iota((columns, sent), 0) == column
        reply = [
            jnp.sum(jnp.where(mark, grid[m * columns : (m + 1) * columns], 0.0), axis=0, keepdims=True)
            for m in range(STEPS)
        ]
        record = record.astype(jnp.int32)
        offset = record % STEPS
        delayed = []
        for n in range(STEPS):
            value = jnp.where(offset == n, reply[0], 0.0)
            for m in range(1, n + 1):
                value = value + jnp.where(offset == n - m, reply[m], 0.0)
            delayed.append(value)
        delayed = jnp.concatenate(delayed + [jnp.zeros((8 - STEPS, sent), jnp.float32)], axis=0)
        key = owner * records + record // STEPS
        gather = (iota((owners * records, sent), 0) == key).astype(jnp.float32)
        part = lax.dot_general(
            delayed, gather, NT, preferred_element_type=jnp.float32, precision=lax.Precision.HIGHEST
        )
        total = part if total is None else total + part
    out_ref[...] = total[:STEPS]


def respond(owners, ranks, records, strain, columns, halves):
    vmem = pl.BlockSpec(memory_space=pltpu.VMEM)
    operands = (strain, columns, *halves[0], *halves[1])
    return pl.pallas_call(
        functools.partial(response_kernel, owners, ranks, records),
        out_shape=jax.ShapeDtypeStruct((STEPS, owners * records), jnp.float32),
        in_specs=[vmem] * len(operands),
        out_specs=vmem,
        compiler_params=pltpu.CompilerParams(vmem_limit_bytes=40 << 20),
        name="respond",
    )(*operands)


def shift_pairs(nx, ny, dx, dy):
    return [
        (i * ny + j, (i + dx) * ny + j + dy)
        for i in range(nx)
        for j in range(ny)
        if 0 <= i + dx < nx and 0 <= j + dy < ny
    ]


def owner_sum(value, owners):
    if owners & (owners - 1):
        return lax.psum(value, OWNERS_AXES)
    bit = 1
    while bit < owners:
        value = value + lax.ppermute(value, OWNERS_AXES, [(i, i ^ bit) for i in range(owners)])
        bit *= 2
    return value


def body(displacement, previous, first_lame, shear_modulus, buoyancy, tile_column, rupture_tiles, slip_offsets, slip_panels):
    gxs, gys = lax.axis_size("gx"), lax.axis_size("gy")
    owners = gxs * gys
    nx, ny, nz = shear_modulus.shape
    halo = STEPS
    slots = tile_column.shape[0]
    records, listed = rupture_tiles.shape
    entries = records * listed
    ranks = entries // owners
    components = slip_panels.shape[2]

    fields = jnp.concatenate(
        [displacement[0], previous[0], first_lame[None], shear_modulus[None], buoyancy[None]], axis=0
    )
    merged = gys == 2
    gy = lax.axis_index("gy")

    def send(value, dx, dy):
        pairs = shift_pairs(gxs, gys, dx, dy)
        if merged and dy:
            pairs = pairs + shift_pairs(gxs, gys, dx, -dy)
        return lax.ppermute(value, OWNERS_AXES, pairs)

    x_low = send(fields[:, nx - halo :], 1, 0)
    x_high = send(fields[:, :halo], -1, 0)
    if merged:
        edge = lax.dynamic_slice_in_dim(fields, jnp.where(gy == 0, ny - halo, 0), halo, axis=2)
        sides = [send(edge, 0, 1), send(edge, 1, 1), send(edge, -1, 1)]
    else:
        upper, lower = fields[:, :, ny - halo :], fields[:, :, :halo]
        sides = [send(upper, dx, 1) for dx in (0, 1, -1)] + [send(lower, dx, -1) for dx in (0, 1, -1)]

    panels = slip_panels.reshape(entries, components, nz).transpose(1, 0, 2)
    payload = pack(owners, slots, ranks, rupture_tiles, slip_offsets, panels)
    arrived = lax.all_to_all(payload, OWNERS_AXES, split_axis=0, concat_axis=0, tiled=True)
    other = lax.ppermute(arrived, "comp", [(0, 1), (1, 0)])

    final, strain = stencil(
        halo, merged, displacement, previous, first_lame, shear_modulus, buoyancy, x_low, x_high, sides
    )
    halves = [unpack(owners, ranks, components, v) for v in (arrived, other)]
    partial = respond(owners, ranks, records, strain, tile_column.reshape(1, slots), halves)
    summed = owner_sum(partial, owners)
    mine = lax.dynamic_slice_in_dim(summed, owner_index() * records, records, axis=1)
    return final, mine.T[None]


def solution(mesh):
    in_specs = (
        P("comp", None, ("site", "gx"), "gy", None),
        P("comp", None, ("site", "gx"), "gy", None),
        P(("site", "gx"), "gy", None),
        P(("site", "gx"), "gy", None),
        P(("site", "gx"), "gy", None),
        P(("site", "gx", "gy")),
        P(("site", "gx", "gy"), None),
        P(("site", "gx", "gy"), None),
        P(("site", "gx", "gy"), None, None, None),
    )
    out_specs = (P("comp", None, ("site", "gx"), "gy", None), P("comp", ("site", "gx", "gy"), None))
    return jax.shard_map(body, mesh=mesh, in_specs=in_specs, out_specs=out_specs, check_vma=False)
```

time: 213 us -> 62.1 us (0.29)
  local copies, waits for them, and re-layouts: 72.6 us -> 7.4 us
  waiting for transfers between devices: 81.9 us -> 19.9 us
  starting transfers between devices: 46.9 us -> 22.2 us
  Pallas kernels: 0 us -> 9.43 us
  other arithmetic: 8.31 us -> 1.79 us
    all_to_all x2 -> x1, waiting for transfers between devices: 65.6 us -> 3.5 us  [body(): lax.all_to_all(payload, OWNERS_AXES, split_axis=0, concat_axis=0, tiled=T...]
    scatter x1 -> x0, local copies, waits for them, and re-layouts: 38.7 us -> none  [body(): jnp.zeros((owners, capacity), jnp.int32).at[source, slot_rank]]
    gather x26 -> x0, local copies, waits for them, and re-layouts: 26.1 us -> none  [the longest x24 17 us: body(): strain.reshape(rows_local * cols_local, depth_points)[tile_column]]
    ppermute x16 -> x9, starting transfers between devices: 36.9 us -> 14.8 us  [the longest x5 10.7 us: send(): return lax.ppermute(value, OWNERS_AXES, pairs)]
    pallas_call x0 -> x3, Pallas kernels: none -> 9.43 us  [the longest x1 5.78 us: stencil(): pl.pallas_call(functools.partial(stencil_kernel, halo, merged), out_shape...]
    unnamed x37 -> x17, local copies, waits for them, and re-layouts: 2.67 us -> 5.85 us
    all_to_all x2 -> x1, starting transfers between devices: 9.99 us -> 7.38 us  [body(): lax.all_to_all(payload, OWNERS_AXES, split_axis=0, concat_axis=0, tiled=T...]
    reshape x4 -> x0, local copies, waits for them, and re-layouts: 2.41 us -> none  [the longest x3 2.33 us: body(): flat_tiles = rupture_tiles.reshape(entries)]
  transfers between devices with their start and end apart: 18 -> 10, of which waited for: 7 -> 7; matrix products, arithmetic and copies ran while one was open for 28% -> 0% of each run, Pallas kernels for 0% -> 9%
where the time goes in v1:
time: 62.1 us; the launch traced here: 61.5 us
  starting transfers between devices  22.2 us (36%)
  waiting for transfers between devices  19.9 us (32%)
  Pallas kernels  9.43 us (15%)
  local copies, waits for them, and re-layouts  7.4 us (12%)
  other arithmetic  1.79 us (3%)
  between operations  0.79 us (1%)
    ppermute x5, starting transfers between devices, send(): return lax.ppermute(value, OWNERS_AXES, pairs)  10.7 us
    ppermute x5, waiting for transfers between devices, send(): return lax.ppermute(value, OWNERS_AXES, pairs)  8.77 us
    ppermute x3, waiting for transfers between devices, owner_sum(): lax.ppermute(value, OWNERS_AXES, [(i, i ^ bit) for i in range(owners)])  7.58 us
    all_to_all x1, starting transfers between devices, body(): lax.all_to_all(payload, OWNERS_AXES, split_axis=0, concat_axis=0, tiled=T...  7.38 us
    unnamed x17, local copies, waits for them, and re-layouts  5.85 us
    pallas_call x1, Pallas kernels, stencil(): pl.pallas_call(functools.partial(stencil_kernel, halo, merged), out_shape...  5.78 us
    ppermute x3, starting transfers between devices, owner_sum(): lax.ppermute(value, OWNERS_AXES, [(i, i ^ bit) for i in range(owners)])  4.11 us
    all_to_all x1, waiting for transfers between devices, body(): lax.all_to_all(payload, OWNERS_AXES, split_axis=0, concat_axis=0, tiled=T...  3.5 us
  transfers between devices with their start and end apart: 10, of which 7 were waited for; matrix products, arithmetic and copies ran while one was open for 0% of the time, Pallas kernels for 9%

profile of v1, /device:TPU:0, one launch (start us, length us, event | category | flops | bytes accessed | tf_op | source)
XLA Modules:
  0.0 61.5 jit_solution(11361434383692048339)
XLA Ops:
  0.6 1.8 %copy.15 = bf16[16,16,6,128]{3,1,0,2:T(8,128)(2,1)} copy(bf16[16,16,6,128]{3,1,2,0:T(8,128)(2,1)} %param.17) | data formatting | bytes 786432 | tf_op args[8]
  2.4 2.4 %pack.1 = (bf16[8,192,128]{2,1,0:T(8,128)(2,1)}, bf16[2,8,128]{2,1,0:T(8,128)(2,1)}) custom-call(s32[16,16]{1,0:T(8,128)} %tiles_ref.1, s32[16,16]{1,0:T(8,128)} %offsets_ref.1, bf16[6,256,128]{2,1,0:T(8,128)(2,1)} %bitcast.24), custom_call_target="tpu_custom_call" | custom-call | tf_op jit(solution)/shard_map/pack/pallas_call | solution.py:69
  4.8 0.7 %copy.16 = bf16[8,2,128]{2,1,0:T(2,128)(2,1)S(1)} copy(bf16[8,2,128]{2,0,1:T(8,128)(2,1)} %bitcast.25) | data formatting | bytes 8192 | tf_op jit(solution)/shard_map/transpose | solution.py:82
  5.5 1.8 %pad_maximum_fusion = bf16[8,194,128]{2,1,0:T(8,128)(2,1)} fusion(bf16[8,2,128]{2,1,0:T(2,128)(2,1)S(1)} %copy.16, bf16[8,192,128]{2,1,0:T(8,128)(2,1)} %get-tuple-element.8), kind=kLoop, calls=%fused_computation | loop fusion | flops 794624 | bytes 794624 | tf_op jit(solution)/shard_map/concatenate | solution.py:82
  7.2 0.0 copy-start
  7.2 7.4 %all-to-all-start = ((bf16[8,194,128]{2,1,0:T(8,128)(2,1)}), bf16[8,194,128]{2,1,0:T(8,128)(2,1)S(1)}, u32[]{:S(2)}, u32[]{:S(2)}) async-start(bf16[8,194,128]{2,1,0:T(8,128)(2,1)} %pad_maximum_fusion), calls=%async_computation | async-start | bytes 819200 | tf_op jit(solution)/shard_map/all_to_all | solution.py:323
  14.6 0.0 copy-done
  14.6 0.0 copy-start.1
  14.7 0.9 %copy-done.1 = f32[1,3,4,32,128]{4,3,2,1,0:T(8,128)S(1)} copy-done((f32[1,3,4,32,128]{4,3,2,1,0:T(8,128)S(1)}, f32[1,3,4,32,128]{4,3,2,1,0:T(8,128)}, u32[]{:S(2)}) %copy-start.1) | copy-done | bytes 196632
  15.6 0.0 copy-start.2
  15.6 0.8 %copy-done.2 = f32[4,32,128]{2,1,0:T(8,128)S(1)} copy-done((f32[4,32,128]{2,1,0:T(8,128)S(1)}, f32[4,32,128]{2,1,0:T(8,128)}, u32[]{:S(2)}) %copy-start.2) | copy-done | bytes 65560
  16.4 0.0 copy-start.3
  16.4 0.8 %copy-done.3 = f32[4,32,128]{2,1,0:T(8,128)S(1)} copy-done((f32[4,32,128]{2,1,0:T(8,128)S(1)}, f32[4,32,128]{2,1,0:T(8,128)}, u32[]{:S(2)}) %copy-start.3) | copy-done | bytes 65560
  17.2 0.0 copy-start.4
  17.3 0.8 %copy-done.4 = f32[4,32,128]{2,1,0:T(8,128)S(1)} copy-done((f32[4,32,128]{2,1,0:T(8,128)S(1)}, f32[4,32,128]{2,1,0:T(8,128)}, u32[]{:S(2)}) %copy-start.4) | copy-done | bytes 65560
  18.1 3.9 %collective-permute-start = (f32[9,4,32,128]{3,2,1,0:T(8,128)S(1)}, f32[9,4,32,128]{3,2,1,0:T(8,128)S(1)}, u32[]{:S(2)}, u32[]{:S(2)}) collective-permute-start(f32[9,4,32,128]{3,2,1,0:T(8,128)S(1)} %bitcast_dynamic-update-slice_fusion.2), channel_id=1, source_target_pairs={{0,4},{2,6},{4,8},{6,10},{8,12},{10,14},{1,5},{3,7},{5,9},{7,11},{... | collective-permute-start | bytes 1769480 | tf_op jit(solution)/shard_map/ppermute | solution.py:310
  22.0 1.3 %collective-permute-start.1 = (f32[9,4,32,128]{3,2,1,0:T(8,128)S(1)}, f32[9,4,32,128]{3,2,1,0:T(8,128)S(1)}, u32[]{:S(2)}, u32[]{:S(2)}) collective-permute-start(f32[9,4,32,128]{3,2,1,0:T(8,128)S(1)} %bitcast_dynamic-update-slice_fusion.2), channel_id=1, source_target_pairs={{4,0},{6,2},{8,4},{10,6},{12,8},{14,10},{5,1},{7,3},{9,5},{11,7},{... | collective-permute-start | bytes 1769480 | tf_op jit(solution)/shard_map/ppermute | solution.py:310
  23.3 3.5 %all-to-all-done = bf16[8,194,128]{2,1,0:T(8,128)(2,1)S(1)} async-done(((bf16[8,194,128]{2,1,0:T(8,128)(2,1)}), bf16[8,194,128]{2,1,0:T(8,128)(2,1)S(1)}, u32[]{:S(2)}, u32[]{:S(2)}) %all-to-all-start) | async-done | bytes 397344 | tf_op jit(solution)/shard_map/all_to_all | solution.py:323
  26.9 0.1 copy.17
  26.9 0.1 collective-permute-start.5
  27.0 1.5 %collective-permute-start.2 = (f32[9,4,4,128]{3,2,1,0:T(4,128)S(1)}, f32[9,4,4,128]{3,2,1,0:T(4,128)S(1)}, u32[]{:S(2)}, u32[]{:S(2)}) collective-permute-start(f32[9,4,4,128]{3,2,1,0:T(4,128)S(1)} %constant_dynamic-slice_fusion), channel_id=1, source_target_pairs={{0,2},{4,6},{8,10},{12,14},{2,0},{6,4},{10,8},{14,12},{1,3},{5,7},... | collective-permute-start | bytes 221192 | tf_op jit(solution)/shard_map/ppermute | solution.py:310
  28.6 2.6 %collective-permute-start.3 = (f32[9,4,4,128]{3,2,1,0:T(4,128)S(1)}, f32[9,4,4,128]{3,2,1,0:T(4,128)S(1)}, u32[]{:S(2)}, u32[]{:S(2)}) collective-permute-start(f32[9,4,4,128]{3,2,1,0:T(4,128)S(1)} %constant_dynamic-slice_fusion), channel_id=1, source_target_pairs={{0,6},{4,10},{8,14},{2,4},{6,8},{10,12},{1,7},{5,11},{9,15},{3,5},... | collective-permute-start | bytes 221192 | tf_op jit(solution)/shard_map/ppermute | solution.py:310
  31.2 0.6 collective-permute-done.2.refs_7_
  31.8 1.3 %collective-permute-start.4 = (f32[9,4,4,128]{3,2,1,0:T(4,128)S(1)}, f32[9,4,4,128]{3,2,1,0:T(4,128)S(1)}, u32[]{:S(2)}, u32[]{:S(2)}) collective-permute-start(f32[9,4,4,128]{3,2,1,0:T(4,128)S(1)} %constant_dynamic-slice_fusion), channel_id=1, source_target_pairs={{4,2},{8,6},{12,10},{6,0},{10,4},{14,8},{5,3},{9,7},{13,11},{7,1},... | collective-permute-start | bytes 221192 | tf_op jit(solution)/shard_map/ppermute | solution.py:310
  33.0 2.6 %collective-permute-done.3.refs_8_ = f32[9,4,4,128]{3,2,1,0:T(4,128)S(1)} collective-permute-done((f32[9,4,4,128]{3,2,1,0:T(4,128)S(1)}, f32[9,4,4,128]{3,2,1,0:T(4,128)S(1)}, u32[]{:S(2)}, u32[]{:S(2)}) %collective-permute-start.3) | collective-permute-done | bytes 73760 | tf_op jit(solution)/shard_map/ppermute | solution.py:310
  35.7 5.6 %collective-permute-done.4.refs_9_ = f32[9,4,4,128]{3,2,1,0:T(4,128)S(1)} collective-permute-done((f32[9,4,4,128]{3,2,1,0:T(4,128)S(1)}, f32[9,4,4,128]{3,2,1,0:T(4,128)S(1)}, u32[]{:S(2)}, u32[]{:S(2)}) %collective-permute-start.4) | collective-permute-done | bytes 73760 | tf_op jit(solution)/shard_map/ppermute | solution.py:310
  41.2 0.0 collective-permute-done.refs_5_
  41.2 0.0 collective-permute-done.1.refs_6_
  41.2 5.8 %stencil.1 = (f32[1,3,4,32,128]{4,3,2,1,0:T(8,128)}, bf16[512,768]{1,0:T(8,128)(2,1)S(1)}) custom-call(f32[1,3,4,32,128]{4,3,2,1,0:T(8,128)S(1)} %copy-done, f32[1,3,4,32,128]{4,3,2,1,0:T(8,128)S(1)} %copy-done.1, f32[4,32,128]{2,1,0:T(8,128)S(1)} %copy-done.2, f32[4,32,128]{2,1,0:T(8,128)S(1)} %copy-done.3, f32[4,32,128]{2,1,0:T(8,128)S(1)} %copy-done.4, ...), custom_call_target="tpu_custom_call" | custom-call | tf_op jit(solution)/shard_map/stencil/pallas_call | solution.py:189
  47.1 0.0 collective-permute-done.5
  47.1 0.1 copy.19.pan1
  47.2 0.0 copy-start.5
  47.2 0.6 %copy-done.5 = s32[128]{0:T(128)S(1)} copy-done((s32[128]{0:T(128)S(1)}, s32[128]{0:T(128)}, u32[]{:S(2)}) %copy-start.5) | copy-done | bytes 536
  47.8 1.3 %respond.1 = f32[4,128]{1,0:T(4,128)S(1)} custom-call(bf16[512,768]{1,0:T(8,128)(2,1)S(1)} %get-tuple-element.7.strain_ref, s32[1,128]{1,0:T(1,128)S(1)} %bitcast.23, bf16[8,192,128]{2,1,0:T(8,128)(2,1)S(1)} %slice.16.pan0, bf16[2,8,128]{2,1,0:T(8,128)(2,1)S(1)} %slice_bitcast_fusion.1.meta0, bf16[8,192,128]{2,1,0:T(8,128)(2,1)S(1)} %copy.19.pan1, ...), custom_call_target="tpu_custom_call" | custom-call | tf_op jit(solution)/shard_map/respond/pallas_call | solution.py:260
  49.1 1.1 %collective-permute-start.6 = (f32[4,128]{1,0:T(4,128)S(1)}, f32[4,128]{1,0:T(4,128)S(1)}, u32[]{:S(2)}, u32[]{:S(2)}) collective-permute-start(f32[4,128]{1,0:T(4,128)S(1)} %respond.1), channel_id=1, source_target_pairs={{0,2},{2,0},{4,6},{6,4},{8,10},{10,8},{12,14},{14,12},{1,3},{3,1},... | collective-permute-start | bytes 6152 | tf_op jit(solution)/shard_map/ppermute | solution.py:284
  50.2 2.5 %collective-permute-done.6 = f32[4,128]{1,0:T(4,128)S(1)} collective-permute-done((f32[4,128]{1,0:T(4,128)S(1)}, f32[4,128]{1,0:T(4,128)S(1)}, u32[]{:S(2)}, u32[]{:S(2)}) %collective-permute-start.6) | collective-permute-done | bytes 2080 | tf_op jit(solution)/shard_map/ppermute | solution.py:284
  52.7 1.1 %collective-permute-start.7 = (f32[4,128]{1,0:T(4,128)S(1)}, f32[4,128]{1,0:T(4,128)S(1)}, u32[]{:S(2)}, u32[]{:S(2)}) collective-permute-start(f32[4,128]{1,0:T(4,128)S(1)} %add.16), channel_id=1, source_target_pairs={{0,4},{2,6},{4,0},{6,2},{8,12},{10,14},{12,8},{14,10},{1,5},{3,7},... | collective-permute-start | bytes 6152 | tf_op jit(solution)/shard_map/ppermute | solution.py:284
  53.8 2.5 %collective-permute-done.7 = f32[4,128]{1,0:T(4,128)S(1)} collective-permute-done((f32[4,128]{1,0:T(4,128)S(1)}, f32[4,128]{1,0:T(4,128)S(1)}, u32[]{:S(2)}, u32[]{:S(2)}) %collective-permute-start.7) | collective-permute-done | bytes 2080 | tf_op jit(solution)/shard_map/ppermute | solution.py:284
  56.3 1.9 %collective-permute-start.8 = (f32[4,128]{1,0:T(4,128)S(1)}, f32[4,128]{1,0:T(4,128)S(1)}, u32[]{:S(2)}, u32[]{:S(2)}) collective-permute-start(f32[4,128]{1,0:T(4,128)S(1)} %add.17), channel_id=1, source_target_pairs={{0,8},{2,10},{4,12},{6,14},{8,0},{10,2},{12,4},{14,6},{1,9},{3,11}... | collective-permute-start | bytes 6152 | tf_op jit(solution)/shard_map/ppermute | solution.py:284
  58.2 2.6 %collective-permute-done.8 = f32[4,128]{1,0:T(4,128)S(1)} collective-permute-done((f32[4,128]{1,0:T(4,128)S(1)}, f32[4,128]{1,0:T(4,128)S(1)}, u32[]{:S(2)}, u32[]{:S(2)}) %collective-permute-start.8) | collective-permute-done | bytes 2080 | tf_op jit(solution)/shard_map/ppermute | solution.py:284
  60.8 0.7 %dynamic-slice_bitcast_fusion = f32[1,16,4]{1,2,0:T(4,128)} fusion(f32[4,128]{1,0:T(4,128)S(1)} %add.18, s32[]{:T(128)S(6)} %select_n.9), kind=kLoop, calls=%fused_computation.8 | loop fusion | bytes 516 | tf_op jit(solution)/shard_map/broadcast_in_dim | solution.py:333
  (13 shorter events, 0.1 us)
Async XLA Ops:
  7.2 7.4 %copy-start = (f32[1,3,4,32,128]{4,3,2,1,0:T(8,128)S(1)}, f32[1,3,4,32,128]{4,3,2,1,0:T(8,128)}, u32[]{:S(2)}) copy-start(f32[1,3,4,32,128]{4,3,2,1,0:T(8,128)} %refs_0_.1) | copy-start | bytes 589828
  7.2 19.6 %all-to-all-start = ((bf16[8,194,128]{2,1,0:T(8,128)(2,1)}), bf16[8,194,128]{2,1,0:T(8,128)(2,1)S(1)}, u32[]{:S(2)}, u32[]{:S(2)}) async-start(bf16[8,194,128]{2,1,0:T(8,128)(2,1)} %pad_maximum_fusion), calls=%async_computation | async-start | bytes 819200 | tf_op jit(solution)/shard_map/all_to_all | solution.py:323
  14.6 0.9 %copy-start.1 = (f32[1,3,4,32,128]{4,3,2,1,0:T(8,128)S(1)}, f32[1,3,4,32,128]{4,3,2,1,0:T(8,128)}, u32[]{:S(2)}) copy-start(f32[1,3,4,32,128]{4,3,2,1,0:T(8,128)} %refs_1_.1) | copy-start | bytes 589828
  15.6 0.8 %copy-start.2 = (f32[4,32,128]{2,1,0:T(8,128)S(1)}, f32[4,32,128]{2,1,0:T(8,128)}, u32[]{:S(2)}) copy-start(f32[4,32,128]{2,1,0:T(8,128)} %refs_2_.1) | copy-start | bytes 196612
  16.4 0.8 %copy-start.3 = (f32[4,32,128]{2,1,0:T(8,128)S(1)}, f32[4,32,128]{2,1,0:T(8,128)}, u32[]{:S(2)}) copy-start(f32[4,32,128]{2,1,0:T(8,128)} %refs_3_.1) | copy-start | bytes 196612
  17.2 0.8 %copy-start.4 = (f32[4,32,128]{2,1,0:T(8,128)S(1)}, f32[4,32,128]{2,1,0:T(8,128)}, u32[]{:S(2)}) copy-start(f32[4,32,128]{2,1,0:T(8,128)} %refs_4_.1) | copy-start | bytes 196612
  18.1 23.1 %collective-permute-start = (f32[9,4,32,128]{3,2,1,0:T(8,128)S(1)}, f32[9,4,32,128]{3,2,1,0:T(8,128)S(1)}, u32[]{:S(2)}, u32[]{:S(2)}) collective-permute-start(f32[9,4,32,128]{3,2,1,0:T(8,128)S(1)} %bitcast_dynamic-update-slice_fusion.2), channel_id=1, source_target_pairs={{0,4},{2,6},{4,8},{6,10},{8,12},{10,14},{1,5},{3,7},{5,9},{7,11},{... | collective-permute-start | bytes 1769480 | tf_op jit(solution)/shard_map/ppermute | solution.py:310
  22.0 19.2 %collective-permute-start.1 = (f32[9,4,32,128]{3,2,1,0:T(8,128)S(1)}, f32[9,4,32,128]{3,2,1,0:T(8,128)S(1)}, u32[]{:S(2)}, u32[]{:S(2)}) collective-permute-start(f32[9,4,32,128]{3,2,1,0:T(8,128)S(1)} %bitcast_dynamic-update-slice_fusion.2), channel_id=1, source_target_pairs={{4,0},{6,2},{8,4},{10,6},{12,8},{14,10},{5,1},{7,3},{9,5},{11,7},{... | collective-permute-start | bytes 1769480 | tf_op jit(solution)/shard_map/ppermute | solution.py:310
  26.9 20.1 %collective-permute-start.5 = (bf16[8,194,128]{2,0,1:T(8,128)(2,1)S(1)}, bf16[8,194,128]{2,0,1:T(8,128)(2,1)S(1)}, u32[]{:S(2)}, u32[]{:S(2)}) collective-permute-start(bf16[8,194,128]{2,0,1:T(8,128)(2,1)S(1)} %copy.17), channel_id=1, source_target_pairs={{0,1},{1,0},{2,3},{3,2},{4,5},{5,4},{6,7},{7,6},{8,9},{9,8},{10,11... | collective-permute-start | bytes 1191944 | tf_op jit(solution)/shard_map/ppermute | solution.py:324
  27.0 4.7 %collective-permute-start.2 = (f32[9,4,4,128]{3,2,1,0:T(4,128)S(1)}, f32[9,4,4,128]{3,2,1,0:T(4,128)S(1)}, u32[]{:S(2)}, u32[]{:S(2)}) collective-permute-start(f32[9,4,4,128]{3,2,1,0:T(4,128)S(1)} %constant_dynamic-slice_fusion), channel_id=1, source_target_pairs={{0,2},{4,6},{8,10},{12,14},{2,0},{6,4},{10,8},{14,12},{1,3},{5,7},... | collective-permute-start | bytes 221192 | tf_op jit(solution)/shard_map/ppermute | solution.py:310
  28.6 7.1 %collective-permute-start.3 = (f32[9,4,4,128]{3,2,1,0:T(4,128)S(1)}, f32[9,4,4,128]{3,2,1,0:T(4,128)S(1)}, u32[]{:S(2)}, u32[]{:S(2)}) collective-permute-start(f32[9,4,4,128]{3,2,1,0:T(4,128)S(1)} %constant_dynamic-slice_fusion), channel_id=1, source_target_pairs={{0,6},{4,10},{8,14},{2,4},{6,8},{10,12},{1,7},{5,11},{9,15},{3,5},... | collective-permute-start | bytes 221192 | tf_op jit(solution)/shard_map/ppermute | solution.py:310
  31.8 9.5 %collective-permute-start.4 = (f32[9,4,4,128]{3,2,1,0:T(4,128)S(1)}, f32[9,4,4,128]{3,2,1,0:T(4,128)S(1)}, u32[]{:S(2)}, u32[]{:S(2)}) collective-permute-start(f32[9,4,4,128]{3,2,1,0:T(4,128)S(1)} %constant_dynamic-slice_fusion), channel_id=1, source_target_pairs={{4,2},{8,6},{12,10},{6,0},{10,4},{14,8},{5,3},{9,7},{13,11},{7,1},... | collective-permute-start | bytes 221192 | tf_op jit(solution)/shard_map/ppermute | solution.py:310
  47.2 0.7 %copy-start.5 = (s32[128]{0:T(128)S(1)}, s32[128]{0:T(128)}, u32[]{:S(2)}) copy-start(s32[128]{0:T(128)} %param.14) | copy-start | bytes 1540
  49.1 3.6 %collective-permute-start.6 = (f32[4,128]{1,0:T(4,128)S(1)}, f32[4,128]{1,0:T(4,128)S(1)}, u32[]{:S(2)}, u32[]{:S(2)}) collective-permute-start(f32[4,128]{1,0:T(4,128)S(1)} %respond.1), channel_id=1, source_target_pairs={{0,2},{2,0},{4,6},{6,4},{8,10},{10,8},{12,14},{14,12},{1,3},{3,1},... | collective-permute-start | bytes 6152 | tf_op jit(solution)/shard_map/ppermute | solution.py:284
  52.7 3.6 %collective-permute-start.7 = (f32[4,128]{1,0:T(4,128)S(1)}, f32[4,128]{1,0:T(4,128)S(1)}, u32[]{:S(2)}, u32[]{:S(2)}) collective-permute-start(f32[4,128]{1,0:T(4,128)S(1)} %add.16), channel_id=1, source_target_pairs={{0,4},{2,6},{4,0},{6,2},{8,12},{10,14},{12,8},{14,10},{1,5},{3,7},... | collective-permute-start | bytes 6152 | tf_op jit(solution)/shard_map/ppermute | solution.py:284
  56.3 4.5 %collective-permute-start.8 = (f32[4,128]{1,0:T(4,128)S(1)}, f32[4,128]{1,0:T(4,128)S(1)}, u32[]{:S(2)}, u32[]{:S(2)}) collective-permute-start(f32[4,128]{1,0:T(4,128)S(1)} %add.17), channel_id=1, source_target_pairs={{0,8},{2,10},{4,12},{6,14},{8,0},{10,2},{12,4},{14,6},{1,9},{3,11}... | collective-permute-start | bytes 6152 | tf_op jit(solution)/shard_map/ppermute | solution.py:284

commit v2 on v1

--- a/solution.py
+++ b/solution.py
@@ -12,6 +12,7 @@
 LANES = 128
 PAD = 8
 OWNERS_AXES = ("gx", "gy")
+FIELDS = 9
 NT = (((1,), (1,)), ((), ()))
 
 
@@ -23,7 +24,7 @@
     return lax.axis_index("gx") * lax.axis_size("gy") + lax.axis_index("gy")
 
 
-def pack_kernel(owners, slots, ranks, tiles_ref, offsets_ref, panels_ref, out_ref, meta_ref):
+def pack_kernel(owners, slots, ranks, tiles_ref, offsets_ref, panels_ref, out_ref, meta_ref=None):
     rows, cols = tiles_ref.shape
     entries = rows * cols
     core = lax.axis_index("comp")
@@ -55,40 +56,117 @@
     group = LANES // ranks
     lane = jnp.where(mine, rank + ranks * (me % group), -1)
     marks = (iota((LANES, entries), 0) == lane).astype(jnp.bfloat16)
-    for k, value in enumerate((slot, record)):
+    meta = []
+    for value in (slot, record):
         table = jnp.where(chosen, value, 0.0).astype(jnp.bfloat16)
-        rows_out = lax.dot_general(table, marks, NT, preferred_element_type=jnp.float32).astype(jnp.bfloat16)
-        meta_ref[k] = rows_out
+        meta.append(lax.dot_general(table, marks, NT, preferred_element_type=jnp.float32).astype(jnp.bfloat16))
+    if meta_ref is None:
+        tail = jnp.concatenate([m.reshape(owners, 1, LANES) for m in meta] * 4, axis=1)
+        out_ref[:, panels_ref.shape[0] * length :, :] = tail
+    else:
+        for k in range(2):
+            meta_ref[k] = meta[k]
+
+
+META_ROWS = 8
 
 
 def pack(owners, slots, ranks, tiles, offsets, panels):
-    friendly = ranks % 16 == 0
-    blocks = owners if friendly else 1
-    sent = owners * ranks
     components = panels.shape[0]
+    vmem = pl.BlockSpec(memory_space=pltpu.VMEM)
+    kernel = functools.partial(pack_kernel, owners, slots, ranks)
+    if ranks % 16 == 0:
+        return pl.pallas_call(
+            kernel,
+            out_shape=jax.ShapeDtypeStruct((owners, components * ranks + META_ROWS, LANES), jnp.bfloat16),
+            in_specs=[vmem] * 3,
+            out_specs=vmem,
+            name="pack",
+        )(tiles, offsets, panels)
     body, meta = pl.pallas_call(
-        functools.partial(pack_kernel, owners, slots, ranks),
+        kernel,
         out_shape=(
-            jax.ShapeDtypeStruct((blocks, components * sent // blocks, LANES), jnp.bfloat16),
+            jax.ShapeDtypeStruct((1, components * owners * ranks, LANES), jnp.bfloat16),
             jax.ShapeDtypeStruct((2, owners, LANES), jnp.bfloat16),
         ),
-        in_specs=[pl.BlockSpec(memory_space=pltpu.VMEM)] * 3,
-        out_specs=(pl.BlockSpec(memory_space=pltpu.VMEM),) * 2,
+        in_specs=[vmem] * 3,
+        out_specs=(vmem, vmem),
         name="pack",
     )(tiles, offsets, panels)
-    if not friendly:
-        body = body.reshape(components, owners, ranks, LANES).transpose(1, 0, 2, 3)
-        body = body.reshape(owners, components * ranks, LANES)
+    body = body.reshape(components, owners, ranks, LANES).transpose(1, 0, 2, 3)
+    body = body.reshape(owners, components * ranks, LANES)
     return jnp.concatenate([body, meta.transpose(1, 0, 2)], axis=1)
 
 
 def unpack(owners, ranks, components, arrived):
+    if ranks % 16 == 0:
+        return (arrived,)
     body = arrived[:, : components * ranks]
     meta = arrived[:, components * ranks :].transpose(1, 0, 2)
-    if ranks % 16:
-        body = body.reshape(owners, components, ranks, LANES).transpose(1, 0, 2, 3)
-        body = body.reshape(1, components * owners * ranks, LANES)
-    return body, meta
+    body = body.reshape(owners, components, ranks, LANES).transpose(1, 0, 2, 3)
+    return body.reshape(1, components * owners * ranks, LANES), meta
+
+
+def planes_for(side, halo, nx):
+    plan = []
+    for field in range(FIELDS):
+        count = halo if field < 3 or (side > 0 and field in (6, 7)) else halo - 1
+        plan.append((field, nx - count if side > 0 else 0, count))
+    return plan
+
+
+def prepare_kernel(halo, merged, *refs):
+    disp, prev, lam, mu, buoy, fields, up, down = refs[:8]
+    edges, sem = refs[8:-1], refs[-1]
+    nx, ny, nz = lam.shape
+    copies = [
+        pltpu.make_async_copy(disp.at[0], fields.at[pl.ds(0, 3)], sem.at[0]),
+        pltpu.make_async_copy(prev.at[0], fields.at[pl.ds(3, 3)], sem.at[1]),
+        pltpu.make_async_copy(lam, fields.at[6], sem.at[2]),
+        pltpu.make_async_copy(mu, fields.at[7], sem.at[3]),
+        pltpu.make_async_copy(buoy, fields.at[8], sem.at[4]),
+    ]
+    for copy in copies:
+        copy.start()
+    gy = lax.axis_index("gy")
+    done = 0
+    for side, target in ((1, up), (-1, down)):
+        at = 0
+        for field, first, count in planes_for(side, halo, nx):
+            while done < len(copies) and field >= (0, 3, 6, 7, 8)[done]:
+                copies[done].wait()
+                done += 1
+            target[at : at + count] = fields[field, first : first + count]
+            at += count
+    high, low = pl.ds(ny - halo, halo), pl.ds(0, halo)
+    if merged:
+
+        @pl.when(gy == 0)
+        def _():
+            edges[0][...] = fields[:, :, high, :]
+
+        @pl.when(gy != 0)
+        def _():
+            edges[0][...] = fields[:, :, low, :]
+    else:
+        edges[0][...] = fields[:, :, high, :]
+        edges[1][...] = fields[:, :, low, :]
+
+
+def prepare(halo, merged, disp, prev, lam, mu, buoy):
+    nx, ny, nz = lam.shape
+    vmem, anywhere = pl.BlockSpec(memory_space=pltpu.VMEM), pl.BlockSpec(memory_space=pl.ANY)
+    totals = [sum(count for _, _, count in planes_for(side, halo, nx)) for side in (1, -1)]
+    shapes = [(FIELDS, nx, ny, nz)] + [(total, ny, nz) for total in totals]
+    shapes += [(FIELDS, nx, halo, nz)] * (1 if merged else 2)
+    return pl.pallas_call(
+        functools.partial(prepare_kernel, halo, merged),
+        out_shape=[jax.ShapeDtypeStruct(shape, jnp.float32) for shape in shapes],
+        in_specs=[anywhere] * 5,
+        out_specs=[vmem] * len(shapes),
+        scratch_shapes=[pltpu.SemaphoreType.DMA((5,))],
+        name="prepare",
+    )(disp, prev, lam, mu, buoy)
 
 
 def shifted_up(value, dim):
@@ -96,28 +174,30 @@
 
 
 def stencil_kernel(halo, merged, *refs):
-    disp, prev, lam, mu, buoy, x_low, x_high = refs[:7]
-    sides = refs[7:13] if not merged else refs[7:10] * 2
+    fields, x_low, x_high = refs[:3]
+    sides = refs[3:9] if not merged else refs[3:6] * 2
     out_ref, strain_ref = refs[-7:-5]
     wave, first, second, scale = refs[-5:-1]
-    nx, ny, nz = lam.shape
+    _, nx, ny, nz = fields.shape
     tall = ny + 2 * PAD
     gy = lax.axis_index("gy")
     own_x, own_y = pl.ds(halo, nx), pl.ds(PAD, ny)
     lows, highs = pl.ds(0, halo), pl.ds(halo + nx, halo)
 
     targets = [wave.at[0, i] for i in range(3)] + [wave.at[1, i] for i in range(3)] + [first, second, scale]
-    owns = [disp[0, i] for i in range(3)] + [prev[0, i] for i in range(3)] + [lam[...], mu[...], buoy[...]]
-    dt2 = TIME_STEP * TIME_STEP
-    for f, (target, own) in enumerate(zip(targets, owns)):
-        factor = dt2 if f == 8 else None
-
-        def put(xs, ys, value, factor=factor, target=target):
-            target[xs, ys, :] = value if factor is None else value * factor
-
-        put(own_x, own_y, own)
-        put(lows, own_y, x_low[f])
-        put(highs, own_y, x_high[f])
+    low_at = high_at = 0
+    for f, target in enumerate(targets):
+
+        def put(xs, ys, value, f=f, target=target):
+            target[xs, ys, :] = value * (TIME_STEP * TIME_STEP) if f == 8 else value
+
+        put(own_x, own_y, fields[f])
+        _, _, count = planes_for(1, halo, nx)[f]
+        put(pl.ds(halo - count, count), own_y, x_low[low_at : low_at + count])
+        low_at += count
+        _, _, count = planes_for(-1, halo, nx)[f]
+        put(pl.ds(halo + nx, count), own_y, x_high[high_at : high_at + count])
+        high_at += count
         for s, ys in ((0, pl.ds(PAD - halo, halo)), (1, pl.ds(PAD + ny, halo))):
             middle, low, high = [r[f] for r in sides[3 * s : 3 * s + 3]]
             if merged:
@@ -181,15 +261,15 @@
                 carry = lax.fori_loop(lo, hi, functools.partial(plane, step, cur, own), carry)
 
 
-def stencil(halo, merged, disp, prev, lam, mu, buoy, x_low, x_high, sides):
-    nx, ny, nz = lam.shape
+def stencil(halo, merged, fields, x_low, x_high, sides):
+    _, nx, ny, nz = fields.shape
     tall, wide = ny + 2 * PAD, nx + 2 * halo
     vmem = pl.BlockSpec(memory_space=pltpu.VMEM)
-    operands = (disp, prev, lam, mu, buoy, x_low, x_high, *sides)
+    operands = (fields, x_low, x_high, *sides)
     return pl.pallas_call(
         functools.partial(stencil_kernel, halo, merged),
         out_shape=(
-            jax.ShapeDtypeStruct(disp.shape, jnp.float32),
+            jax.ShapeDtypeStruct((1, 3, nx, ny, nz), jnp.float32),
             jax.ShapeDtypeStruct((STEPS * nx * ny, 6 * nz), jnp.bfloat16),
         ),
         in_specs=[vmem] * len(operands),
@@ -198,20 +278,25 @@
         + [pltpu.VMEM((wide, tall, nz), jnp.float32)] * 3
         + [pltpu.SMEM((1,), jnp.int32)],
         compiler_params=pltpu.CompilerParams(vmem_limit_bytes=40 << 20),
+        cost_estimate=pl.CostEstimate(flops=10**10, transcendentals=10**8, bytes_accessed=10**8),
         name="stencil",
     )(*operands)
 
 
-def response_kernel(owners, ranks, records, strain_ref, column_ref, pan0, meta0, pan1, meta1, out_ref):
+def response_kernel(owners, ranks, records, strain_ref, column_ref, *refs):
     points = column_ref.shape[1]
     sent = owners * ranks
     group = LANES // ranks
     columns = strain_ref.shape[0] // STEPS
-    total = None
-    for pan, meta in ((pan0, meta0), (pan1, meta1)):
+    total, out_ref = None, refs[-1]
+    friendly = ranks % 16 == 0
+    for half in range(2):
+        pan = refs[half if friendly else 2 * half]
+        length = sent // pan.shape[0]
         rows = []
         for k in range(2):
-            table = meta[k].astype(jnp.float32)
+            table = pan[:, 6 * length + k, :] if friendly else refs[2 * half + 1][k]
+            table = table.astype(jnp.float32)
             parts = [
                 jnp.sum(table[g * group : (g + 1) * group], axis=0, keepdims=True) for g in range(owners // group)
             ]
@@ -221,7 +306,6 @@
         spread = (iota((points, sent), 0) == slot.astype(jnp.int32)).astype(jnp.bfloat16)
         table = jnp.broadcast_to(column_ref[...].astype(jnp.float32), (8, points)).astype(jnp.bfloat16)
         column = jnp.dot(table, spread, preferred_element_type=jnp.float32)[:1].astype(jnp.int32)
-        length = pan.shape[1] // 6
         grid = None
         for i in range(3):
             right = jnp.concatenate(
@@ -297,11 +381,10 @@
     ranks = entries // owners
     components = slip_panels.shape[2]
 
-    fields = jnp.concatenate(
-        [displacement[0], previous[0], first_lame[None], shear_modulus[None], buoyancy[None]], axis=0
+    merged = gys == 2
+    fields, upward, downward, *edges = prepare(
+        halo, merged, displacement, previous, first_lame, shear_modulus, buoyancy
     )
-    merged = gys == 2
-    gy = lax.axis_index("gy")
 
     def send(value, dx, dy):
         pairs = shift_pairs(gxs, gys, dx, dy)
@@ -309,23 +392,19 @@
             pairs = pairs + shift_pairs(gxs, gys, dx, -dy)
         return lax.ppermute(value, OWNERS_AXES, pairs)
 
-    x_low = send(fields[:, nx - halo :], 1, 0)
-    x_high = send(fields[:, :halo], -1, 0)
     if merged:
-        edge = lax.dynamic_slice_in_dim(fields, jnp.where(gy == 0, ny - halo, 0), halo, axis=2)
-        sides = [send(edge, 0, 1), send(edge, 1, 1), send(edge, -1, 1)]
+        sides = [send(edges[0], dx, 1) for dx in (0, 1, -1)]
     else:
-        upper, lower = fields[:, :, ny - halo :], fields[:, :, :halo]
-        sides = [send(upper, dx, 1) for dx in (0, 1, -1)] + [send(lower, dx, -1) for dx in (0, 1, -1)]
-
+        sides = [send(edge, dx, dy) for edge, dy in zip(edges, (1, -1)) for dx in (0, 1, -1)]
+    x_low, x_high = send(upward, 1, 0), send(downward, -1, 0)
+
+    sides[0], slip_panels = lax.optimization_barrier((sides[0], slip_panels))
     panels = slip_panels.reshape(entries, components, nz).transpose(1, 0, 2)
     payload = pack(owners, slots, ranks, rupture_tiles, slip_offsets, panels)
     arrived = lax.all_to_all(payload, OWNERS_AXES, split_axis=0, concat_axis=0, tiled=True)
+    final, strain = stencil(halo, merged, fields, x_low, x_high, sides)
+    arrived, strain = lax.optimization_barrier((arrived, strain))
     other = lax.ppermute(arrived, "comp", [(0, 1), (1, 0)])
-
-    final, strain = stencil(
-        halo, merged, displacement, previous, first_lame, shear_modulus, buoyancy, x_low, x_high, sides
-    )
     halves = [unpack(owners, ranks, components, v) for v in (arrived, other)]
     partial = respond(owners, ranks, records, strain, tile_column.reshape(1, slots), halves)
     summed = owner_sum(partial, owners)

time: 62.1 us -> 53.3 us (0.86)
  local copies, waits for them, and re-layouts: 7.4 us -> 1.44 us
  waiting for transfers between devices: 19.9 us -> 14.9 us
  Pallas kernels: 9.43 us -> 11.9 us
  starting transfers between devices: 22.2 us -> 24 us
  other arithmetic: 1.79 us -> 0.01 us
    ppermute x5, waiting for transfers between devices: 8.77 us -> 0.01 us  [send(): return lax.ppermute(value, OWNERS_AXES, pairs)]
    unnamed x17 -> x6, local copies, waits for them, and re-layouts: 5.85 us -> 0.01 us
    ppermute x5, starting transfers between devices: 10.7 us -> 13.6 us  [send(): return lax.ppermute(value, OWNERS_AXES, pairs)]
    pallas_call x1 -> x2, Pallas kernels: 2.37 us -> 4.82 us  [the longest x1 2.41 us: prepare(): pl.pallas_call(functools.partial(prepare_kernel, halo, merged), out_shape...]
    concatenate x1 -> x0, other arithmetic: 1.78 us -> none  [pack(): return jnp.concatenate([body, meta.transpose(1, 0, 2)], axis=1)]
    ppermute x1, waiting for transfers between devices: 0.01 us -> 1.74 us  [body(): other = lax.ppermute(arrived, 'comp', [(0, 1), (1, 0)])]
    all_to_all x1, waiting for transfers between devices: 3.5 us -> 4.81 us  [body(): lax.all_to_all(payload, OWNERS_AXES, split_axis=0, concat_axis=0, tiled=T...]
    optimization_barrier x0 -> x1, local copies, waits for them, and re-layouts: none -> 0.78 us  [body(): sides[0], slip_panels = lax.optimization_barrier((sides[0], slip_panels))]
  transfers between devices with their start and end apart: 10 -> 10, of which waited for: 7 -> 5; matrix products, arithmetic and copies ran while one was open for 0% -> 1% of each run, Pallas kernels for 9% -> 15%
where the time goes in v2:
time: 53.3 us; the launch traced here: 52.9 us
  starting transfers between devices  24 us (45%)
  waiting for transfers between devices  14.9 us (28%)
  Pallas kernels  11.9 us (22%)
  local copies, waits for them, and re-layouts  1.44 us (3%)
  between operations  0.74 us (1%)
    ppermute x5, starting transfers between devices, send(): return lax.ppermute(value, OWNERS_AXES, pairs)  13.6 us
    ppermute x3, waiting for transfers between devices, owner_sum(): lax.ppermute(value, OWNERS_AXES, [(i, i ^ bit) for i in range(owners)])  8.31 us
    all_to_all x1, starting transfers between devices, body(): lax.all_to_all(payload, OWNERS_AXES, split_axis=0, concat_axis=0, tiled=T...  7 us
    pallas_call x1, Pallas kernels, stencil(): pl.pallas_call(functools.partial(stencil_kernel, halo, merged), out_shape...  5.77 us
    all_to_all x1, waiting for transfers between devices, body(): lax.all_to_all(payload, OWNERS_AXES, split_axis=0, concat_axis=0, tiled=T...  4.81 us
    ppermute x3, starting transfers between devices, owner_sum(): lax.ppermute(value, OWNERS_AXES, [(i, i ^ bit) for i in range(owners)])  3.37 us
    pallas_call x1, Pallas kernels, prepare(): pl.pallas_call(functools.partial(prepare_kernel, halo, merged), out_shape...  2.41 us
    pallas_call x1, Pallas kernels, pack(): pl.pallas_call(kernel, out_shape=jax.ShapeDtypeStruct((owners, components...  2.41 us
  transfers between devices with their start and end apart: 10, of which 5 were waited for; matrix products, arithmetic and copies ran while one was open for 1% of the time, Pallas kernels for 15%

profile of v2, /device:TPU:0, one launch (start us, length us, event | category | flops | bytes accessed | tf_op | source)
XLA Modules:
  0.0 52.9 jit_solution(3873108084196507006)
XLA Ops:
  0.6 0.0 copy-start.2
  0.6 2.4 %prepare.1 = (f32[9,4,32,128]{3,2,1,0:T(8,128)}, f32[32,32,128]{2,1,0:T(8,128)}, f32[30,32,128]{2,1,0:T(8,128)}, f32[9,4,4,128]{3,2,1,0:T(4,128)}) custom-call(f32[1,3,4,32,128]{4,3,2,1,0:T(8,128)} %refs_0_.1, f32[1,3,4,32,128]{4,3,2,1,0:T(8,128)} %refs_1_.1, f32[4,32,128]{2,1,0:T(8,128)} %refs_2_.1, f32[4,32,128]{2,1,0:T(8,128)} %refs_3_.1, ...), custom_call_target="tpu_custom_call" | custom-call | tf_op jit(solution)/shard_map/prepare/pallas_call | solution.py:162
  3.1 5.0 %collective-permute-start = (f32[32,32,128]{2,1,0:T(8,128)}, f32[32,32,128]{2,1,0:T(8,128)S(1)}, u32[]{:S(2)}, u32[]{:S(2)}) collective-permute-start(f32[32,32,128]{2,1,0:T(8,128)} %get-tuple-element.13), channel_id=1, source_target_pairs={{0,4},{2,6},{4,8},{6,10},{8,12},{10,14},{1,5},{3,7},{5,9},{7,11},{... | collective-permute-start | bytes 1572872 | tf_op jit(solution)/shard_map/ppermute | solution.py:393
  8.0 1.3 %collective-permute-start.1 = (f32[30,32,128]{2,1,0:T(8,128)}, f32[30,32,128]{2,1,0:T(8,128)S(1)}, u32[]{:S(2)}, u32[]{:S(2)}) collective-permute-start(f32[30,32,128]{2,1,0:T(8,128)} %get-tuple-element.14), channel_id=1, source_target_pairs={{4,0},{6,2},{8,4},{10,6},{12,8},{14,10},{5,1},{7,3},{9,5},{11,7},{... | collective-permute-start | bytes 1474568 | tf_op jit(solution)/shard_map/ppermute | solution.py:393
  9.3 1.6 %collective-permute-start.2 = (f32[9,4,4,128]{3,2,1,0:T(4,128)}, f32[9,4,4,128]{3,2,1,0:T(4,128)S(1)}, u32[]{:S(2)}, u32[]{:S(2)}) collective-permute-start(f32[9,4,4,128]{3,2,1,0:T(4,128)} %get-tuple-element.15), channel_id=1, source_target_pairs={{0,2},{4,6},{8,10},{12,14},{2,0},{6,4},{10,8},{14,12},{1,3},{5,7},... | collective-permute-start | bytes 221192 | tf_op jit(solution)/shard_map/ppermute | solution.py:393
  10.9 4.5 %collective-permute-start.3 = (f32[9,4,4,128]{3,2,1,0:T(4,128)}, f32[9,4,4,128]{3,2,1,0:T(4,128)S(1)}, u32[]{:S(2)}, u32[]{:S(2)}) collective-permute-start(f32[9,4,4,128]{3,2,1,0:T(4,128)} %get-tuple-element.15), channel_id=1, source_target_pairs={{0,6},{4,10},{8,14},{2,4},{6,8},{10,12},{1,7},{5,11},{9,15},{3,5},... | collective-permute-start | bytes 221192 | tf_op jit(solution)/shard_map/ppermute | solution.py:393
  15.4 1.3 %collective-permute-start.4 = (f32[9,4,4,128]{3,2,1,0:T(4,128)}, f32[9,4,4,128]{3,2,1,0:T(4,128)S(1)}, u32[]{:S(2)}, u32[]{:S(2)}) collective-permute-start(f32[9,4,4,128]{3,2,1,0:T(4,128)} %get-tuple-element.15), channel_id=1, source_target_pairs={{4,2},{8,6},{12,10},{6,0},{10,4},{14,8},{5,3},{9,7},{13,11},{7,1},... | collective-permute-start | bytes 221192 | tf_op jit(solution)/shard_map/ppermute | solution.py:393
  16.7 0.0 collective-permute-done.2.refs_3_
  16.7 0.0 copy-done.2
  16.7 0.8 %copy.11 = bf16[16,16,6,128]{3,1,0,2:T(8,128)(2,1)} copy(bf16[16,16,6,128]{3,1,2,0:T(8,128)(2,1)S(1)} %copy-done.2) | data formatting | bytes 786432 | tf_op jit(solution)/shard_map/optimization_barrier | solution.py:401
  17.5 2.4 %pack.1 = bf16[8,200,128]{2,1,0:T(8,128)(2,1)} custom-call(s32[16,16]{1,0:T(8,128)} %tiles_ref.1, s32[16,16]{1,0:T(8,128)} %offsets_ref.1, bf16[6,256,128]{2,1,0:T(8,128)(2,1)} %bitcast.9), custom_call_target="tpu_custom_call" | custom-call | tf_op jit(solution)/shard_map/pack/pallas_call | solution.py:79
  19.9 0.0 copy-start.1
  19.9 7.0 %all-to-all-start = ((bf16[8,200,128]{2,1,0:T(8,128)(2,1)}), bf16[8,200,128]{2,1,0:T(8,128)(2,1)S(1)}, u32[]{:S(2)}, u32[]{:S(2)}) async-start(bf16[8,200,128]{2,1,0:T(8,128)(2,1)} %pack.1), calls=%async_computation | async-start | bytes 819200 | tf_op jit(solution)/shard_map/all_to_all | solution.py:404
  26.9 0.0 collective-permute-done.3.refs_4_
  26.9 0.0 collective-permute-done.4.refs_5_
  26.9 0.0 collective-permute-done.1.refs_2_
  26.9 0.0 collective-permute-done.refs_1_
  27.0 0.0 copy-done.1
  27.0 5.8 %stencil.1 = (f32[1,3,4,32,128]{4,3,2,1,0:T(8,128)}, bf16[512,768]{1,0:T(8,128)(2,1)S(1)}) custom-call(f32[9,4,32,128]{3,2,1,0:T(8,128)S(1)} %copy-done.1, f32[32,32,128]{2,1,0:T(8,128)S(1)} %collective-permute-done.refs_1_, f32[30,32,128]{2,1,0:T(8,128)S(1)} %collective-permute-done.1.refs_2_, f32[9,4,4,128]{3,2,1,0:T(4,128)S(1)} %collective-permute-done.2.refs_3_, ...), custom_call_target="tpu_custom_call" | custom-call | flops 10000000000 | bytes 100000000 | tf_op jit(solution)/shard_map/stencil/pallas_call | solution.py:269
  32.7 4.8 %all-to-all-done.refs_0_ = bf16[8,200,128]{2,1,0:T(8,128)(2,1)S(1)} async-done(((bf16[8,200,128]{2,1,0:T(8,128)(2,1)}), bf16[8,200,128]{2,1,0:T(8,128)(2,1)S(1)}, u32[]{:S(2)}, u32[]{:S(2)}) %all-to-all-start) | async-done | bytes 409632 | tf_op jit(solution)/shard_map/all_to_all | solution.py:404
  37.5 0.0 copy-start
  37.5 0.0 collective-permute-start.5
  37.5 1.7 %collective-permute-done.5.refs_1_ = bf16[8,200,128]{2,1,0:T(8,128)(2,1)S(1)} collective-permute-done((bf16[8,200,128]{2,1,0:T(8,128)(2,1)S(1)}, bf16[8,200,128]{2,1,0:T(8,128)(2,1)S(1)}, u32[]{:S(2)}, u32[]{:S(2)}) %collective-permute-start.5) | collective-permute-done | bytes 409632 | tf_op jit(solution)/shard_map/ppermute | solution.py:407
  39.3 0.0 copy-done
  39.3 1.3 %respond.1 = f32[4,128]{1,0:T(4,128)S(1)} custom-call(bf16[512,768]{1,0:T(8,128)(2,1)S(1)} %get-tuple-element.20.strain_ref, s32[1,128]{1,0:T(1,128)S(1)} %bitcast.8, bf16[8,200,128]{2,1,0:T(8,128)(2,1)S(1)} %all-to-all-done.refs_0_, bf16[8,200,128]{2,1,0:T(8,128)(2,1)S(1)} %collective-permute-done.5.refs_1_), custom_call_target="tpu_custom_call" | custom-call | tf_op jit(solution)/shard_map/respond/pallas_call | solution.py:344
  40.6 1.5 %collective-permute-start.6 = (f32[4,128]{1,0:T(4,128)S(1)}, f32[4,128]{1,0:T(4,128)S(1)}, u32[]{:S(2)}, u32[]{:S(2)}) collective-permute-start(f32[4,128]{1,0:T(4,128)S(1)} %respond.1), channel_id=1, source_target_pairs={{0,2},{2,0},{4,6},{6,4},{8,10},{10,8},{12,14},{14,12},{1,3},{3,1},... | collective-permute-start | bytes 6152 | tf_op jit(solution)/shard_map/ppermute | solution.py:368
  42.1 2.1 %collective-permute-done.6 = f32[4,128]{1,0:T(4,128)S(1)} collective-permute-done((f32[4,128]{1,0:T(4,128)S(1)}, f32[4,128]{1,0:T(4,128)S(1)}, u32[]{:S(2)}, u32[]{:S(2)}) %collective-permute-start.6) | collective-permute-done | bytes 2080 | tf_op jit(solution)/shard_map/ppermute | solution.py:368
  44.2 0.9 %collective-permute-start.7 = (f32[4,128]{1,0:T(4,128)S(1)}, f32[4,128]{1,0:T(4,128)S(1)}, u32[]{:S(2)}, u32[]{:S(2)}) collective-permute-start(f32[4,128]{1,0:T(4,128)S(1)} %add.15), channel_id=1, source_target_pairs={{0,4},{2,6},{4,0},{6,2},{8,12},{10,14},{12,8},{14,10},{1,5},{3,7},... | collective-permute-start | bytes 6152 | tf_op jit(solution)/shard_map/ppermute | solution.py:368
  45.1 2.7 %collective-permute-done.7 = f32[4,128]{1,0:T(4,128)S(1)} collective-permute-done((f32[4,128]{1,0:T(4,128)S(1)}, f32[4,128]{1,0:T(4,128)S(1)}, u32[]{:S(2)}, u32[]{:S(2)}) %collective-permute-start.7) | collective-permute-done | bytes 2080 | tf_op jit(solution)/shard_map/ppermute | solution.py:368
  47.8 1.0 %collective-permute-start.8 = (f32[4,128]{1,0:T(4,128)S(1)}, f32[4,128]{1,0:T(4,128)S(1)}, u32[]{:S(2)}, u32[]{:S(2)}) collective-permute-start(f32[4,128]{1,0:T(4,128)S(1)} %add.16), channel_id=1, source_target_pairs={{0,8},{2,10},{4,12},{6,14},{8,0},{10,2},{12,4},{14,6},{1,9},{3,11}... | collective-permute-start | bytes 6152 | tf_op jit(solution)/shard_map/ppermute | solution.py:368
  48.8 3.5 %collective-permute-done.8 = f32[4,128]{1,0:T(4,128)S(1)} collective-permute-done((f32[4,128]{1,0:T(4,128)S(1)}, f32[4,128]{1,0:T(4,128)S(1)}, u32[]{:S(2)}, u32[]{:S(2)}) %collective-permute-start.8) | collective-permute-done | bytes 2080 | tf_op jit(solution)/shard_map/ppermute | solution.py:368
  52.3 0.7 %dynamic-slice_bitcast_fusion = f32[1,16,4]{1,2,0:T(4,128)} fusion(f32[4,128]{1,0:T(4,128)S(1)} %add.17, s32[]{:T(128)S(6)} %select_n.3), kind=kLoop, calls=%fused_computation | loop fusion | bytes 516 | tf_op jit(solution)/shard_map/broadcast_in_dim | solution.py:412
  (3 shorter events, 0.0 us)
Async XLA Ops:
  0.6 16.1 %copy-start.2 = (bf16[16,16,6,128]{3,1,2,0:T(8,128)(2,1)S(1)}, bf16[16,16,6,128]{3,1,2,0:T(8,128)(2,1)}, u32[]{:S(2)}) copy-start(bf16[16,16,6,128]{3,1,2,0:T(8,128)(2,1)} %param.17) | copy-start | bytes 1179652
  3.1 23.9 %collective-permute-start = (f32[32,32,128]{2,1,0:T(8,128)}, f32[32,32,128]{2,1,0:T(8,128)S(1)}, u32[]{:S(2)}, u32[]{:S(2)}) collective-permute-start(f32[32,32,128]{2,1,0:T(8,128)} %get-tuple-element.13), channel_id=1, source_target_pairs={{0,4},{2,6},{4,8},{6,10},{8,12},{10,14},{1,5},{3,7},{5,9},{7,11},{... | collective-permute-start | bytes 1572872 | tf_op jit(solution)/shard_map/ppermute | solution.py:393
  8.0 18.9 %collective-permute-start.1 = (f32[30,32,128]{2,1,0:T(8,128)}, f32[30,32,128]{2,1,0:T(8,128)S(1)}, u32[]{:S(2)}, u32[]{:S(2)}) collective-permute-start(f32[30,32,128]{2,1,0:T(8,128)} %get-tuple-element.14), channel_id=1, source_target_pairs={{4,0},{6,2},{8,4},{10,6},{12,8},{14,10},{5,1},{7,3},{9,5},{11,7},{... | collective-permute-start | bytes 1474568 | tf_op jit(solution)/shard_map/ppermute | solution.py:393
  9.3 7.4 %collective-permute-start.2 = (f32[9,4,4,128]{3,2,1,0:T(4,128)}, f32[9,4,4,128]{3,2,1,0:T(4,128)S(1)}, u32[]{:S(2)}, u32[]{:S(2)}) collective-permute-start(f32[9,4,4,128]{3,2,1,0:T(4,128)} %get-tuple-element.15), channel_id=1, source_target_pairs={{0,2},{4,6},{8,10},{12,14},{2,0},{6,4},{10,8},{14,12},{1,3},{5,7},... | collective-permute-start | bytes 221192 | tf_op jit(solution)/shard_map/ppermute | solution.py:393
  10.9 16.0 %collective-permute-start.3 = (f32[9,4,4,128]{3,2,1,0:T(4,128)}, f32[9,4,4,128]{3,2,1,0:T(4,128)S(1)}, u32[]{:S(2)}, u32[]{:S(2)}) collective-permute-start(f32[9,4,4,128]{3,2,1,0:T(4,128)} %get-tuple-element.15), channel_id=1, source_target_pairs={{0,6},{4,10},{8,14},{2,4},{6,8},{10,12},{1,7},{5,11},{9,15},{3,5},... | collective-permute-start | bytes 221192 | tf_op jit(solution)/shard_map/ppermute | solution.py:393
  15.4 11.5 %collective-permute-start.4 = (f32[9,4,4,128]{3,2,1,0:T(4,128)}, f32[9,4,4,128]{3,2,1,0:T(4,128)S(1)}, u32[]{:S(2)}, u32[]{:S(2)}) collective-permute-start(f32[9,4,4,128]{3,2,1,0:T(4,128)} %get-tuple-element.15), channel_id=1, source_target_pairs={{4,2},{8,6},{12,10},{6,0},{10,4},{14,8},{5,3},{9,7},{13,11},{7,1},... | collective-permute-start | bytes 221192 | tf_op jit(solution)/shard_map/ppermute | solution.py:393
  19.9 7.0 %copy-start.1 = (f32[9,4,32,128]{3,2,1,0:T(8,128)S(1)}, f32[9,4,32,128]{3,2,1,0:T(8,128)}, u32[]{:S(2)}) copy-start(f32[9,4,32,128]{3,2,1,0:T(8,128)} %get-tuple-element.12.refs_0_) | copy-start | bytes 1769476
  19.9 17.6 %all-to-all-start = ((bf16[8,200,128]{2,1,0:T(8,128)(2,1)}), bf16[8,200,128]{2,1,0:T(8,128)(2,1)S(1)}, u32[]{:S(2)}, u32[]{:S(2)}) async-start(bf16[8,200,128]{2,1,0:T(8,128)(2,1)} %pack.1), calls=%async_computation | async-start | bytes 819200 | tf_op jit(solution)/shard_map/all_to_all | solution.py:404
  37.5 1.8 %copy-start = (s32[128]{0:T(128)S(1)}, s32[128]{0:T(128)}, u32[]{:S(2)}) copy-start(s32[128]{0:T(128)} %param.14) | copy-start | bytes 1540
  37.5 1.7 %collective-permute-start.5 = (bf16[8,200,128]{2,1,0:T(8,128)(2,1)S(1)}, bf16[8,200,128]{2,1,0:T(8,128)(2,1)S(1)}, u32[]{:S(2)}, u32[]{:S(2)}) collective-permute-start(bf16[8,200,128]{2,1,0:T(8,128)(2,1)S(1)} %all-to-all-done.refs_0_), channel_id=1, source_target_pairs={{0,1},{1,0},{2,3},{3,2},{4,5},{5,4},{6,7},{7,6},{8,9},{9,8},{10,11... | collective-permute-start | bytes 1228808 | tf_op jit(solution)/shard_map/ppermute | solution.py:407
  40.6 3.6 %collective-permute-start.6 = (f32[4,128]{1,0:T(4,128)S(1)}, f32[4,128]{1,0:T(4,128)S(1)}, u32[]{:S(2)}, u32[]{:S(2)}) collective-permute-start(f32[4,128]{1,0:T(4,128)S(1)} %respond.1), channel_id=1, source_target_pairs={{0,2},{2,0},{4,6},{6,4},{8,10},{10,8},{12,14},{14,12},{1,3},{3,1},... | collective-permute-start | bytes 6152 | tf_op jit(solution)/shard_map/ppermute | solution.py:368
  44.2 3.6 %collective-permute-start.7 = (f32[4,128]{1,0:T(4,128)S(1)}, f32[4,128]{1,0:T(4,128)S(1)}, u32[]{:S(2)}, u32[]{:S(2)}) collective-permute-start(f32[4,128]{1,0:T(4,128)S(1)} %add.15), channel_id=1, source_target_pairs={{0,4},{2,6},{4,0},{6,2},{8,12},{10,14},{12,8},{14,10},{1,5},{3,7},... | collective-permute-start | bytes 6152 | tf_op jit(solution)/shard_map/ppermute | solution.py:368
  47.8 4.5 %collective-permute-start.8 = (f32[4,128]{1,0:T(4,128)S(1)}, f32[4,128]{1,0:T(4,128)S(1)}, u32[]{:S(2)}, u32[]{:S(2)}) collective-permute-start(f32[4,128]{1,0:T(4,128)S(1)} %add.16), channel_id=1, source_target_pairs={{0,8},{2,10},{4,12},{6,14},{8,0},{10,2},{12,4},{14,6},{1,9},{3,11}... | collective-permute-start | bytes 6152 | tf_op jit(solution)/shard_map/ppermute | solution.py:368

commit v3 on v2

--- a/solution.py
+++ b/solution.py
@@ -107,17 +107,56 @@
     return body.reshape(1, components * owners * ranks, LANES), meta
 
 
-def planes_for(side, halo, nx):
-    plan = []
+def planes_for(field, side, halo):
+    return halo if field < 3 or (side > 0 and field in (6, 7)) else halo - 1
+
+
+def coded_planes(side, halo):
+    return sum(planes_for(f, side, halo) + (f < 6) for f in range(FIELDS))
+
+
+def encode(side, halo, nx, read, write):
+    at = 0
     for field in range(FIELDS):
-        count = halo if field < 3 or (side > 0 and field in (6, 7)) else halo - 1
-        plan.append((field, nx - count if side > 0 else 0, count))
-    return plan
+        near = None
+        for k in range(planes_for(field, side, halo)):
+            value = read(field, nx - 1 - k if side > 0 else k)
+            if field >= 6:
+                parts = [value.astype(jnp.bfloat16)]
+            elif near is None:
+                high = value.astype(jnp.bfloat16)
+                low = (value - high.astype(jnp.float32)).astype(jnp.bfloat16)
+                near = high.astype(jnp.float32) + low.astype(jnp.float32)
+                parts = [high, low]
+            else:
+                step = (value - near).astype(jnp.bfloat16)
+                near = near + step.astype(jnp.float32)
+                parts = [step]
+            for part in parts:
+                write(at, part)
+                at += 1
+
+
+def decode(side, halo, nx, read, write):
+    at = 0
+    for field in range(FIELDS):
+        near = None
+        for k in range(planes_for(field, side, halo)):
+            value = read(at).astype(jnp.float32)
+            at += 1
+            if field < 6:
+                if near is None:
+                    value = value + read(at).astype(jnp.float32)
+                    at += 1
+                else:
+                    value = near + value
+                near = value
+            write(field, halo - 1 - k if side > 0 else halo + nx + k, value)
 
 
 def prepare_kernel(halo, merged, *refs):
-    disp, prev, lam, mu, buoy, fields, up, down = refs[:8]
-    edges, sem = refs[8:-1], refs[-1]
+    disp, prev, lam, mu, buoy, up, down = refs[:7]
+    edges, fields, sem = refs[7:-2], refs[-2], refs[-1]
     nx, ny, nz = lam.shape
     copies = [
         pltpu.make_async_copy(disp.at[0], fields.at[pl.ds(0, 3)], sem.at[0]),
@@ -128,43 +167,47 @@
     ]
     for copy in copies:
         copy.start()
-    gy = lax.axis_index("gy")
-    done = 0
-    for side, target in ((1, up), (-1, down)):
-        at = 0
-        for field, first, count in planes_for(side, halo, nx):
-            while done < len(copies) and field >= (0, 3, 6, 7, 8)[done]:
-                copies[done].wait()
-                done += 1
-            target[at : at + count] = fields[field, first : first + count]
-            at += count
-    high, low = pl.ds(ny - halo, halo), pl.ds(0, halo)
+    for copy in copies:
+        copy.wait()
+
+    def coded(side, rows, target):
+        def write(at, value):
+            target[at] = value
+
+        encode(side, halo, nx, lambda f, x: fields[f, x, rows, :], write)
+
+    every, high, low = pl.ds(0, ny), pl.ds(ny - halo, halo), pl.ds(0, halo)
+    coded(1, every, up)
+    coded(-1, every, down)
+
+    def edge(rows, targets):
+        targets[0][...] = fields[:, :, rows, :]
+        coded(1, rows, targets[1])
+        coded(-1, rows, targets[2])
+
     if merged:
-
-        @pl.when(gy == 0)
-        def _():
-            edges[0][...] = fields[:, :, high, :]
-
-        @pl.when(gy != 0)
-        def _():
-            edges[0][...] = fields[:, :, low, :]
+        gy = lax.axis_index("gy")
+        pl.when(gy == 0)(lambda: edge(high, edges))
+        pl.when(gy != 0)(lambda: edge(low, edges))
     else:
-        edges[0][...] = fields[:, :, high, :]
-        edges[1][...] = fields[:, :, low, :]
+        edge(high, edges[:3])
+        edge(low, edges[3:])
 
 
 def prepare(halo, merged, disp, prev, lam, mu, buoy):
     nx, ny, nz = lam.shape
     vmem, anywhere = pl.BlockSpec(memory_space=pltpu.VMEM), pl.BlockSpec(memory_space=pl.ANY)
-    totals = [sum(count for _, _, count in planes_for(side, halo, nx)) for side in (1, -1)]
-    shapes = [(FIELDS, nx, ny, nz)] + [(total, ny, nz) for total in totals]
-    shapes += [(FIELDS, nx, halo, nz)] * (1 if merged else 2)
+    counts = [coded_planes(side, halo) for side in (1, -1)]
+    shapes = [jax.ShapeDtypeStruct((count, ny, nz), jnp.bfloat16) for count in counts]
+    edge = [jax.ShapeDtypeStruct((FIELDS, nx, halo, nz), jnp.float32)]
+    edge += [jax.ShapeDtypeStruct((count, halo, nz), jnp.bfloat16) for count in counts]
+    shapes += edge if merged else edge * 2
     return pl.pallas_call(
         functools.partial(prepare_kernel, halo, merged),
-        out_shape=[jax.ShapeDtypeStruct(shape, jnp.float32) for shape in shapes],
+        out_shape=shapes,
         in_specs=[anywhere] * 5,
         out_specs=[vmem] * len(shapes),
-        scratch_shapes=[pltpu.SemaphoreType.DMA((5,))],
+        scratch_shapes=[pltpu.VMEM((FIELDS, nx, ny, nz), jnp.float32), pltpu.SemaphoreType.DMA((5,))],
         name="prepare",
     )(disp, prev, lam, mu, buoy)
 
@@ -174,38 +217,34 @@
 
 
 def stencil_kernel(halo, merged, *refs):
-    fields, x_low, x_high = refs[:3]
-    sides = refs[3:9] if not merged else refs[3:6] * 2
+    disp, prev, lam, mu, buoy, x_low, x_high = refs[:7]
+    sides = refs[7:13] if not merged else refs[7:10] * 2
     out_ref, strain_ref = refs[-7:-5]
     wave, first, second, scale = refs[-5:-1]
-    _, nx, ny, nz = fields.shape
+    nx, ny, nz = lam.shape
     tall = ny + 2 * PAD
     gy = lax.axis_index("gy")
     own_x, own_y = pl.ds(halo, nx), pl.ds(PAD, ny)
-    lows, highs = pl.ds(0, halo), pl.ds(halo + nx, halo)
-
     targets = [wave.at[0, i] for i in range(3)] + [wave.at[1, i] for i in range(3)] + [first, second, scale]
-    low_at = high_at = 0
-    for f, target in enumerate(targets):
-
-        def put(xs, ys, value, f=f, target=target):
-            target[xs, ys, :] = value * (TIME_STEP * TIME_STEP) if f == 8 else value
-
-        put(own_x, own_y, fields[f])
-        _, _, count = planes_for(1, halo, nx)[f]
-        put(pl.ds(halo - count, count), own_y, x_low[low_at : low_at + count])
-        low_at += count
-        _, _, count = planes_for(-1, halo, nx)[f]
-        put(pl.ds(halo + nx, count), own_y, x_high[high_at : high_at + count])
-        high_at += count
-        for s, ys in ((0, pl.ds(PAD - halo, halo)), (1, pl.ds(PAD + ny, halo))):
-            middle, low, high = [r[f] for r in sides[3 * s : 3 * s + 3]]
-            if merged:
-                here = gy == (1 - s)
-                middle, low, high = [jnp.where(here, v, 0.0) for v in (middle, low, high)]
-            put(own_x, ys, middle)
-            put(lows, ys, low)
-            put(highs, ys, high)
+
+    def put(field, xs, ys, value):
+        targets[field][xs, ys, :] = value * (TIME_STEP * TIME_STEP) if field == 8 else value
+
+    owns = [disp[0, i] for i in range(3)] + [prev[0, i] for i in range(3)] + [lam[...], mu[...], buoy[...]]
+    for f, own in enumerate(owns):
+        put(f, own_x, own_y, own)
+    decode(1, halo, nx, lambda at: x_low[at], lambda f, x, v: put(f, x, own_y, v))
+    decode(-1, halo, nx, lambda at: x_high[at], lambda f, x, v: put(f, x, own_y, v))
+    for s, ys in ((0, pl.ds(PAD - halo, halo)), (1, pl.ds(PAD + ny, halo))):
+        middle, low, high = sides[3 * s : 3 * s + 3]
+
+        def only(value, s=s):
+            return jnp.where(gy == (1 - s), value, 0.0) if merged else value
+
+        for f in range(FIELDS):
+            put(f, own_x, ys, only(middle[f]))
+        decode(1, halo, nx, lambda at: low[at], lambda f, x, v: put(f, x, ys, only(v)))
+        decode(-1, halo, nx, lambda at: high[at], lambda f, x, v: put(f, x, ys, only(v)))
 
     lane = iota((tall, nz), 1)
     not_last, not_first = lane < nz - 1, lane > 0
@@ -261,11 +300,11 @@
                 carry = lax.fori_loop(lo, hi, functools.partial(plane, step, cur, own), carry)
 
 
-def stencil(halo, merged, fields, x_low, x_high, sides):
-    _, nx, ny, nz = fields.shape
+def stencil(halo, merged, disp, prev, lam, mu, buoy, x_low, x_high, sides):
+    nx, ny, nz = lam.shape
     tall, wide = ny + 2 * PAD, nx + 2 * halo
     vmem = pl.BlockSpec(memory_space=pltpu.VMEM)
-    operands = (fields, x_low, x_high, *sides)
+    operands = (disp, prev, lam, mu, buoy, x_low, x_high, *sides)
     return pl.pallas_call(
         functools.partial(stencil_kernel, halo, merged),
         out_shape=(
@@ -382,7 +421,7 @@
     components = slip_panels.shape[2]
 
     merged = gys == 2
-    fields, upward, downward, *edges = prepare(
+    upward, downward, *edges = prepare(
         halo, merged, displacement, previous, first_lame, shear_modulus, buoyancy
     )
 
@@ -392,17 +431,17 @@
             pairs = pairs + shift_pairs(gxs, gys, dx, -dy)
         return lax.ppermute(value, OWNERS_AXES, pairs)
 
-    if merged:
-        sides = [send(edges[0], dx, 1) for dx in (0, 1, -1)]
-    else:
-        sides = [send(edge, dx, dy) for edge, dy in zip(edges, (1, -1)) for dx in (0, 1, -1)]
+    ways = [(0, 1), (1, 1), (-1, 1)] + ([] if merged else [(0, -1), (1, -1), (-1, -1)])
+    sides = [send(edge, dx, dy) for edge, (dx, dy) in zip(edges, ways)]
     x_low, x_high = send(upward, 1, 0), send(downward, -1, 0)
 
     sides[0], slip_panels = lax.optimization_barrier((sides[0], slip_panels))
     panels = slip_panels.reshape(entries, components, nz).transpose(1, 0, 2)
     payload = pack(owners, slots, ranks, rupture_tiles, slip_offsets, panels)
     arrived = lax.all_to_all(payload, OWNERS_AXES, split_axis=0, concat_axis=0, tiled=True)
-    final, strain = stencil(halo, merged, fields, x_low, x_high, sides)
+    final, strain = stencil(
+        halo, merged, displacement, previous, first_lame, shear_modulus, buoyancy, x_low, x_high, sides
+    )
     arrived, strain = lax.optimization_barrier((arrived, strain))
     other = lax.ppermute(arrived, "comp", [(0, 1), (1, 0)])
     halves = [unpack(owners, ranks, components, v) for v in (arrived, other)]

time: 53.3 us -> 53 us (level)
  transfers between devices with their start and end apart: 10 -> 10, of which waited for: 5 -> 5; matrix products, arithmetic and copies ran while one was open for 1% -> 1% of each run, Pallas kernels for 15% -> 16%
where the time goes in v3:
time: 53 us; the launch traced here: 52.7 us
  starting transfers between devices  24 us (45%)
  waiting for transfers between devices  14.8 us (28%)
  Pallas kernels  11.6 us (22%)
  local copies, waits for them, and re-layouts  1.45 us (3%)
  between operations  0.78 us (1%)
    ppermute x5, starting transfers between devices, send(): return lax.ppermute(value, OWNERS_AXES, pairs)  13.6 us
    ppermute x3, waiting for transfers between devices, owner_sum(): lax.ppermute(value, OWNERS_AXES, [(i, i ^ bit) for i in range(owners)])  8.31 us
    all_to_all x1, starting transfers between devices, body(): lax.all_to_all(payload, OWNERS_AXES, split_axis=0, concat_axis=0, tiled=T...  7.02 us
    pallas_call x1, Pallas kernels, stencil(): pl.pallas_call(functools.partial(stencil_kernel, halo, merged), out_shape...  5.77 us
    all_to_all x1, waiting for transfers between devices, body(): lax.all_to_all(payload, OWNERS_AXES, split_axis=0, concat_axis=0, tiled=T...  4.77 us
    ppermute x3, starting transfers between devices, owner_sum(): lax.ppermute(value, OWNERS_AXES, [(i, i ^ bit) for i in range(owners)])  3.37 us
    pallas_call x1, Pallas kernels, pack(): pl.pallas_call(kernel, out_shape=jax.ShapeDtypeStruct((owners, components...  2.41 us
    pallas_call x1, Pallas kernels, prepare(): pl.pallas_call(functools.partial(prepare_kernel, halo, merged), out_shape...  2.16 us
  transfers between devices with their start and end apart: 10, of which 5 were waited for; matrix products, arithmetic and copies ran while one was open for 1% of the time, Pallas kernels for 16%

profile of v3, /device:TPU:0, one launch (start us, length us, event | category | flops | bytes accessed | tf_op | source)
XLA Modules:
  0.0 52.7 jit_solution(4568284399486462704)
XLA Ops:
  0.6 0.0 copy-start.6
  0.6 2.2 %prepare.1 = (bf16[38,32,128]{2,1,0:T(8,128)(2,1)}, bf16[36,32,128]{2,1,0:T(8,128)(2,1)}, f32[9,4,4,128]{3,2,1,0:T(4,128)}, bf16[38,4,128]{2,1,0:T(4,128)(2,1)}, bf16[36,4,128]{2,1,0:T(4,128)(2,1)}) custom-call(f32[1,3,4,32,128]{4,3,2,1,0:T(8,128)} %refs_0_.3, f32[1,3,4,32,128]{4,3,2,1,0:T(8,128)} %refs_1_.3, f32[4,32,128]{2,1,0:T(8,128)} %refs_2_.3, ...), custom_call_target="tpu_custom_call" | custom-call | tf_op jit(solution)/shard_map/prepare/pallas_call | solution.py:205
  2.8 4.9 %collective-permute-start = (bf16[38,32,128]{2,1,0:T(8,128)(2,1)}, bf16[38,32,128]{2,1,0:T(8,128)(2,1)S(1)}, u32[]{:S(2)}, u32[]{:S(2)}) collective-permute-start(bf16[38,32,128]{2,1,0:T(8,128)(2,1)} %get-tuple-element.13), channel_id=1, source_target_pairs={{0,4},{2,6},{4,8},{6,10},{8,12},{10,14},{1,5},{3,7},{5,9},{7,11},{... | collective-permute-start | bytes 933896 | tf_op jit(solution)/shard_map/ppermute | solution.py:432
  7.8 1.3 %collective-permute-start.1 = (bf16[36,32,128]{2,1,0:T(8,128)(2,1)}, bf16[36,32,128]{2,1,0:T(8,128)(2,1)S(1)}, u32[]{:S(2)}, u32[]{:S(2)}) collective-permute-start(bf16[36,32,128]{2,1,0:T(8,128)(2,1)} %get-tuple-element.14), channel_id=1, source_target_pairs={{4,0},{6,2},{8,4},{10,6},{12,8},{14,10},{5,1},{7,3},{9,5},{11,7},{... | collective-permute-start | bytes 884744 | tf_op jit(solution)/shard_map/ppermute | solution.py:432
  9.1 1.6 %collective-permute-start.2 = (f32[9,4,4,128]{3,2,1,0:T(4,128)}, f32[9,4,4,128]{3,2,1,0:T(4,128)S(1)}, u32[]{:S(2)}, u32[]{:S(2)}) collective-permute-start(f32[9,4,4,128]{3,2,1,0:T(4,128)} %get-tuple-element.15), channel_id=1, source_target_pairs={{0,2},{4,6},{8,10},{12,14},{2,0},{6,4},{10,8},{14,12},{1,3},{5,7},... | collective-permute-start | bytes 221192 | tf_op jit(solution)/shard_map/ppermute | solution.py:432
  10.6 4.5 %collective-permute-start.3 = (bf16[38,4,128]{2,1,0:T(4,128)(2,1)}, bf16[38,4,128]{2,1,0:T(4,128)(2,1)S(1)}, u32[]{:S(2)}, u32[]{:S(2)}) collective-permute-start(bf16[38,4,128]{2,1,0:T(4,128)(2,1)} %get-tuple-element.17), channel_id=1, source_target_pairs={{0,6},{4,10},{8,14},{2,4},{6,8},{10,12},{1,7},{5,11},{9,15},{3,5},... | collective-permute-start | bytes 116744 | tf_op jit(solution)/shard_map/ppermute | solution.py:432
  15.1 1.3 %collective-permute-start.4 = (bf16[36,4,128]{2,1,0:T(4,128)(2,1)}, bf16[36,4,128]{2,1,0:T(4,128)(2,1)S(1)}, u32[]{:S(2)}, u32[]{:S(2)}) collective-permute-start(bf16[36,4,128]{2,1,0:T(4,128)(2,1)} %get-tuple-element.18), channel_id=1, source_target_pairs={{4,2},{8,6},{12,10},{6,0},{10,4},{14,8},{5,3},{9,7},{13,11},{7,1},... | collective-permute-start | bytes 110600 | tf_op jit(solution)/shard_map/ppermute | solution.py:432
  16.4 0.0 collective-permute-done.2.refs_7_
  16.4 0.0 copy-done.6
  16.5 0.8 %copy.11 = bf16[16,16,6,128]{3,1,0,2:T(8,128)(2,1)} copy(bf16[16,16,6,128]{3,1,2,0:T(8,128)(2,1)S(1)} %copy-done.6) | data formatting | bytes 786432 | tf_op jit(solution)/shard_map/optimization_barrier | solution.py:438
  17.2 2.4 %pack.1 = bf16[8,200,128]{2,1,0:T(8,128)(2,1)} custom-call(s32[16,16]{1,0:T(8,128)} %tiles_ref.1, s32[16,16]{1,0:T(8,128)} %offsets_ref.1, bf16[6,256,128]{2,1,0:T(8,128)(2,1)} %bitcast.9), custom_call_target="tpu_custom_call" | custom-call | tf_op jit(solution)/shard_map/pack/pallas_call | solution.py:79
  19.6 0.0 copy-start
  19.6 0.0 copy-start.1
  19.6 0.0 copy-start.2
  19.6 0.0 copy-start.3
  19.6 0.0 copy-start.4
  19.7 7.0 %all-to-all-start = ((bf16[8,200,128]{2,1,0:T(8,128)(2,1)}), bf16[8,200,128]{2,1,0:T(8,128)(2,1)S(1)}, u32[]{:S(2)}, u32[]{:S(2)}) async-start(bf16[8,200,128]{2,1,0:T(8,128)(2,1)} %pack.1), calls=%async_computation | async-start | bytes 819200 | tf_op jit(solution)/shard_map/all_to_all | solution.py:441
  26.7 0.0 collective-permute-done.4.refs_9_
  26.7 0.0 collective-permute-done.3.refs_8_
  26.7 0.0 collective-permute-done.1.refs_6_
  26.7 0.0 collective-permute-done.refs_5_
  26.7 0.0 copy-done
  26.7 0.0 copy-done.1
  26.7 0.0 copy-done.2
  26.7 0.0 copy-done.3
  26.8 0.0 copy-done.4
  26.8 5.8 %stencil.1 = (f32[1,3,4,32,128]{4,3,2,1,0:T(8,128)}, bf16[512,768]{1,0:T(8,128)(2,1)S(1)}) custom-call(f32[1,3,4,32,128]{4,3,2,1,0:T(8,128)S(1)} %copy-done, f32[1,3,4,32,128]{4,3,2,1,0:T(8,128)S(1)} %copy-done.1, f32[4,32,128]{2,1,0:T(8,128)S(1)} %copy-done.2, f32[4,32,128]{2,1,0:T(8,128)S(1)} %copy-done.3, f32[4,32,128]{2,1,0:T(8,128)S(1)} %copy-done.4, ...), custom_call_target="tpu_custom_call" | custom-call | flops 10000000000 | bytes 100000000 | tf_op jit(solution)/shard_map/stencil/pallas_call | solution.py:308
  32.5 4.8 %all-to-all-done.refs_0_ = bf16[8,200,128]{2,1,0:T(8,128)(2,1)S(1)} async-done(((bf16[8,200,128]{2,1,0:T(8,128)(2,1)}), bf16[8,200,128]{2,1,0:T(8,128)(2,1)S(1)}, u32[]{:S(2)}, u32[]{:S(2)}) %all-to-all-start) | async-done | bytes 409632 | tf_op jit(solution)/shard_map/all_to_all | solution.py:441
  37.3 0.0 copy-start.5
  37.3 0.0 collective-permute-start.5
  37.3 1.7 %collective-permute-done.5.refs_1_ = bf16[8,200,128]{2,1,0:T(8,128)(2,1)S(1)} collective-permute-done((bf16[8,200,128]{2,1,0:T(8,128)(2,1)S(1)}, bf16[8,200,128]{2,1,0:T(8,128)(2,1)S(1)}, u32[]{:S(2)}, u32[]{:S(2)}) %collective-permute-start.5) | collective-permute-done | bytes 409632 | tf_op jit(solution)/shard_map/ppermute | solution.py:446
  39.1 0.0 copy-done.5
  39.1 1.3 %respond.1 = f32[4,128]{1,0:T(4,128)S(1)} custom-call(bf16[512,768]{1,0:T(8,128)(2,1)S(1)} %get-tuple-element.22.strain_ref, s32[1,128]{1,0:T(1,128)S(1)} %bitcast.8, bf16[8,200,128]{2,1,0:T(8,128)(2,1)S(1)} %all-to-all-done.refs_0_, bf16[8,200,128]{2,1,0:T(8,128)(2,1)S(1)} %collective-permute-done.5.refs_1_), custom_call_target="tpu_custom_call" | custom-call | tf_op jit(solution)/shard_map/respond/pallas_call | solution.py:383
  40.3 1.5 %collective-permute-start.6 = (f32[4,128]{1,0:T(4,128)S(1)}, f32[4,128]{1,0:T(4,128)S(1)}, u32[]{:S(2)}, u32[]{:S(2)}) collective-permute-start(f32[4,128]{1,0:T(4,128)S(1)} %respond.1), channel_id=1, source_target_pairs={{0,2},{2,0},{4,6},{6,4},{8,10},{10,8},{12,14},{14,12},{1,3},{3,1},... | collective-permute-start | bytes 6152 | tf_op jit(solution)/shard_map/ppermute | solution.py:407
  41.8 2.1 %collective-permute-done.6 = f32[4,128]{1,0:T(4,128)S(1)} collective-permute-done((f32[4,128]{1,0:T(4,128)S(1)}, f32[4,128]{1,0:T(4,128)S(1)}, u32[]{:S(2)}, u32[]{:S(2)}) %collective-permute-start.6) | collective-permute-done | bytes 2080 | tf_op jit(solution)/shard_map/ppermute | solution.py:407
  44.0 0.9 %collective-permute-start.7 = (f32[4,128]{1,0:T(4,128)S(1)}, f32[4,128]{1,0:T(4,128)S(1)}, u32[]{:S(2)}, u32[]{:S(2)}) collective-permute-start(f32[4,128]{1,0:T(4,128)S(1)} %add.15), channel_id=1, source_target_pairs={{0,4},{2,6},{4,0},{6,2},{8,12},{10,14},{12,8},{14,10},{1,5},{3,7},... | collective-permute-start | bytes 6152 | tf_op jit(solution)/shard_map/ppermute | solution.py:407
  44.9 2.7 %collective-permute-done.7 = f32[4,128]{1,0:T(4,128)S(1)} collective-permute-done((f32[4,128]{1,0:T(4,128)S(1)}, f32[4,128]{1,0:T(4,128)S(1)}, u32[]{:S(2)}, u32[]{:S(2)}) %collective-permute-start.7) | collective-permute-done | bytes 2080 | tf_op jit(solution)/shard_map/ppermute | solution.py:407
  47.6 1.0 %collective-permute-start.8 = (f32[4,128]{1,0:T(4,128)S(1)}, f32[4,128]{1,0:T(4,128)S(1)}, u32[]{:S(2)}, u32[]{:S(2)}) collective-permute-start(f32[4,128]{1,0:T(4,128)S(1)} %add.16), channel_id=1, source_target_pairs={{0,8},{2,10},{4,12},{6,14},{8,0},{10,2},{12,4},{14,6},{1,9},{3,11}... | collective-permute-start | bytes 6152 | tf_op jit(solution)/shard_map/ppermute | solution.py:407
  48.5 3.5 %collective-permute-done.8 = f32[4,128]{1,0:T(4,128)S(1)} collective-permute-done((f32[4,128]{1,0:T(4,128)S(1)}, f32[4,128]{1,0:T(4,128)S(1)}, u32[]{:S(2)}, u32[]{:S(2)}) %collective-permute-start.8) | collective-permute-done | bytes 2080 | tf_op jit(solution)/shard_map/ppermute | solution.py:407
  52.0 0.7 %dynamic-slice_bitcast_fusion = f32[1,16,4]{1,2,0:T(4,128)} fusion(f32[4,128]{1,0:T(4,128)S(1)} %add.17, s32[]{:T(128)S(6)} %select_n.3), kind=kLoop, calls=%fused_computation | loop fusion | bytes 516 | tf_op jit(solution)/shard_map/broadcast_in_dim | solution.py:451
  (3 shorter events, 0.0 us)
Async XLA Ops:
  0.6 15.8 %copy-start.6 = (bf16[16,16,6,128]{3,1,2,0:T(8,128)(2,1)S(1)}, bf16[16,16,6,128]{3,1,2,0:T(8,128)(2,1)}, u32[]{:S(2)}) copy-start(bf16[16,16,6,128]{3,1,2,0:T(8,128)(2,1)} %param.17) | copy-start | bytes 1179652
  2.8 23.9 %collective-permute-start = (bf16[38,32,128]{2,1,0:T(8,128)(2,1)}, bf16[38,32,128]{2,1,0:T(8,128)(2,1)S(1)}, u32[]{:S(2)}, u32[]{:S(2)}) collective-permute-start(bf16[38,32,128]{2,1,0:T(8,128)(2,1)} %get-tuple-element.13), channel_id=1, source_target_pairs={{0,4},{2,6},{4,8},{6,10},{8,12},{10,14},{1,5},{3,7},{5,9},{7,11},{... | collective-permute-start | bytes 933896 | tf_op jit(solution)/shard_map/ppermute | solution.py:432
  7.8 18.9 %collective-permute-start.1 = (bf16[36,32,128]{2,1,0:T(8,128)(2,1)}, bf16[36,32,128]{2,1,0:T(8,128)(2,1)S(1)}, u32[]{:S(2)}, u32[]{:S(2)}) collective-permute-start(bf16[36,32,128]{2,1,0:T(8,128)(2,1)} %get-tuple-element.14), channel_id=1, source_target_pairs={{4,0},{6,2},{8,4},{10,6},{12,8},{14,10},{5,1},{7,3},{9,5},{11,7},{... | collective-permute-start | bytes 884744 | tf_op jit(solution)/shard_map/ppermute | solution.py:432
  9.1 7.4 %collective-permute-start.2 = (f32[9,4,4,128]{3,2,1,0:T(4,128)}, f32[9,4,4,128]{3,2,1,0:T(4,128)S(1)}, u32[]{:S(2)}, u32[]{:S(2)}) collective-permute-start(f32[9,4,4,128]{3,2,1,0:T(4,128)} %get-tuple-element.15), channel_id=1, source_target_pairs={{0,2},{4,6},{8,10},{12,14},{2,0},{6,4},{10,8},{14,12},{1,3},{5,7},... | collective-permute-start | bytes 221192 | tf_op jit(solution)/shard_map/ppermute | solution.py:432
  10.6 16.1 %collective-permute-start.3 = (bf16[38,4,128]{2,1,0:T(4,128)(2,1)}, bf16[38,4,128]{2,1,0:T(4,128)(2,1)S(1)}, u32[]{:S(2)}, u32[]{:S(2)}) collective-permute-start(bf16[38,4,128]{2,1,0:T(4,128)(2,1)} %get-tuple-element.17), channel_id=1, source_target_pairs={{0,6},{4,10},{8,14},{2,4},{6,8},{10,12},{1,7},{5,11},{9,15},{3,5},... | collective-permute-start | bytes 116744 | tf_op jit(solution)/shard_map/ppermute | solution.py:432
  15.1 11.5 %collective-permute-start.4 = (bf16[36,4,128]{2,1,0:T(4,128)(2,1)}, bf16[36,4,128]{2,1,0:T(4,128)(2,1)S(1)}, u32[]{:S(2)}, u32[]{:S(2)}) collective-permute-start(bf16[36,4,128]{2,1,0:T(4,128)(2,1)} %get-tuple-element.18), channel_id=1, source_target_pairs={{4,2},{8,6},{12,10},{6,0},{10,4},{14,8},{5,3},{9,7},{13,11},{7,1},... | collective-permute-start | bytes 110600 | tf_op jit(solution)/shard_map/ppermute | solution.py:432
  19.6 7.1 %copy-start = (f32[1,3,4,32,128]{4,3,2,1,0:T(8,128)S(1)}, f32[1,3,4,32,128]{4,3,2,1,0:T(8,128)}, u32[]{:S(2)}) copy-start(f32[1,3,4,32,128]{4,3,2,1,0:T(8,128)} %refs_0_.3) | copy-start | bytes 589828
  19.6 7.1 %copy-start.1 = (f32[1,3,4,32,128]{4,3,2,1,0:T(8,128)S(1)}, f32[1,3,4,32,128]{4,3,2,1,0:T(8,128)}, u32[]{:S(2)}) copy-start(f32[1,3,4,32,128]{4,3,2,1,0:T(8,128)} %refs_1_.3) | copy-start | bytes 589828
  19.6 7.1 %copy-start.2 = (f32[4,32,128]{2,1,0:T(8,128)S(1)}, f32[4,32,128]{2,1,0:T(8,128)}, u32[]{:S(2)}) copy-start(f32[4,32,128]{2,1,0:T(8,128)} %refs_2_.3) | copy-start | bytes 196612
  19.6 7.1 %copy-start.3 = (f32[4,32,128]{2,1,0:T(8,128)S(1)}, f32[4,32,128]{2,1,0:T(8,128)}, u32[]{:S(2)}) copy-start(f32[4,32,128]{2,1,0:T(8,128)} %refs_3_.3) | copy-start | bytes 196612
  19.6 7.1 %copy-start.4 = (f32[4,32,128]{2,1,0:T(8,128)S(1)}, f32[4,32,128]{2,1,0:T(8,128)}, u32[]{:S(2)}) copy-start(f32[4,32,128]{2,1,0:T(8,128)} %refs_4_.3) | copy-start | bytes 196612
  19.7 17.6 %all-to-all-start = ((bf16[8,200,128]{2,1,0:T(8,128)(2,1)}), bf16[8,200,128]{2,1,0:T(8,128)(2,1)S(1)}, u32[]{:S(2)}, u32[]{:S(2)}) async-start(bf16[8,200,128]{2,1,0:T(8,128)(2,1)} %pack.1), calls=%async_computation | async-start | bytes 819200 | tf_op jit(solution)/shard_map/all_to_all | solution.py:441
  37.3 1.8 %copy-start.5 = (s32[128]{0:T(128)S(1)}, s32[128]{0:T(128)}, u32[]{:S(2)}) copy-start(s32[128]{0:T(128)} %param.14) | copy-start | bytes 1540
  37.3 1.7 %collective-permute-start.5 = (bf16[8,200,128]{2,1,0:T(8,128)(2,1)S(1)}, bf16[8,200,128]{2,1,0:T(8,128)(2,1)S(1)}, u32[]{:S(2)}, u32[]{:S(2)}) collective-permute-start(bf16[8,200,128]{2,1,0:T(8,128)(2,1)S(1)} %all-to-all-done.refs_0_), channel_id=1, source_target_pairs={{0,1},{1,0},{2,3},{3,2},{4,5},{5,4},{6,7},{7,6},{8,9},{9,8},{10,11... | collective-permute-start | bytes 1228808 | tf_op jit(solution)/shard_map/ppermute | solution.py:446
  40.3 3.6 %collective-permute-start.6 = (f32[4,128]{1,0:T(4,128)S(1)}, f32[4,128]{1,0:T(4,128)S(1)}, u32[]{:S(2)}, u32[]{:S(2)}) collective-permute-start(f32[4,128]{1,0:T(4,128)S(1)} %respond.1), channel_id=1, source_target_pairs={{0,2},{2,0},{4,6},{6,4},{8,10},{10,8},{12,14},{14,12},{1,3},{3,1},... | collective-permute-start | bytes 6152 | tf_op jit(solution)/shard_map/ppermute | solution.py:407
  44.0 3.6 %collective-permute-start.7 = (f32[4,128]{1,0:T(4,128)S(1)}, f32[4,128]{1,0:T(4,128)S(1)}, u32[]{:S(2)}, u32[]{:S(2)}) collective-permute-start(f32[4,128]{1,0:T(4,128)S(1)} %add.15), channel_id=1, source_target_pairs={{0,4},{2,6},{4,0},{6,2},{8,12},{10,14},{12,8},{14,10},{1,5},{3,7},... | collective-permute-start | bytes 6152 | tf_op jit(solution)/shard_map/ppermute | solution.py:407
  47.6 4.5 %collective-permute-start.8 = (f32[4,128]{1,0:T(4,128)S(1)}, f32[4,128]{1,0:T(4,128)S(1)}, u32[]{:S(2)}, u32[]{:S(2)}) collective-permute-start(f32[4,128]{1,0:T(4,128)S(1)} %add.16), channel_id=1, source_target_pairs={{0,8},{2,10},{4,12},{6,14},{8,0},{10,2},{12,4},{14,6},{1,9},{3,11}... | collective-permute-start | bytes 6152 | tf_op jit(solution)/shard_map/ppermute | solution.py:407

commit v4 on v3

--- a/solution.py
+++ b/solution.py
@@ -107,20 +107,20 @@
     return body.reshape(1, components * owners * ranks, LANES), meta
 
 
-def planes_for(field, side, halo):
-    return halo if field < 3 or (side > 0 and field in (6, 7)) else halo - 1
-
-
-def coded_planes(side, halo):
-    return sum(planes_for(f, side, halo) + (f < 6) for f in range(FIELDS))
-
-
-def encode(side, halo, nx, read, write):
+def planes_for(field, halo):
+    return halo if field < 3 or field in (6, 7) else halo - 1
+
+
+def coded_planes(halo):
+    return sum(planes_for(f, halo) + (f < 6) for f in range(FIELDS))
+
+
+def encode(halo, read, write):
     at = 0
     for field in range(FIELDS):
         near = None
-        for k in range(planes_for(field, side, halo)):
-            value = read(field, nx - 1 - k if side > 0 else k)
+        for k in range(planes_for(field, halo)):
+            value = read(field, k)
             if field >= 6:
                 parts = [value.astype(jnp.bfloat16)]
             elif near is None:
@@ -137,11 +137,11 @@
                 at += 1
 
 
-def decode(side, halo, nx, read, write):
+def decode(halo, read, write):
     at = 0
     for field in range(FIELDS):
         near = None
-        for k in range(planes_for(field, side, halo)):
+        for k in range(planes_for(field, halo)):
             value = read(at).astype(jnp.float32)
             at += 1
             if field < 6:
@@ -151,12 +151,12 @@
                 else:
                     value = near + value
                 near = value
-            write(field, halo - 1 - k if side > 0 else halo + nx + k, value)
-
-
-def prepare_kernel(halo, merged, *refs):
-    disp, prev, lam, mu, buoy, up, down = refs[:7]
-    edges, fields, sem = refs[7:-2], refs[-2], refs[-1]
+            write(field, k, value)
+
+
+def prepare_kernel(halo, *refs):
+    disp, prev, lam, mu, buoy = refs[:5]
+    outs, fields, sem = refs[5:-2], refs[-2], refs[-1]
     nx, ny, nz = lam.shape
     copies = [
         pltpu.make_async_copy(disp.at[0], fields.at[pl.ds(0, 3)], sem.at[0]),
@@ -169,41 +169,37 @@
         copy.start()
     for copy in copies:
         copy.wait()
-
-    def coded(side, rows, target):
+    odd_x, odd_y = lax.axis_index("gx") % 2, lax.axis_index("gy") % 2
+
+    def coded(p, rows, target):
         def write(at, value):
             target[at] = value
 
-        encode(side, halo, nx, lambda f, x: fields[f, x, rows, :], write)
-
-    every, high, low = pl.ds(0, ny), pl.ds(ny - halo, halo), pl.ds(0, halo)
-    coded(1, every, up)
-    coded(-1, every, down)
+        encode(halo, lambda f, k: fields[f, jnp.where(odd_x == p, nx - 1 - k, k), rows, :], write)
+
+    for p in range(2):
+        coded(p, pl.ds(0, ny), outs[p])
 
     def edge(rows, targets):
         targets[0][...] = fields[:, :, rows, :]
-        coded(1, rows, targets[1])
-        coded(-1, rows, targets[2])
-
-    if merged:
-        gy = lax.axis_index("gy")
-        pl.when(gy == 0)(lambda: edge(high, edges))
-        pl.when(gy != 0)(lambda: edge(low, edges))
-    else:
-        edge(high, edges[:3])
-        edge(low, edges[3:])
-
-
-def prepare(halo, merged, disp, prev, lam, mu, buoy):
+        for p in range(2):
+            coded(p, rows, targets[1 + p])
+
+    for q, targets in enumerate((outs[2:5], outs[5:8])):
+        if targets:
+            pl.when(odd_y == q)(functools.partial(edge, pl.ds(ny - halo, halo), targets))
+            pl.when(odd_y != q)(functools.partial(edge, pl.ds(0, halo), targets))
+
+
+def prepare(halo, ways, disp, prev, lam, mu, buoy):
     nx, ny, nz = lam.shape
     vmem, anywhere = pl.BlockSpec(memory_space=pltpu.VMEM), pl.BlockSpec(memory_space=pl.ANY)
-    counts = [coded_planes(side, halo) for side in (1, -1)]
-    shapes = [jax.ShapeDtypeStruct((count, ny, nz), jnp.bfloat16) for count in counts]
+    count = coded_planes(halo)
     edge = [jax.ShapeDtypeStruct((FIELDS, nx, halo, nz), jnp.float32)]
-    edge += [jax.ShapeDtypeStruct((count, halo, nz), jnp.bfloat16) for count in counts]
-    shapes += edge if merged else edge * 2
+    edge += [jax.ShapeDtypeStruct((count, halo, nz), jnp.bfloat16)] * 2
+    shapes = [jax.ShapeDtypeStruct((count, ny, nz), jnp.bfloat16)] * 2 + edge * ways
     return pl.pallas_call(
-        functools.partial(prepare_kernel, halo, merged),
+        functools.partial(prepare_kernel, halo),
         out_shape=shapes,
         in_specs=[anywhere] * 5,
         out_specs=[vmem] * len(shapes),
@@ -216,35 +212,41 @@
     return pltpu.roll(value, value.shape[dim] - 1, dim)
 
 
-def stencil_kernel(halo, merged, *refs):
-    disp, prev, lam, mu, buoy, x_low, x_high = refs[:7]
-    sides = refs[7:13] if not merged else refs[7:10] * 2
-    out_ref, strain_ref = refs[-7:-5]
+def stencil_kernel(halo, *refs):
+    disp, prev, lam, mu, buoy = refs[:5]
+    halos, (out_ref, strain_ref) = refs[5:-7], refs[-7:-5]
     wave, first, second, scale = refs[-5:-1]
     nx, ny, nz = lam.shape
     tall = ny + 2 * PAD
-    gy = lax.axis_index("gy")
+    odd_x, odd_y = lax.axis_index("gx") % 2, lax.axis_index("gy") % 2
     own_x, own_y = pl.ds(halo, nx), pl.ds(PAD, ny)
     targets = [wave.at[0, i] for i in range(3)] + [wave.at[1, i] for i in range(3)] + [first, second, scale]
 
     def put(field, xs, ys, value):
         targets[field][xs, ys, :] = value * (TIME_STEP * TIME_STEP) if field == 8 else value
+
+    def spread(p, ys, read):
+        def write(field, k, value):
+            put(field, jnp.where(odd_x == p, halo + nx + k, halo - 1 - k), ys, value)
+
+        decode(halo, read, write)
 
     owns = [disp[0, i] for i in range(3)] + [prev[0, i] for i in range(3)] + [lam[...], mu[...], buoy[...]]
     for f, own in enumerate(owns):
         put(f, own_x, own_y, own)
-    decode(1, halo, nx, lambda at: x_low[at], lambda f, x, v: put(f, x, own_y, v))
-    decode(-1, halo, nx, lambda at: x_high[at], lambda f, x, v: put(f, x, own_y, v))
-    for s, ys in ((0, pl.ds(PAD - halo, halo)), (1, pl.ds(PAD + ny, halo))):
-        middle, low, high = sides[3 * s : 3 * s + 3]
-
-        def only(value, s=s):
-            return jnp.where(gy == (1 - s), value, 0.0) if merged else value
+    for p in range(2):
+        spread(p, own_y, lambda at, p=p: halos[p][at])
+    for upper, ys in ((True, pl.ds(PAD + ny, halo)), (False, pl.ds(PAD - halo, halo))):
+
+        def side(i, at, upper=upper):
+            taken = (odd_y == 0) if upper else (odd_y != 0)
+            value = halos[2 + i][at].astype(jnp.float32)
+            return jnp.where(taken, value, halos[5 + i][at].astype(jnp.float32) if len(halos) > 5 else 0.0)
 
         for f in range(FIELDS):
-            put(f, own_x, ys, only(middle[f]))
-        decode(1, halo, nx, lambda at: low[at], lambda f, x, v: put(f, x, ys, only(v)))
-        decode(-1, halo, nx, lambda at: high[at], lambda f, x, v: put(f, x, ys, only(v)))
+            put(f, own_x, ys, side(0, f))
+        for p in range(2):
+            spread(p, ys, lambda at, p=p, side=side: side(1 + p, at))
 
     lane = iota((tall, nz), 1)
     not_last, not_first = lane < nz - 1, lane > 0
@@ -300,13 +302,13 @@
                 carry = lax.fori_loop(lo, hi, functools.partial(plane, step, cur, own), carry)
 
 
-def stencil(halo, merged, disp, prev, lam, mu, buoy, x_low, x_high, sides):
+def stencil(halo, disp, prev, lam, mu, buoy, halos):
     nx, ny, nz = lam.shape
     tall, wide = ny + 2 * PAD, nx + 2 * halo
     vmem = pl.BlockSpec(memory_space=pltpu.VMEM)
-    operands = (disp, prev, lam, mu, buoy, x_low, x_high, *sides)
+    operands = (disp, prev, lam, mu, buoy, *halos)
     return pl.pallas_call(
-        functools.partial(stencil_kernel, halo, merged),
+        functools.partial(stencil_kernel, halo),
         out_shape=(
             jax.ShapeDtypeStruct((1, 3, nx, ny, nz), jnp.float32),
             jax.ShapeDtypeStruct((STEPS * nx * ny, 6 * nz), jnp.bfloat16),
@@ -390,13 +392,21 @@
     )(*operands)
 
 
-def shift_pairs(nx, ny, dx, dy):
-    return [
-        (i * ny + j, (i + dx) * ny + j + dy)
-        for i in range(nx)
-        for j in range(ny)
-        if 0 <= i + dx < nx and 0 <= j + dy < ny
-    ]
+def partner(index, length, turn):
+    if turn is None:
+        return index
+    other = index + 1 if index % 2 == turn else index - 1
+    return other if 0 <= other < length else None
+
+
+def exchange(value, gxs, gys, turn_x, turn_y):
+    pairs = []
+    for i in range(gxs):
+        for j in range(gys):
+            x, y = partner(i, gxs, turn_x), partner(j, gys, turn_y)
+            if x is not None and y is not None:
+                pairs.append((i * gys + j, x * gys + y))
+    return lax.ppermute(value, OWNERS_AXES, pairs)
 
 
 def owner_sum(value, owners):
@@ -420,30 +430,20 @@
     ranks = entries // owners
     components = slip_panels.shape[2]
 
-    merged = gys == 2
-    upward, downward, *edges = prepare(
-        halo, merged, displacement, previous, first_lame, shear_modulus, buoyancy
-    )
-
-    def send(value, dx, dy):
-        pairs = shift_pairs(gxs, gys, dx, dy)
-        if merged and dy:
-            pairs = pairs + shift_pairs(gxs, gys, dx, -dy)
-        return lax.ppermute(value, OWNERS_AXES, pairs)
-
-    ways = [(0, 1), (1, 1), (-1, 1)] + ([] if merged else [(0, -1), (1, -1), (-1, -1)])
-    sides = [send(edge, dx, dy) for edge, (dx, dy) in zip(edges, ways)]
-    x_low, x_high = send(upward, 1, 0), send(downward, -1, 0)
-
-    sides[0], slip_panels = lax.optimization_barrier((sides[0], slip_panels))
     panels = slip_panels.reshape(entries, components, nz).transpose(1, 0, 2)
     payload = pack(owners, slots, ranks, rupture_tiles, slip_offsets, panels)
     arrived = lax.all_to_all(payload, OWNERS_AXES, split_axis=0, concat_axis=0, tiled=True)
-    final, strain = stencil(
-        halo, merged, displacement, previous, first_lame, shear_modulus, buoyancy, x_low, x_high, sides
-    )
-    arrived, strain = lax.optimization_barrier((arrived, strain))
+
+    waves = (displacement, previous, first_lame, shear_modulus, buoyancy)
+    turns_y = range(1 if gys == 2 else 2)
+    gated, _ = lax.optimization_barrier((waves, payload))
+    sent = prepare(halo, len(turns_y), *gated)
+    ways = [(0, None), (1, None)] + [(x, q) for q in turns_y for x in (None, 0, 1)]
+    halos = [exchange(value, gxs, gys, *way) for value, way in zip(sent, ways)]
+
+    arrived, halos = lax.optimization_barrier((arrived, halos))
     other = lax.ppermute(arrived, "comp", [(0, 1), (1, 0)])
+    final, strain = stencil(halo, *waves, halos)
     halves = [unpack(owners, ranks, components, v) for v in (arrived, other)]
     partial = respond(owners, ranks, records, strain, tile_column.reshape(1, slots), halves)
     summed = owner_sum(partial, owners)

time: 53 us -> 51.6 us (0.974)
  waiting for transfers between devices: 14.8 us -> 12.8 us
  local copies, waits for them, and re-layouts: 1.45 us -> 3.1 us
  starting transfers between devices: 24 us -> 22.9 us
    ppermute x5, waiting for transfers between devices: 0.01 us -> 6.05 us  [exchange(): return lax.ppermute(value, OWNERS_AXES, pairs)]
    all_to_all x1, waiting for transfers between devices: 4.77 us -> 0.01 us  [body(): lax.all_to_all(payload, OWNERS_AXES, split_axis=0, concat_axis=0, tiled=T...]
    ppermute x5, starting transfers between devices: 13.6 us -> 9.05 us  [exchange(): return lax.ppermute(value, OWNERS_AXES, pairs)]
    ppermute x3, starting transfers between devices: 3.37 us -> 6.49 us  [owner_sum(): lax.ppermute(value, OWNERS_AXES, [(i, i ^ bit) for i in range(owners)])]
    unnamed x14 -> x13, local copies, waits for them, and re-layouts: 0.03 us -> 2.44 us
    ppermute x1, waiting for transfers between devices: 1.74 us -> 0.01 us  [body(): other = lax.ppermute(arrived, 'comp', [(0, 1), (1, 0)])]
    ppermute x3, waiting for transfers between devices: 8.31 us -> 6.77 us  [owner_sum(): lax.ppermute(value, OWNERS_AXES, [(i, i ^ bit) for i in range(owners)])]
    optimization_barrier x1 -> x0, local copies, waits for them, and re-layouts: 0.77 us -> none  [body(): sides[0], slip_panels = lax.optimization_barrier((sides[0], slip_panels))]
  transfers between devices with their start and end apart: 10 -> 10, of which waited for: 5 -> 4; matrix products, arithmetic and copies ran while one was open for 1% -> 0% of each run, Pallas kernels for 16% -> 16%
where the time goes in v4:
time: 51.6 us; the launch traced here: 51.3 us
  starting transfers between devices  22.9 us (44%)
  waiting for transfers between devices  12.8 us (25%)
  Pallas kernels  11.7 us (23%)
  local copies, waits for them, and re-layouts  3.1 us (6%)
  between operations  0.77 us (1%)
    ppermute x5, starting transfers between devices, exchange(): return lax.ppermute(value, OWNERS_AXES, pairs)  9.05 us
    all_to_all x1, starting transfers between devices, body(): lax.all_to_all(payload, OWNERS_AXES, split_axis=0, concat_axis=0, tiled=T...  7.25 us
    ppermute x3, waiting for transfers between devices, owner_sum(): lax.ppermute(value, OWNERS_AXES, [(i, i ^ bit) for i in range(owners)])  6.77 us
    ppermute x3, starting transfers between devices, owner_sum(): lax.ppermute(value, OWNERS_AXES, [(i, i ^ bit) for i in range(owners)])  6.49 us
    ppermute x5, waiting for transfers between devices, exchange(): return lax.ppermute(value, OWNERS_AXES, pairs)  6.05 us
    pallas_call x1, Pallas kernels, stencil(): pl.pallas_call(functools.partial(stencil_kernel, halo), out_shape=(jax.Sh...  5.84 us
    unnamed x13, local copies, waits for them, and re-layouts  2.44 us
    pallas_call x1, Pallas kernels, pack(): pl.pallas_call(kernel, out_shape=jax.ShapeDtypeStruct((owners, components...  2.4 us
  transfers between devices with their start and end apart: 10, of which 4 were waited for; matrix products, arithmetic and copies ran while one was open for 0% of the time, Pallas kernels for 16%

profile of v4, /device:TPU:0, one launch (start us, length us, event | category | flops | bytes accessed | tf_op | source)
XLA Modules:
  0.0 51.3 jit_solution(8749740696195570836)
XLA Ops:
  0.6 1.8 %copy.11 = bf16[16,16,6,128]{3,1,0,2:T(8,128)(2,1)} copy(bf16[16,16,6,128]{3,1,2,0:T(8,128)(2,1)} %param.17) | data formatting | bytes 786432 | tf_op args[8]
  2.4 2.4 %pack.1 = bf16[8,200,128]{2,1,0:T(8,128)(2,1)} custom-call(s32[16,16]{1,0:T(8,128)} %tiles_ref.1, s32[16,16]{1,0:T(8,128)} %offsets_ref.1, bf16[6,256,128]{2,1,0:T(8,128)(2,1)} %bitcast.9), custom_call_target="tpu_custom_call" | custom-call | tf_op jit(solution)/shard_map/pack/pallas_call | solution.py:79
  4.8 7.3 %all-to-all-start = ((bf16[8,200,128]{2,1,0:T(8,128)(2,1)}), bf16[8,200,128]{2,1,0:T(8,128)(2,1)S(1)}, u32[]{:S(2)}, u32[]{:S(2)}) async-start(bf16[8,200,128]{2,1,0:T(8,128)(2,1)} %pack.1), calls=%async_computation | async-start | bytes 819200 | tf_op jit(solution)/shard_map/all_to_all | solution.py:435
  12.0 0.0 copy-start
  12.0 0.0 copy-start.1
  12.1 0.0 copy-start.2
  12.1 0.0 copy-start.3
  12.1 0.0 copy-start.4
  12.1 2.2 %prepare.1 = (bf16[38,32,128]{2,1,0:T(8,128)(2,1)}, bf16[38,32,128]{2,1,0:T(8,128)(2,1)}, f32[9,4,4,128]{3,2,1,0:T(4,128)}, bf16[38,4,128]{2,1,0:T(4,128)(2,1)}, bf16[38,4,128]{2,1,0:T(4,128)(2,1)}) custom-call(f32[1,3,4,32,128]{4,3,2,1,0:T(8,128)} %refs_0_.2, f32[1,3,4,32,128]{4,3,2,1,0:T(8,128)} %refs_1_.2, f32[4,32,128]{2,1,0:T(8,128)} %refs_2_.2, ...), custom_call_target="tpu_custom_call" | custom-call | tf_op jit(solution)/shard_map/prepare/pallas_call | solution.py:201
  14.3 2.0 %collective-permute-start = (bf16[38,32,128]{2,1,0:T(8,128)(2,1)}, bf16[38,32,128]{2,1,0:T(8,128)(2,1)S(1)}, u32[]{:S(2)}, u32[]{:S(2)}) collective-permute-start(bf16[38,32,128]{2,1,0:T(8,128)(2,1)} %get-tuple-element.25), channel_id=1, source_target_pairs={{0,4},{2,6},{4,0},{6,2},{8,12},{10,14},{12,8},{14,10},{1,5},{3,7},... | collective-permute-start | bytes 933896 | tf_op jit(solution)/shard_map/ppermute | solution.py:409
  16.4 0.7 %collective-permute-start.1 = (bf16[38,32,128]{2,1,0:T(8,128)(2,1)}, bf16[38,32,128]{2,1,0:T(8,128)(2,1)S(1)}, u32[]{:S(2)}, u32[]{:S(2)}) collective-permute-start(bf16[38,32,128]{2,1,0:T(8,128)(2,1)} %get-tuple-element.26), channel_id=1, source_target_pairs={{4,8},{6,10},{8,4},{10,6},{5,9},{7,11},{9,5},{11,7},{20,24},{22,26... | collective-permute-start | bytes 933896 | tf_op jit(solution)/shard_map/ppermute | solution.py:409
  17.0 1.5 %collective-permute-start.2 = (f32[9,4,4,128]{3,2,1,0:T(4,128)}, f32[9,4,4,128]{3,2,1,0:T(4,128)S(1)}, u32[]{:S(2)}, u32[]{:S(2)}) collective-permute-start(f32[9,4,4,128]{3,2,1,0:T(4,128)} %get-tuple-element.27), channel_id=1, source_target_pairs={{0,2},{2,0},{4,6},{6,4},{8,10},{10,8},{12,14},{14,12},{1,3},{3,1},... | collective-permute-start | bytes 221192 | tf_op jit(solution)/shard_map/ppermute | solution.py:409
  18.6 4.2 %collective-permute-start.3 = (bf16[38,4,128]{2,1,0:T(4,128)(2,1)}, bf16[38,4,128]{2,1,0:T(4,128)(2,1)S(1)}, u32[]{:S(2)}, u32[]{:S(2)}) collective-permute-start(bf16[38,4,128]{2,1,0:T(4,128)(2,1)} %get-tuple-element.28), channel_id=1, source_target_pairs={{0,6},{2,4},{4,2},{6,0},{8,14},{10,12},{12,10},{14,8},{1,7},{3,5},... | collective-permute-start | bytes 116744 | tf_op jit(solution)/shard_map/ppermute | solution.py:409
  22.7 0.7 %collective-permute-start.4 = (bf16[38,4,128]{2,1,0:T(4,128)(2,1)}, bf16[38,4,128]{2,1,0:T(4,128)(2,1)S(1)}, u32[]{:S(2)}, u32[]{:S(2)}) collective-permute-start(bf16[38,4,128]{2,1,0:T(4,128)(2,1)} %get-tuple-element.29), channel_id=1, source_target_pairs={{4,10},{6,8},{8,6},{10,4},{5,11},{7,9},{9,7},{11,5},{20,26},{22,24... | collective-permute-start | bytes 116744 | tf_op jit(solution)/shard_map/ppermute | solution.py:409
  23.4 6.0 %collective-permute-done.3.refs_8_ = bf16[38,4,128]{2,1,0:T(4,128)(2,1)S(1)} collective-permute-done((bf16[38,4,128]{2,1,0:T(4,128)(2,1)}, bf16[38,4,128]{2,1,0:T(4,128)(2,1)S(1)}, u32[]{:S(2)}, u32[]{:S(2)}) %collective-permute-start.3) | collective-permute-done | bytes 38944 | tf_op jit(solution)/shard_map/ppermute | solution.py:409
  29.4 0.0 collective-permute-done.4.refs_9_
  29.4 0.0 collective-permute-done.2.refs_7_
  29.4 0.0 collective-permute-done.refs_5_
  29.4 0.0 collective-permute-done.1.refs_6_
  29.4 0.0 all-to-all-done.refs_0_
  29.5 0.1 collective-permute-start.5
  29.5 0.0 copy-done
  29.5 0.0 copy-done.1
  29.6 0.0 copy-done.2
  29.6 0.0 copy-done.3
  29.6 0.0 copy-done.4
  29.6 5.8 %stencil.1 = (f32[1,3,4,32,128]{4,3,2,1,0:T(8,128)}, bf16[512,768]{1,0:T(8,128)(2,1)S(1)}) custom-call(f32[1,3,4,32,128]{4,3,2,1,0:T(8,128)S(1)} %copy-done, f32[1,3,4,32,128]{4,3,2,1,0:T(8,128)S(1)} %copy-done.1, f32[4,32,128]{2,1,0:T(8,128)S(1)} %copy-done.2, f32[4,32,128]{2,1,0:T(8,128)S(1)} %copy-done.3, f32[4,32,128]{2,1,0:T(8,128)S(1)} %copy-done.4, ...), custom_call_target="tpu_custom_call" | custom-call | flops 10000000000 | bytes 100000000 | tf_op jit(solution)/shard_map/stencil/pallas_call | solution.py:310
  35.4 0.0 collective-permute-done.5.refs_1_
  35.4 0.0 copy-start.5
  35.4 0.7 %copy-done.5 = s32[128]{0:T(128)S(1)} copy-done((s32[128]{0:T(128)S(1)}, s32[128]{0:T(128)}, u32[]{:S(2)}) %copy-start.5) | copy-done | bytes 536
  36.1 1.3 %respond.1 = f32[4,128]{1,0:T(4,128)S(1)} custom-call(bf16[512,768]{1,0:T(8,128)(2,1)S(1)} %get-tuple-element.36.strain_ref, s32[1,128]{1,0:T(1,128)S(1)} %bitcast.8, bf16[8,200,128]{2,1,0:T(8,128)(2,1)S(1)} %all-to-all-done.refs_0_, bf16[8,200,128]{2,1,0:T(8,128)(2,1)S(1)} %collective-permute-done.5.refs_1_), custom_call_target="tpu_custom_call" | custom-call | tf_op jit(solution)/shard_map/respond/pallas_call | solution.py:385
  37.4 0.9 %collective-permute-start.6 = (f32[4,128]{1,0:T(4,128)S(1)}, f32[4,128]{1,0:T(4,128)S(1)}, u32[]{:S(2)}, u32[]{:S(2)}) collective-permute-start(f32[4,128]{1,0:T(4,128)S(1)} %respond.1), channel_id=1, source_target_pairs={{0,2},{2,0},{4,6},{6,4},{8,10},{10,8},{12,14},{14,12},{1,3},{3,1},... | collective-permute-start | bytes 6152 | tf_op jit(solution)/shard_map/ppermute | solution.py:417
  38.2 2.8 %collective-permute-done.6 = f32[4,128]{1,0:T(4,128)S(1)} collective-permute-done((f32[4,128]{1,0:T(4,128)S(1)}, f32[4,128]{1,0:T(4,128)S(1)}, u32[]{:S(2)}, u32[]{:S(2)}) %collective-permute-start.6) | collective-permute-done | bytes 2080 | tf_op jit(solution)/shard_map/ppermute | solution.py:417
  41.0 3.6 %collective-permute-start.7 = (f32[4,128]{1,0:T(4,128)S(1)}, f32[4,128]{1,0:T(4,128)S(1)}, u32[]{:S(2)}, u32[]{:S(2)}) collective-permute-start(f32[4,128]{1,0:T(4,128)S(1)} %add.15), channel_id=1, source_target_pairs={{0,4},{2,6},{4,0},{6,2},{8,12},{10,14},{12,8},{14,10},{1,5},{3,7},... | collective-permute-start | bytes 6152 | tf_op jit(solution)/shard_map/ppermute | solution.py:417
  44.6 1.6 %collective-permute-done.7 = f32[4,128]{1,0:T(4,128)S(1)} collective-permute-done((f32[4,128]{1,0:T(4,128)S(1)}, f32[4,128]{1,0:T(4,128)S(1)}, u32[]{:S(2)}, u32[]{:S(2)}) %collective-permute-start.7) | collective-permute-done | bytes 2080 | tf_op jit(solution)/shard_map/ppermute | solution.py:417
  46.2 2.0 %collective-permute-start.8 = (f32[4,128]{1,0:T(4,128)S(1)}, f32[4,128]{1,0:T(4,128)S(1)}, u32[]{:S(2)}, u32[]{:S(2)}) collective-permute-start(f32[4,128]{1,0:T(4,128)S(1)} %add.16), channel_id=1, source_target_pairs={{0,8},{2,10},{4,12},{6,14},{8,0},{10,2},{12,4},{14,6},{1,9},{3,11}... | collective-permute-start | bytes 6152 | tf_op jit(solution)/shard_map/ppermute | solution.py:417
  48.2 2.5 %collective-permute-done.8 = f32[4,128]{1,0:T(4,128)S(1)} collective-permute-done((f32[4,128]{1,0:T(4,128)S(1)}, f32[4,128]{1,0:T(4,128)S(1)}, u32[]{:S(2)}, u32[]{:S(2)}) %collective-permute-start.8) | collective-permute-done | bytes 2080 | tf_op jit(solution)/shard_map/ppermute | solution.py:417
  50.6 0.7 %dynamic-slice_bitcast_fusion = f32[1,16,4]{1,2,0:T(4,128)} fusion(f32[4,128]{1,0:T(4,128)S(1)} %add.17, s32[]{:T(128)S(6)} %select_n.3), kind=kLoop, calls=%fused_computation | loop fusion | bytes 516 | tf_op jit(solution)/shard_map/broadcast_in_dim | solution.py:451
  (3 shorter events, 0.0 us)
Async XLA Ops:
  4.8 24.7 %all-to-all-start = ((bf16[8,200,128]{2,1,0:T(8,128)(2,1)}), bf16[8,200,128]{2,1,0:T(8,128)(2,1)S(1)}, u32[]{:S(2)}, u32[]{:S(2)}) async-start(bf16[8,200,128]{2,1,0:T(8,128)(2,1)} %pack.1), calls=%async_computation | async-start | bytes 819200 | tf_op jit(solution)/shard_map/all_to_all | solution.py:435
  12.0 17.5 %copy-start = (f32[1,3,4,32,128]{4,3,2,1,0:T(8,128)S(1)}, f32[1,3,4,32,128]{4,3,2,1,0:T(8,128)}, u32[]{:S(2)}) copy-start(f32[1,3,4,32,128]{4,3,2,1,0:T(8,128)} %refs_0_.2) | copy-start | bytes 589828
  12.0 17.5 %copy-start.1 = (f32[1,3,4,32,128]{4,3,2,1,0:T(8,128)S(1)}, f32[1,3,4,32,128]{4,3,2,1,0:T(8,128)}, u32[]{:S(2)}) copy-start(f32[1,3,4,32,128]{4,3,2,1,0:T(8,128)} %refs_1_.2) | copy-start | bytes 589828
  12.1 17.5 %copy-start.2 = (f32[4,32,128]{2,1,0:T(8,128)S(1)}, f32[4,32,128]{2,1,0:T(8,128)}, u32[]{:S(2)}) copy-start(f32[4,32,128]{2,1,0:T(8,128)} %refs_2_.2) | copy-start | bytes 196612
  12.1 17.5 %copy-start.3 = (f32[4,32,128]{2,1,0:T(8,128)S(1)}, f32[4,32,128]{2,1,0:T(8,128)}, u32[]{:S(2)}) copy-start(f32[4,32,128]{2,1,0:T(8,128)} %refs_3_.2) | copy-start | bytes 196612
  12.1 17.5 %copy-start.4 = (f32[4,32,128]{2,1,0:T(8,128)S(1)}, f32[4,32,128]{2,1,0:T(8,128)}, u32[]{:S(2)}) copy-start(f32[4,32,128]{2,1,0:T(8,128)} %refs_4_.2) | copy-start | bytes 196612
  14.3 15.1 %collective-permute-start = (bf16[38,32,128]{2,1,0:T(8,128)(2,1)}, bf16[38,32,128]{2,1,0:T(8,128)(2,1)S(1)}, u32[]{:S(2)}, u32[]{:S(2)}) collective-permute-start(bf16[38,32,128]{2,1,0:T(8,128)(2,1)} %get-tuple-element.25), channel_id=1, source_target_pairs={{0,4},{2,6},{4,0},{6,2},{8,12},{10,14},{12,8},{14,10},{1,5},{3,7},... | collective-permute-start | bytes 933896 | tf_op jit(solution)/shard_map/ppermute | solution.py:409
  16.4 13.1 %collective-permute-start.1 = (bf16[38,32,128]{2,1,0:T(8,128)(2,1)}, bf16[38,32,128]{2,1,0:T(8,128)(2,1)S(1)}, u32[]{:S(2)}, u32[]{:S(2)}) collective-permute-start(bf16[38,32,128]{2,1,0:T(8,128)(2,1)} %get-tuple-element.26), channel_id=1, source_target_pairs={{4,8},{6,10},{8,4},{10,6},{5,9},{7,11},{9,5},{11,7},{20,24},{22,26... | collective-permute-start | bytes 933896 | tf_op jit(solution)/shard_map/ppermute | solution.py:409
  17.0 12.4 %collective-permute-start.2 = (f32[9,4,4,128]{3,2,1,0:T(4,128)}, f32[9,4,4,128]{3,2,1,0:T(4,128)S(1)}, u32[]{:S(2)}, u32[]{:S(2)}) collective-permute-start(f32[9,4,4,128]{3,2,1,0:T(4,128)} %get-tuple-element.27), channel_id=1, source_target_pairs={{0,2},{2,0},{4,6},{6,4},{8,10},{10,8},{12,14},{14,12},{1,3},{3,1},... | collective-permute-start | bytes 221192 | tf_op jit(solution)/shard_map/ppermute | solution.py:409
  18.6 10.8 %collective-permute-start.3 = (bf16[38,4,128]{2,1,0:T(4,128)(2,1)}, bf16[38,4,128]{2,1,0:T(4,128)(2,1)S(1)}, u32[]{:S(2)}, u32[]{:S(2)}) collective-permute-start(bf16[38,4,128]{2,1,0:T(4,128)(2,1)} %get-tuple-element.28), channel_id=1, source_target_pairs={{0,6},{2,4},{4,2},{6,0},{8,14},{10,12},{12,10},{14,8},{1,7},{3,5},... | collective-permute-start | bytes 116744 | tf_op jit(solution)/shard_map/ppermute | solution.py:409
  22.7 6.7 %collective-permute-start.4 = (bf16[38,4,128]{2,1,0:T(4,128)(2,1)}, bf16[38,4,128]{2,1,0:T(4,128)(2,1)S(1)}, u32[]{:S(2)}, u32[]{:S(2)}) collective-permute-start(bf16[38,4,128]{2,1,0:T(4,128)(2,1)} %get-tuple-element.29), channel_id=1, source_target_pairs={{4,10},{6,8},{8,6},{10,4},{5,11},{7,9},{9,7},{11,5},{20,26},{22,24... | collective-permute-start | bytes 116744 | tf_op jit(solution)/shard_map/ppermute | solution.py:409
  29.5 6.0 %collective-permute-start.5 = (bf16[8,200,128]{2,1,0:T(8,128)(2,1)S(1)}, bf16[8,200,128]{2,1,0:T(8,128)(2,1)S(1)}, u32[]{:S(2)}, u32[]{:S(2)}) collective-permute-start(bf16[8,200,128]{2,1,0:T(8,128)(2,1)S(1)} %all-to-all-done.refs_0_), channel_id=1, source_target_pairs={{0,1},{1,0},{2,3},{3,2},{4,5},{5,4},{6,7},{7,6},{8,9},{9,8},{10,11... | collective-permute-start | bytes 1228808 | tf_op jit(solution)/shard_map/ppermute | solution.py:445
  35.4 0.7 %copy-start.5 = (s32[128]{0:T(128)S(1)}, s32[128]{0:T(128)}, u32[]{:S(2)}) copy-start(s32[128]{0:T(128)} %param.14) | copy-start | bytes 1540
  37.4 3.6 %collective-permute-start.6 = (f32[4,128]{1,0:T(4,128)S(1)}, f32[4,128]{1,0:T(4,128)S(1)}, u32[]{:S(2)}, u32[]{:S(2)}) collective-permute-start(f32[4,128]{1,0:T(4,128)S(1)} %respond.1), channel_id=1, source_target_pairs={{0,2},{2,0},{4,6},{6,4},{8,10},{10,8},{12,14},{14,12},{1,3},{3,1},... | collective-permute-start | bytes 6152 | tf_op jit(solution)/shard_map/ppermute | solution.py:417
  41.0 5.2 %collective-permute-start.7 = (f32[4,128]{1,0:T(4,128)S(1)}, f32[4,128]{1,0:T(4,128)S(1)}, u32[]{:S(2)}, u32[]{:S(2)}) collective-permute-start(f32[4,128]{1,0:T(4,128)S(1)} %add.15), channel_id=1, source_target_pairs={{0,4},{2,6},{4,0},{6,2},{8,12},{10,14},{12,8},{14,10},{1,5},{3,7},... | collective-permute-start | bytes 6152 | tf_op jit(solution)/shard_map/ppermute | solution.py:417
  46.2 4.5 %collective-permute-start.8 = (f32[4,128]{1,0:T(4,128)S(1)}, f32[4,128]{1,0:T(4,128)S(1)}, u32[]{:S(2)}, u32[]{:S(2)}) collective-permute-start(f32[4,128]{1,0:T(4,128)S(1)} %add.16), channel_id=1, source_target_pairs={{0,8},{2,10},{4,12},{6,14},{8,0},{10,2},{12,4},{14,6},{1,9},{3,11}... | collective-permute-start | bytes 6152 | tf_op jit(solution)/shard_map/ppermute | solution.py:417

commit v5 on v4

--- a/solution.py
+++ b/solution.py
@@ -409,13 +409,19 @@
     return lax.ppermute(value, OWNERS_AXES, pairs)
 
 
-def owner_sum(value, owners):
-    if owners & (owners - 1):
-        return lax.psum(value, OWNERS_AXES)
-    bit = 1
-    while bit < owners:
-        value = value + lax.ppermute(value, OWNERS_AXES, [(i, i ^ bit) for i in range(owners)])
-        bit *= 2
+def owner_sum(value):
+    for axis in ("gy", "gx"):
+        size = lax.axis_size(axis)
+        if size & (size - 1):
+            value = lax.psum(value, axis)
+        elif size <= 4:
+            parts = [lax.ppermute(value, axis, [(i, i ^ k) for i in range(size)]) for k in range(1, size)]
+            value = functools.reduce(jnp.add, parts, value)
+        else:
+            bit = 1
+            while bit < size:
+                value = value + lax.ppermute(value, axis, [(i, i ^ bit) for i in range(size)])
+                bit *= 2
     return value
 
 
@@ -430,23 +436,23 @@
     ranks = entries // owners
     components = slip_panels.shape[2]
 
+    waves = (displacement, previous, first_lame, shear_modulus, buoyancy)
+    turns_y = range(1 if gys == 2 else 2)
+    sent = prepare(halo, len(turns_y), *waves)
+    ways = [(0, None), (1, None)] + [(x, q) for q in turns_y for x in (None, 0, 1)]
+    halos = [exchange(value, gxs, gys, *way) for value, way in zip(sent, ways)]
+
+    halos[2], slip_panels = lax.optimization_barrier((halos[2], slip_panels))
     panels = slip_panels.reshape(entries, components, nz).transpose(1, 0, 2)
     payload = pack(owners, slots, ranks, rupture_tiles, slip_offsets, panels)
     arrived = lax.all_to_all(payload, OWNERS_AXES, split_axis=0, concat_axis=0, tiled=True)
 
-    waves = (displacement, previous, first_lame, shear_modulus, buoyancy)
-    turns_y = range(1 if gys == 2 else 2)
-    gated, _ = lax.optimization_barrier((waves, payload))
-    sent = prepare(halo, len(turns_y), *gated)
-    ways = [(0, None), (1, None)] + [(x, q) for q in turns_y for x in (None, 0, 1)]
-    halos = [exchange(value, gxs, gys, *way) for value, way in zip(sent, ways)]
-
-    arrived, halos = lax.optimization_barrier((arrived, halos))
+    final, strain = stencil(halo, *waves, halos)
+    arrived, strain = lax.optimization_barrier((arrived, strain))
     other = lax.ppermute(arrived, "comp", [(0, 1), (1, 0)])
-    final, strain = stencil(halo, *waves, halos)
     halves = [unpack(owners, ranks, components, v) for v in (arrived, other)]
     partial = respond(owners, ranks, records, strain, tile_column.reshape(1, slots), halves)
-    summed = owner_sum(partial, owners)
+    summed = owner_sum(partial)
     mine = lax.dynamic_slice_in_dim(summed, owner_index() * records, records, axis=1)
     return final, mine.T[None]
 

time: 51.6 us -> 47.1 us (0.913)
  local copies, waits for them, and re-layouts: 3.1 us -> 1.45 us
  starting transfers between devices: 22.9 us -> 21.3 us
  waiting for transfers between devices: 12.8 us -> 11.6 us
    ppermute x5, waiting for transfers between devices: 6.05 us -> 0.01 us  [exchange(): return lax.ppermute(value, OWNERS_AXES, pairs)]
    all_to_all x1, waiting for transfers between devices: 0.01 us -> 4.99 us  [body(): lax.all_to_all(payload, OWNERS_AXES, split_axis=0, concat_axis=0, tiled=T...]
    unnamed x13 -> x14, local copies, waits for them, and re-layouts: 2.44 us -> 0.03 us
    all_to_all x1, starting transfers between devices: 7.25 us -> 5.06 us  [body(): lax.all_to_all(payload, OWNERS_AXES, split_axis=0, concat_axis=0, tiled=T...]
    ppermute x3 -> x4, waiting for transfers between devices: 6.77 us -> 4.86 us  [owner_sum(): lax.ppermute(value, axis, [(i, i ^ k) for i in range(size)])]
    ppermute x1, waiting for transfers between devices: 0.01 us -> 1.74 us  [body(): other = lax.ppermute(arrived, 'comp', [(0, 1), (1, 0)])]
    ppermute x5, starting transfers between devices: 9.05 us -> 10.3 us  [exchange(): return lax.ppermute(value, OWNERS_AXES, pairs)]
    optimization_barrier x0 -> x1, local copies, waits for them, and re-layouts: none -> 0.77 us  [body(): halos[2], slip_panels = lax.optimization_barrier((halos[2], slip_panels))]
  transfers between devices with their start and end apart: 10 -> 11, of which waited for: 4 -> 5; matrix products, arithmetic and copies ran while one was open for 0% -> 2% of each run, Pallas kernels for 16% -> 18%
where the time goes in v5:
time: 47.1 us; the launch traced here: 46.8 us
  starting transfers between devices  21.3 us (45%)
  Pallas kernels  11.8 us (25%)
  waiting for transfers between devices  11.6 us (25%)
  local copies, waits for them, and re-layouts  1.45 us (3%)
  between operations  0.77 us (2%)
    ppermute x5, starting transfers between devices, exchange(): return lax.ppermute(value, OWNERS_AXES, pairs)  10.3 us
    ppermute x4, starting transfers between devices, owner_sum(): lax.ppermute(value, axis, [(i, i ^ k) for i in range(size)])  5.88 us
    pallas_call x1, Pallas kernels, stencil(): pl.pallas_call(functools.partial(stencil_kernel, halo), out_shape=(jax.Sh...  5.84 us
    all_to_all x1, starting transfers between devices, body(): lax.all_to_all(payload, OWNERS_AXES, split_axis=0, concat_axis=0, tiled=T...  5.06 us
    all_to_all x1, waiting for transfers between devices, body(): lax.all_to_all(payload, OWNERS_AXES, split_axis=0, concat_axis=0, tiled=T...  4.99 us
    ppermute x4, waiting for transfers between devices, owner_sum(): lax.ppermute(value, axis, [(i, i ^ k) for i in range(size)])  4.86 us
    pallas_call x1, Pallas kernels, pack(): pl.pallas_call(kernel, out_shape=jax.ShapeDtypeStruct((owners, components...  2.4 us
    pallas_call x1, Pallas kernels, prepare(): pl.pallas_call(functools.partial(prepare_kernel, halo), out_shape=shapes,...  2.23 us
  transfers between devices with their start and end apart: 11, of which 5 were waited for; matrix products, arithmetic and copies ran while one was open for 2% of the time, Pallas kernels for 18%

profile of v5, /device:TPU:0, one launch (start us, length us, event | category | flops | bytes accessed | tf_op | source)
XLA Modules:
  0.0 46.8 jit_solution(11082569536512633642)
XLA Ops:
  0.6 0.0 copy-start.6
  0.6 2.2 %prepare.1 = (bf16[38,32,128]{2,1,0:T(8,128)(2,1)}, bf16[38,32,128]{2,1,0:T(8,128)(2,1)}, f32[9,4,4,128]{3,2,1,0:T(4,128)}, bf16[38,4,128]{2,1,0:T(4,128)(2,1)}, bf16[38,4,128]{2,1,0:T(4,128)(2,1)}) custom-call(f32[1,3,4,32,128]{4,3,2,1,0:T(8,128)} %refs_0_.3, f32[1,3,4,32,128]{4,3,2,1,0:T(8,128)} %refs_1_.3, f32[4,32,128]{2,1,0:T(8,128)} %refs_2_.3, ...), custom_call_target="tpu_custom_call" | custom-call | tf_op jit(solution)/shard_map/prepare/pallas_call | solution.py:201
  2.9 3.1 %collective-permute-start = (bf16[38,32,128]{2,1,0:T(8,128)(2,1)}, bf16[38,32,128]{2,1,0:T(8,128)(2,1)S(1)}, u32[]{:S(2)}, u32[]{:S(2)}) collective-permute-start(bf16[38,32,128]{2,1,0:T(8,128)(2,1)} %get-tuple-element.13), channel_id=1, source_target_pairs={{0,4},{2,6},{4,0},{6,2},{8,12},{10,14},{12,8},{14,10},{1,5},{3,7},... | collective-permute-start | bytes 933896 | tf_op jit(solution)/shard_map/ppermute | solution.py:409
  6.0 0.7 %collective-permute-start.1 = (bf16[38,32,128]{2,1,0:T(8,128)(2,1)}, bf16[38,32,128]{2,1,0:T(8,128)(2,1)S(1)}, u32[]{:S(2)}, u32[]{:S(2)}) collective-permute-start(bf16[38,32,128]{2,1,0:T(8,128)(2,1)} %get-tuple-element.14), channel_id=1, source_target_pairs={{4,8},{6,10},{8,4},{10,6},{5,9},{7,11},{9,5},{11,7},{20,24},{22,26... | collective-permute-start | bytes 933896 | tf_op jit(solution)/shard_map/ppermute | solution.py:409
  6.6 1.6 %collective-permute-start.2 = (f32[9,4,4,128]{3,2,1,0:T(4,128)}, f32[9,4,4,128]{3,2,1,0:T(4,128)S(1)}, u32[]{:S(2)}, u32[]{:S(2)}) collective-permute-start(f32[9,4,4,128]{3,2,1,0:T(4,128)} %get-tuple-element.15), channel_id=1, source_target_pairs={{0,2},{2,0},{4,6},{6,4},{8,10},{10,8},{12,14},{14,12},{1,3},{3,1},... | collective-permute-start | bytes 221192 | tf_op jit(solution)/shard_map/ppermute | solution.py:409
  8.2 4.3 %collective-permute-start.3 = (bf16[38,4,128]{2,1,0:T(4,128)(2,1)}, bf16[38,4,128]{2,1,0:T(4,128)(2,1)S(1)}, u32[]{:S(2)}, u32[]{:S(2)}) collective-permute-start(bf16[38,4,128]{2,1,0:T(4,128)(2,1)} %get-tuple-element.17), channel_id=1, source_target_pairs={{0,6},{2,4},{4,2},{6,0},{8,14},{10,12},{12,10},{14,8},{1,7},{3,5},... | collective-permute-start | bytes 116744 | tf_op jit(solution)/shard_map/ppermute | solution.py:409
  12.5 0.7 %collective-permute-start.4 = (bf16[38,4,128]{2,1,0:T(4,128)(2,1)}, bf16[38,4,128]{2,1,0:T(4,128)(2,1)S(1)}, u32[]{:S(2)}, u32[]{:S(2)}) collective-permute-start(bf16[38,4,128]{2,1,0:T(4,128)(2,1)} %get-tuple-element.18), channel_id=1, source_target_pairs={{4,10},{6,8},{8,6},{10,4},{5,11},{7,9},{9,7},{11,5},{20,26},{22,24... | collective-permute-start | bytes 116744 | tf_op jit(solution)/shard_map/ppermute | solution.py:409
  13.2 0.0 collective-permute-done.2.refs_7_
  13.2 0.0 copy-done.6
  13.2 0.8 %copy.11 = bf16[16,16,6,128]{3,1,0,2:T(8,128)(2,1)} copy(bf16[16,16,6,128]{3,1,2,0:T(8,128)(2,1)S(1)} %copy-done.6) | data formatting | bytes 786432 | tf_op jit(solution)/shard_map/optimization_barrier | solution.py:445
  14.0 2.4 %pack.1 = bf16[8,200,128]{2,1,0:T(8,128)(2,1)} custom-call(s32[16,16]{1,0:T(8,128)} %tiles_ref.1, s32[16,16]{1,0:T(8,128)} %offsets_ref.1, bf16[6,256,128]{2,1,0:T(8,128)(2,1)} %bitcast.9), custom_call_target="tpu_custom_call" | custom-call | tf_op jit(solution)/shard_map/pack/pallas_call | solution.py:79
  16.4 0.0 copy-start
  16.4 0.0 copy-start.1
  16.4 0.0 copy-start.2
  16.4 0.0 copy-start.3
  16.4 0.0 copy-start.4
  16.4 5.1 %all-to-all-start = ((bf16[8,200,128]{2,1,0:T(8,128)(2,1)}), bf16[8,200,128]{2,1,0:T(8,128)(2,1)S(1)}, u32[]{:S(2)}, u32[]{:S(2)}) async-start(bf16[8,200,128]{2,1,0:T(8,128)(2,1)} %pack.1), calls=%async_computation | async-start | bytes 819200 | tf_op jit(solution)/shard_map/all_to_all | solution.py:448
  21.5 0.0 collective-permute-done.3.refs_8_
  21.5 0.0 collective-permute-done.4.refs_9_
  21.5 0.0 collective-permute-done.refs_5_
  21.5 0.0 collective-permute-done.1.refs_6_
  21.5 0.0 copy-done
  21.5 0.0 copy-done.1
  21.5 0.0 copy-done.2
  21.5 0.0 copy-done.3
  21.6 0.0 copy-done.4
  21.6 5.8 %stencil.1 = (f32[1,3,4,32,128]{4,3,2,1,0:T(8,128)}, bf16[512,768]{1,0:T(8,128)(2,1)S(1)}) custom-call(f32[1,3,4,32,128]{4,3,2,1,0:T(8,128)S(1)} %copy-done, f32[1,3,4,32,128]{4,3,2,1,0:T(8,128)S(1)} %copy-done.1, f32[4,32,128]{2,1,0:T(8,128)S(1)} %copy-done.2, f32[4,32,128]{2,1,0:T(8,128)S(1)} %copy-done.3, f32[4,32,128]{2,1,0:T(8,128)S(1)} %copy-done.4, ...), custom_call_target="tpu_custom_call" | custom-call | flops 10000000000 | bytes 100000000 | tf_op jit(solution)/shard_map/stencil/pallas_call | solution.py:310
  27.4 5.0 %all-to-all-done.refs_0_ = bf16[8,200,128]{2,1,0:T(8,128)(2,1)S(1)} async-done(((bf16[8,200,128]{2,1,0:T(8,128)(2,1)}), bf16[8,200,128]{2,1,0:T(8,128)(2,1)S(1)}, u32[]{:S(2)}, u32[]{:S(2)}) %all-to-all-start) | async-done | bytes 409632 | tf_op jit(solution)/shard_map/all_to_all | solution.py:448
  32.4 0.0 copy-start.5
  32.4 0.0 collective-permute-start.5
  32.4 1.7 %collective-permute-done.5.refs_1_ = bf16[8,200,128]{2,1,0:T(8,128)(2,1)S(1)} collective-permute-done((bf16[8,200,128]{2,1,0:T(8,128)(2,1)S(1)}, bf16[8,200,128]{2,1,0:T(8,128)(2,1)S(1)}, u32[]{:S(2)}, u32[]{:S(2)}) %collective-permute-start.5) | collective-permute-done | bytes 409632 | tf_op jit(solution)/shard_map/ppermute | solution.py:452
  34.1 0.0 copy-done.5
  34.1 1.3 %respond.1 = f32[4,128]{1,0:T(4,128)S(1)} custom-call(bf16[512,768]{1,0:T(8,128)(2,1)S(1)} %get-tuple-element.22.strain_ref, s32[1,128]{1,0:T(1,128)S(1)} %bitcast.8, bf16[8,200,128]{2,1,0:T(8,128)(2,1)S(1)} %all-to-all-done.refs_0_, bf16[8,200,128]{2,1,0:T(8,128)(2,1)S(1)} %collective-permute-done.5.refs_1_), custom_call_target="tpu_custom_call" | custom-call | tf_op jit(solution)/shard_map/respond/pallas_call | solution.py:385
  35.4 1.5 %collective-permute-start.6 = (f32[4,128]{1,0:T(4,128)S(1)}, f32[4,128]{1,0:T(4,128)S(1)}, u32[]{:S(2)}, u32[]{:S(2)}) collective-permute-start(f32[4,128]{1,0:T(4,128)S(1)} %respond.1), channel_id=1, source_target_pairs={{0,2},{2,0},{1,3},{3,1},{4,6},{6,4},{5,7},{7,5},{8,10},{10,8},{9,1... | collective-permute-start | bytes 6152 | tf_op jit(solution)/shard_map/ppermute | solution.py:418
  36.9 2.1 %collective-permute-done.6 = f32[4,128]{1,0:T(4,128)S(1)} collective-permute-done((f32[4,128]{1,0:T(4,128)S(1)}, f32[4,128]{1,0:T(4,128)S(1)}, u32[]{:S(2)}, u32[]{:S(2)}) %collective-permute-start.6) | collective-permute-done | bytes 2080 | tf_op jit(solution)/shard_map/ppermute | solution.py:418
  39.1 0.9 %collective-permute-start.7 = (f32[4,128]{1,0:T(4,128)S(1)}, f32[4,128]{1,0:T(4,128)S(1)}, u32[]{:S(2)}, u32[]{:S(2)}) collective-permute-start(f32[4,128]{1,0:T(4,128)S(1)} %add.18), channel_id=1, source_target_pairs={{0,4},{4,0},{8,12},{12,8},{1,5},{5,1},{9,13},{13,9},{2,6},{6,2},{1... | collective-permute-start | bytes 6152 | tf_op jit(solution)/shard_map/ppermute | solution.py:418
  40.0 0.8 %collective-permute-start.8 = (f32[4,128]{1,0:T(4,128)S(1)}, f32[4,128]{1,0:T(4,128)S(1)}, u32[]{:S(2)}, u32[]{:S(2)}) collective-permute-start(f32[4,128]{1,0:T(4,128)S(1)} %add.18), channel_id=1, source_target_pairs={{0,8},{4,12},{8,0},{12,4},{1,9},{5,13},{9,1},{13,5},{2,10},{6,14},... | collective-permute-start | bytes 6152 | tf_op jit(solution)/shard_map/ppermute | solution.py:418
  40.8 2.6 %collective-permute-start.9 = (f32[4,128]{1,0:T(4,128)S(1)}, f32[4,128]{1,0:T(4,128)S(1)}, u32[]{:S(2)}, u32[]{:S(2)}) collective-permute-start(f32[4,128]{1,0:T(4,128)S(1)} %add.18), channel_id=1, source_target_pairs={{0,12},{4,8},{8,4},{12,0},{1,13},{5,9},{9,5},{13,1},{2,14},{6,10},... | collective-permute-start | bytes 6152 | tf_op jit(solution)/shard_map/ppermute | solution.py:418
  43.4 0.0 collective-permute-done.7
  43.5 1.0 %collective-permute-done.8 = f32[4,128]{1,0:T(4,128)S(1)} collective-permute-done((f32[4,128]{1,0:T(4,128)S(1)}, f32[4,128]{1,0:T(4,128)S(1)}, u32[]{:S(2)}, u32[]{:S(2)}) %collective-permute-start.8) | collective-permute-done | bytes 2080 | tf_op jit(solution)/shard_map/ppermute | solution.py:418
  44.5 1.7 %collective-permute-done.9 = f32[4,128]{1,0:T(4,128)S(1)} collective-permute-done((f32[4,128]{1,0:T(4,128)S(1)}, f32[4,128]{1,0:T(4,128)S(1)}, u32[]{:S(2)}, u32[]{:S(2)}) %collective-permute-start.9) | collective-permute-done | bytes 2080 | tf_op jit(solution)/shard_map/ppermute | solution.py:418
  46.2 0.7 %dynamic-slice_bitcast_fusion = f32[1,16,4]{1,2,0:T(4,128)} fusion(f32[4,128]{1,0:T(4,128)S(1)} %add_add_fusion, s32[]{:T(128)S(6)} %select_n.3), kind=kLoop, calls=%fused_computation | loop fusion | bytes 516 | tf_op jit(solution)/shard_map/broadcast_in_dim | solution.py:457
  (2 shorter events, 0.0 us)
Async XLA Ops:
  0.6 12.6 %copy-start.6 = (bf16[16,16,6,128]{3,1,2,0:T(8,128)(2,1)S(1)}, bf16[16,16,6,128]{3,1,2,0:T(8,128)(2,1)}, u32[]{:S(2)}) copy-start(bf16[16,16,6,128]{3,1,2,0:T(8,128)(2,1)} %param.17) | copy-start | bytes 1179652
  2.9 18.6 %collective-permute-start = (bf16[38,32,128]{2,1,0:T(8,128)(2,1)}, bf16[38,32,128]{2,1,0:T(8,128)(2,1)S(1)}, u32[]{:S(2)}, u32[]{:S(2)}) collective-permute-start(bf16[38,32,128]{2,1,0:T(8,128)(2,1)} %get-tuple-element.13), channel_id=1, source_target_pairs={{0,4},{2,6},{4,0},{6,2},{8,12},{10,14},{12,8},{14,10},{1,5},{3,7},... | collective-permute-start | bytes 933896 | tf_op jit(solution)/shard_map/ppermute | solution.py:409
  6.0 15.5 %collective-permute-start.1 = (bf16[38,32,128]{2,1,0:T(8,128)(2,1)}, bf16[38,32,128]{2,1,0:T(8,128)(2,1)S(1)}, u32[]{:S(2)}, u32[]{:S(2)}) collective-permute-start(bf16[38,32,128]{2,1,0:T(8,128)(2,1)} %get-tuple-element.14), channel_id=1, source_target_pairs={{4,8},{6,10},{8,4},{10,6},{5,9},{7,11},{9,5},{11,7},{20,24},{22,26... | collective-permute-start | bytes 933896 | tf_op jit(solution)/shard_map/ppermute | solution.py:409
  6.6 6.6 %collective-permute-start.2 = (f32[9,4,4,128]{3,2,1,0:T(4,128)}, f32[9,4,4,128]{3,2,1,0:T(4,128)S(1)}, u32[]{:S(2)}, u32[]{:S(2)}) collective-permute-start(f32[9,4,4,128]{3,2,1,0:T(4,128)} %get-tuple-element.15), channel_id=1, source_target_pairs={{0,2},{2,0},{4,6},{6,4},{8,10},{10,8},{12,14},{14,12},{1,3},{3,1},... | collective-permute-start | bytes 221192 | tf_op jit(solution)/shard_map/ppermute | solution.py:409
  8.2 13.3 %collective-permute-start.3 = (bf16[38,4,128]{2,1,0:T(4,128)(2,1)}, bf16[38,4,128]{2,1,0:T(4,128)(2,1)S(1)}, u32[]{:S(2)}, u32[]{:S(2)}) collective-permute-start(bf16[38,4,128]{2,1,0:T(4,128)(2,1)} %get-tuple-element.17), channel_id=1, source_target_pairs={{0,6},{2,4},{4,2},{6,0},{8,14},{10,12},{12,10},{14,8},{1,7},{3,5},... | collective-permute-start | bytes 116744 | tf_op jit(solution)/shard_map/ppermute | solution.py:409
  12.5 8.9 %collective-permute-start.4 = (bf16[38,4,128]{2,1,0:T(4,128)(2,1)}, bf16[38,4,128]{2,1,0:T(4,128)(2,1)S(1)}, u32[]{:S(2)}, u32[]{:S(2)}) collective-permute-start(bf16[38,4,128]{2,1,0:T(4,128)(2,1)} %get-tuple-element.18), channel_id=1, source_target_pairs={{4,10},{6,8},{8,6},{10,4},{5,11},{7,9},{9,7},{11,5},{20,26},{22,24... | collective-permute-start | bytes 116744 | tf_op jit(solution)/shard_map/ppermute | solution.py:409
  16.4 5.1 %copy-start = (f32[1,3,4,32,128]{4,3,2,1,0:T(8,128)S(1)}, f32[1,3,4,32,128]{4,3,2,1,0:T(8,128)}, u32[]{:S(2)}) copy-start(f32[1,3,4,32,128]{4,3,2,1,0:T(8,128)} %refs_0_.3) | copy-start | bytes 589828
  16.4 5.1 %copy-start.1 = (f32[1,3,4,32,128]{4,3,2,1,0:T(8,128)S(1)}, f32[1,3,4,32,128]{4,3,2,1,0:T(8,128)}, u32[]{:S(2)}) copy-start(f32[1,3,4,32,128]{4,3,2,1,0:T(8,128)} %refs_1_.3) | copy-start | bytes 589828
  16.4 5.1 %copy-start.2 = (f32[4,32,128]{2,1,0:T(8,128)S(1)}, f32[4,32,128]{2,1,0:T(8,128)}, u32[]{:S(2)}) copy-start(f32[4,32,128]{2,1,0:T(8,128)} %refs_2_.3) | copy-start | bytes 196612
  16.4 5.2 %copy-start.3 = (f32[4,32,128]{2,1,0:T(8,128)S(1)}, f32[4,32,128]{2,1,0:T(8,128)}, u32[]{:S(2)}) copy-start(f32[4,32,128]{2,1,0:T(8,128)} %refs_3_.3) | copy-start | bytes 196612
  16.4 5.2 %copy-start.4 = (f32[4,32,128]{2,1,0:T(8,128)S(1)}, f32[4,32,128]{2,1,0:T(8,128)}, u32[]{:S(2)}) copy-start(f32[4,32,128]{2,1,0:T(8,128)} %refs_4_.3) | copy-start | bytes 196612
  16.4 16.0 %all-to-all-start = ((bf16[8,200,128]{2,1,0:T(8,128)(2,1)}), bf16[8,200,128]{2,1,0:T(8,128)(2,1)S(1)}, u32[]{:S(2)}, u32[]{:S(2)}) async-start(bf16[8,200,128]{2,1,0:T(8,128)(2,1)} %pack.1), calls=%async_computation | async-start | bytes 819200 | tf_op jit(solution)/shard_map/all_to_all | solution.py:448
  32.4 1.8 %copy-start.5 = (s32[128]{0:T(128)S(1)}, s32[128]{0:T(128)}, u32[]{:S(2)}) copy-start(s32[128]{0:T(128)} %param.14) | copy-start | bytes 1540
  32.4 1.7 %collective-permute-start.5 = (bf16[8,200,128]{2,1,0:T(8,128)(2,1)S(1)}, bf16[8,200,128]{2,1,0:T(8,128)(2,1)S(1)}, u32[]{:S(2)}, u32[]{:S(2)}) collective-permute-start(bf16[8,200,128]{2,1,0:T(8,128)(2,1)S(1)} %all-to-all-done.refs_0_), channel_id=1, source_target_pairs={{0,1},{1,0},{2,3},{3,2},{4,5},{5,4},{6,7},{7,6},{8,9},{9,8},{10,11... | collective-permute-start | bytes 1228808 | tf_op jit(solution)/shard_map/ppermute | solution.py:452
  35.4 3.6 %collective-permute-start.6 = (f32[4,128]{1,0:T(4,128)S(1)}, f32[4,128]{1,0:T(4,128)S(1)}, u32[]{:S(2)}, u32[]{:S(2)}) collective-permute-start(f32[4,128]{1,0:T(4,128)S(1)} %respond.1), channel_id=1, source_target_pairs={{0,2},{2,0},{1,3},{3,1},{4,6},{6,4},{5,7},{7,5},{8,10},{10,8},{9,1... | collective-permute-start | bytes 6152 | tf_op jit(solution)/shard_map/ppermute | solution.py:418
  39.1 4.4 %collective-permute-start.7 = (f32[4,128]{1,0:T(4,128)S(1)}, f32[4,128]{1,0:T(4,128)S(1)}, u32[]{:S(2)}, u32[]{:S(2)}) collective-permute-start(f32[4,128]{1,0:T(4,128)S(1)} %add.18), channel_id=1, source_target_pairs={{0,4},{4,0},{8,12},{12,8},{1,5},{5,1},{9,13},{13,9},{2,6},{6,2},{1... | collective-permute-start | bytes 6152 | tf_op jit(solution)/shard_map/ppermute | solution.py:418
  40.0 4.5 %collective-permute-start.8 = (f32[4,128]{1,0:T(4,128)S(1)}, f32[4,128]{1,0:T(4,128)S(1)}, u32[]{:S(2)}, u32[]{:S(2)}) collective-permute-start(f32[4,128]{1,0:T(4,128)S(1)} %add.18), channel_id=1, source_target_pairs={{0,8},{4,12},{8,0},{12,4},{1,9},{5,13},{9,1},{13,5},{2,10},{6,14},... | collective-permute-start | bytes 6152 | tf_op jit(solution)/shard_map/ppermute | solution.py:418
  40.8 5.4 %collective-permute-start.9 = (f32[4,128]{1,0:T(4,128)S(1)}, f32[4,128]{1,0:T(4,128)S(1)}, u32[]{:S(2)}, u32[]{:S(2)}) collective-permute-start(f32[4,128]{1,0:T(4,128)S(1)} %add.18), channel_id=1, source_target_pairs={{0,12},{4,8},{8,4},{12,0},{1,13},{5,9},{9,5},{13,1},{2,14},{6,10},... | collective-permute-start | bytes 6152 | tf_op jit(solution)/shard_map/ppermute | solution.py:418

commit v6 on v5

--- a/solution.py
+++ b/solution.py
@@ -376,7 +376,8 @@
             delayed, gather, NT, preferred_element_type=jnp.float32, precision=lax.Precision.HIGHEST
         )
         total = part if total is None else total + part
-    out_ref[...] = total[:STEPS]
+    for s in range(owners):
+        out_ref[s] = total[:STEPS, s * records : (s + 1) * records]
 
 
 def respond(owners, ranks, records, strain, columns, halves):
@@ -384,7 +385,7 @@
     operands = (strain, columns, *halves[0], *halves[1])
     return pl.pallas_call(
         functools.partial(response_kernel, owners, ranks, records),
-        out_shape=jax.ShapeDtypeStruct((STEPS, owners * records), jnp.float32),
+        out_shape=jax.ShapeDtypeStruct((owners, STEPS, records), jnp.float32),
         in_specs=[vmem] * len(operands),
         out_specs=vmem,
         compiler_params=pltpu.CompilerParams(vmem_limit_bytes=40 << 20),
@@ -407,22 +408,6 @@
             if x is not None and y is not None:
                 pairs.append((i * gys + j, x * gys + y))
     return lax.ppermute(value, OWNERS_AXES, pairs)
-
-
-def owner_sum(value):
-    for axis in ("gy", "gx"):
-        size = lax.axis_size(axis)
-        if size & (size - 1):
-            value = lax.psum(value, axis)
-        elif size <= 4:
-            parts = [lax.ppermute(value, axis, [(i, i ^ k) for i in range(size)]) for k in range(1, size)]
-            value = functools.reduce(jnp.add, parts, value)
-        else:
-            bit = 1
-            while bit < size:
-                value = value + lax.ppermute(value, axis, [(i, i ^ bit) for i in range(size)])
-                bit *= 2
-    return value
 
 
 def body(displacement, previous, first_lame, shear_modulus, buoyancy, tile_column, rupture_tiles, slip_offsets, slip_panels):
@@ -440,9 +425,9 @@
     turns_y = range(1 if gys == 2 else 2)
     sent = prepare(halo, len(turns_y), *waves)
     ways = [(0, None), (1, None)] + [(x, q) for q in turns_y for x in (None, 0, 1)]
+    slip_panels, sent = lax.optimization_barrier((slip_panels, sent))
     halos = [exchange(value, gxs, gys, *way) for value, way in zip(sent, ways)]
 
-    halos[2], slip_panels = lax.optimization_barrier((halos[2], slip_panels))
     panels = slip_panels.reshape(entries, components, nz).transpose(1, 0, 2)
     payload = pack(owners, slots, ranks, rupture_tiles, slip_offsets, panels)
     arrived = lax.all_to_all(payload, OWNERS_AXES, split_axis=0, concat_axis=0, tiled=True)
@@ -452,9 +437,8 @@
     other = lax.ppermute(arrived, "comp", [(0, 1), (1, 0)])
     halves = [unpack(owners, ranks, components, v) for v in (arrived, other)]
     partial = respond(owners, ranks, records, strain, tile_column.reshape(1, slots), halves)
-    summed = owner_sum(partial)
-    mine = lax.dynamic_slice_in_dim(summed, owner_index() * records, records, axis=1)
-    return final, mine.T[None]
+    shares = lax.all_to_all(partial, OWNERS_AXES, split_axis=0, concat_axis=0, tiled=True)
+    return final, jnp.sum(shares, axis=0).T[None]
 
 
 def solution(mesh):

time: 47.1 us -> 46.5 us (0.987)
  blocking collectives: 0 us -> 10.1 us
  starting transfers between devices: 21.3 us -> 15.4 us
  waiting for transfers between devices: 11.6 us -> 6.73 us
  local copies, waits for them, and re-layouts: 1.45 us -> 0.81 us
  other arithmetic: 0.01 us -> 0.6 us
    all_to_all x0 -> x1, blocking collectives: none -> 10.1 us  [body(): lax.all_to_all(partial, OWNERS_AXES, split_axis=0, concat_axis=0, tiled=T...]
    ppermute x4 -> x0, starting transfers between devices: 5.88 us -> none  [owner_sum(): lax.ppermute(value, axis, [(i, i ^ k) for i in range(size)])]
    ppermute x4 -> x0, waiting for transfers between devices: 4.86 us -> none  [owner_sum(): lax.ppermute(value, axis, [(i, i ^ k) for i in range(size)])]
    broadcast_in_dim x1 -> x0, local copies, waits for them, and re-layouts: 0.65 us -> none  [body(): return (final, mine.T[None])]
    reduce_sum x0 -> x1, other arithmetic: none -> 0.6 us  [body(): return (final, jnp.sum(shares, axis=0).T[None])]
  transfers between devices with their start and end apart: 11 -> 7, of which waited for: 5 -> 2; matrix products, arithmetic and copies ran while one was open for 2% -> 2% of each run, Pallas kernels for 18% -> 18%
where the time goes in v6:
time: 46.5 us; the launch traced here: 46.1 us
  starting transfers between devices  15.4 us (33%)
  Pallas kernels  11.8 us (25%)
  blocking collectives  10.1 us (22%)
  waiting for transfers between devices  6.73 us (14%)
  local copies, waits for them, and re-layouts  0.81 us (2%)
  between operations  0.77 us (2%)
  other arithmetic  0.6 us (1%)
    ppermute x5, starting transfers between devices, exchange(): return lax.ppermute(value, OWNERS_AXES, pairs)  10.3 us
    all_to_all x1, blocking collectives, body(): lax.all_to_all(partial, OWNERS_AXES, split_axis=0, concat_axis=0, tiled=T...  10.1 us
    pallas_call x1, Pallas kernels, stencil(): pl.pallas_call(functools.partial(stencil_kernel, halo), out_shape=(jax.Sh...  5.84 us
    all_to_all x1, starting transfers between devices, body(): lax.all_to_all(payload, OWNERS_AXES, split_axis=0, concat_axis=0, tiled=T...  5.06 us
    all_to_all x1, waiting for transfers between devices, body(): lax.all_to_all(payload, OWNERS_AXES, split_axis=0, concat_axis=0, tiled=T...  4.97 us
    pallas_call x1, Pallas kernels, pack(): pl.pallas_call(kernel, out_shape=jax.ShapeDtypeStruct((owners, components...  2.39 us
    pallas_call x1, Pallas kernels, prepare(): pl.pallas_call(functools.partial(prepare_kernel, halo), out_shape=shapes,...  2.18 us
    ppermute x1, waiting for transfers between devices, body(): other = lax.ppermute(arrived, 'comp', [(0, 1), (1, 0)])  1.74 us
  transfers between devices with their start and end apart: 7, of which 2 were waited for; matrix products, arithmetic and copies ran while one was open for 2% of the time, Pallas kernels for 18%

profile of v6, /device:TPU:0, one launch (start us, length us, event | category | flops | bytes accessed | tf_op | source)
XLA Modules:
  0.0 46.1 jit_solution(1811654144752375476)
XLA Ops:
  0.6 0.0 copy-start.6
  0.6 2.2 %prepare.1 = (bf16[38,32,128]{2,1,0:T(8,128)(2,1)}, bf16[38,32,128]{2,1,0:T(8,128)(2,1)}, f32[9,4,4,128]{3,2,1,0:T(4,128)}, bf16[38,4,128]{2,1,0:T(4,128)(2,1)}, bf16[38,4,128]{2,1,0:T(4,128)(2,1)}) custom-call(f32[1,3,4,32,128]{4,3,2,1,0:T(8,128)} %refs_0_.3, f32[1,3,4,32,128]{4,3,2,1,0:T(8,128)} %refs_1_.3, f32[4,32,128]{2,1,0:T(8,128)} %refs_2_.3, ...), custom_call_target="tpu_custom_call" | custom-call | tf_op jit(solution)/shard_map/prepare/pallas_call | solution.py:201
  2.8 3.1 %collective-permute-start = (bf16[38,32,128]{2,1,0:T(8,128)(2,1)}, bf16[38,32,128]{2,1,0:T(8,128)(2,1)S(1)}, u32[]{:S(2)}, u32[]{:S(2)}) collective-permute-start(bf16[38,32,128]{2,1,0:T(8,128)(2,1)} %get-tuple-element.22), channel_id=1, source_target_pairs={{0,4},{2,6},{4,0},{6,2},{8,12},{10,14},{12,8},{14,10},{1,5},{3,7},... | collective-permute-start | bytes 933896 | tf_op jit(solution)/shard_map/ppermute | solution.py:410
  5.9 0.7 %collective-permute-start.1 = (bf16[38,32,128]{2,1,0:T(8,128)(2,1)}, bf16[38,32,128]{2,1,0:T(8,128)(2,1)S(1)}, u32[]{:S(2)}, u32[]{:S(2)}) collective-permute-start(bf16[38,32,128]{2,1,0:T(8,128)(2,1)} %get-tuple-element.23), channel_id=1, source_target_pairs={{4,8},{6,10},{8,4},{10,6},{5,9},{7,11},{9,5},{11,7},{20,24},{22,26... | collective-permute-start | bytes 933896 | tf_op jit(solution)/shard_map/ppermute | solution.py:410
  6.6 1.6 %collective-permute-start.2 = (f32[9,4,4,128]{3,2,1,0:T(4,128)}, f32[9,4,4,128]{3,2,1,0:T(4,128)S(1)}, u32[]{:S(2)}, u32[]{:S(2)}) collective-permute-start(f32[9,4,4,128]{3,2,1,0:T(4,128)} %get-tuple-element.24), channel_id=1, source_target_pairs={{0,2},{2,0},{4,6},{6,4},{8,10},{10,8},{12,14},{14,12},{1,3},{3,1},... | collective-permute-start | bytes 221192 | tf_op jit(solution)/shard_map/ppermute | solution.py:410
  8.2 4.3 %collective-permute-start.3 = (bf16[38,4,128]{2,1,0:T(4,128)(2,1)}, bf16[38,4,128]{2,1,0:T(4,128)(2,1)S(1)}, u32[]{:S(2)}, u32[]{:S(2)}) collective-permute-start(bf16[38,4,128]{2,1,0:T(4,128)(2,1)} %get-tuple-element.25), channel_id=1, source_target_pairs={{0,6},{2,4},{4,2},{6,0},{8,14},{10,12},{12,10},{14,8},{1,7},{3,5},... | collective-permute-start | bytes 116744 | tf_op jit(solution)/shard_map/ppermute | solution.py:410
  12.5 0.7 %collective-permute-start.4 = (bf16[38,4,128]{2,1,0:T(4,128)(2,1)}, bf16[38,4,128]{2,1,0:T(4,128)(2,1)S(1)}, u32[]{:S(2)}, u32[]{:S(2)}) collective-permute-start(bf16[38,4,128]{2,1,0:T(4,128)(2,1)} %get-tuple-element.26), channel_id=1, source_target_pairs={{4,10},{6,8},{8,6},{10,4},{5,11},{7,9},{9,7},{11,5},{20,26},{22,24... | collective-permute-start | bytes 116744 | tf_op jit(solution)/shard_map/ppermute | solution.py:410
  13.2 0.0 copy-done.6
  13.2 0.8 %copy.11 = bf16[16,16,6,128]{3,1,0,2:T(8,128)(2,1)} copy(bf16[16,16,6,128]{3,1,2,0:T(8,128)(2,1)S(1)} %copy-done.6) | data formatting | bytes 786432 | tf_op jit(solution)/shard_map/optimization_barrier | solution.py:428
  14.0 2.4 %pack.1 = bf16[8,200,128]{2,1,0:T(8,128)(2,1)} custom-call(s32[16,16]{1,0:T(8,128)} %tiles_ref.1, s32[16,16]{1,0:T(8,128)} %offsets_ref.1, bf16[6,256,128]{2,1,0:T(8,128)(2,1)} %bitcast.8), custom_call_target="tpu_custom_call" | custom-call | tf_op jit(solution)/shard_map/pack/pallas_call | solution.py:79
  16.3 0.0 copy-start
  16.3 0.0 copy-start.1
  16.4 0.0 copy-start.2
  16.4 0.0 copy-start.3
  16.4 0.0 copy-start.4
  16.4 5.1 %all-to-all-start = ((bf16[8,200,128]{2,1,0:T(8,128)(2,1)}), bf16[8,200,128]{2,1,0:T(8,128)(2,1)S(1)}, u32[]{:S(2)}, u32[]{:S(2)}) async-start(bf16[8,200,128]{2,1,0:T(8,128)(2,1)} %pack.1), calls=%async_computation | async-start | bytes 819200 | tf_op jit(solution)/shard_map/all_to_all | solution.py:433
  21.4 0.0 collective-permute-done.3.refs_8_
  21.4 0.0 collective-permute-done.4.refs_9_
  21.5 0.0 collective-permute-done.2.refs_7_
  21.5 0.0 collective-permute-done.refs_5_
  21.5 0.0 collective-permute-done.1.refs_6_
  21.5 0.0 copy-done
  21.5 0.0 copy-done.1
  21.5 0.0 copy-done.2
  21.5 0.0 copy-done.3
  21.5 0.0 copy-done.4
  21.5 5.8 %stencil.1 = (f32[1,3,4,32,128]{4,3,2,1,0:T(8,128)}, bf16[512,768]{1,0:T(8,128)(2,1)S(1)}) custom-call(f32[1,3,4,32,128]{4,3,2,1,0:T(8,128)S(1)} %copy-done, f32[1,3,4,32,128]{4,3,2,1,0:T(8,128)S(1)} %copy-done.1, f32[4,32,128]{2,1,0:T(8,128)S(1)} %copy-done.2, f32[4,32,128]{2,1,0:T(8,128)S(1)} %copy-done.3, f32[4,32,128]{2,1,0:T(8,128)S(1)} %copy-done.4, ...), custom_call_target="tpu_custom_call" | custom-call | flops 10000000000 | bytes 100000000 | tf_op jit(solution)/shard_map/stencil/pallas_call | solution.py:310
  27.4 5.0 %all-to-all-done.refs_0_ = bf16[8,200,128]{2,1,0:T(8,128)(2,1)S(1)} async-done(((bf16[8,200,128]{2,1,0:T(8,128)(2,1)}), bf16[8,200,128]{2,1,0:T(8,128)(2,1)S(1)}, u32[]{:S(2)}, u32[]{:S(2)}) %all-to-all-start) | async-done | bytes 409632 | tf_op jit(solution)/shard_map/all_to_all | solution.py:433
  32.3 0.0 copy-start.5
  32.3 0.0 collective-permute-start.5
  32.3 1.7 %collective-permute-done.5.refs_1_ = bf16[8,200,128]{2,1,0:T(8,128)(2,1)S(1)} collective-permute-done((bf16[8,200,128]{2,1,0:T(8,128)(2,1)S(1)}, bf16[8,200,128]{2,1,0:T(8,128)(2,1)S(1)}, u32[]{:S(2)}, u32[]{:S(2)}) %collective-permute-start.5) | collective-permute-done | bytes 409632 | tf_op jit(solution)/shard_map/ppermute | solution.py:437
  34.1 0.0 copy-done.5
  34.1 1.4 %respond.1 = f32[8,4,16]{2,1,0:T(4,128)S(1)} custom-call(bf16[512,768]{1,0:T(8,128)(2,1)S(1)} %get-tuple-element.30.strain_ref, s32[1,128]{1,0:T(1,128)S(1)} %bitcast.7, bf16[8,200,128]{2,1,0:T(8,128)(2,1)S(1)} %all-to-all-done.refs_0_, bf16[8,200,128]{2,1,0:T(8,128)(2,1)S(1)} %collective-permute-done.5.refs_1_), custom_call_target="tpu_custom_call" | custom-call | tf_op jit(solution)/shard_map/respond/pallas_call | solution.py:386
  35.5 10.1 %all_to_all.10 = f32[8,4,16]{2,1,0:T(4,128)S(1)} all-to-all(f32[8,4,16]{2,1,0:T(4,128)S(1)} %respond.1), channel_id=1, replica_groups=mesh['site'=2,'gx'=4,'gy'=2,'comp'=2] {'gx','gy'}, dimensions={0} | all-to-all | bytes 4096 | tf_op jit(solution)/shard_map/all_to_all | solution.py:440
  45.5 0.6 %reduce_sum.9 = f32[4,16]{1,0:T(4,128)} reduce(f32[8,4,16]{2,1,0:T(4,128)S(1)} %all_to_all.10, f32[]{:T(128)} %constant.0.clone.1), dimensions={0}, to_apply=%region_0.0 | reduce | flops 448 | bytes 2308 | tf_op jit(solution)/shard_map/reduce_sum | solution.py:441
Async XLA Ops:
  0.6 12.5 %copy-start.6 = (bf16[16,16,6,128]{3,1,2,0:T(8,128)(2,1)S(1)}, bf16[16,16,6,128]{3,1,2,0:T(8,128)(2,1)}, u32[]{:S(2)}) copy-start(bf16[16,16,6,128]{3,1,2,0:T(8,128)(2,1)} %param.17) | copy-start | bytes 1179652
  2.8 18.6 %collective-permute-start = (bf16[38,32,128]{2,1,0:T(8,128)(2,1)}, bf16[38,32,128]{2,1,0:T(8,128)(2,1)S(1)}, u32[]{:S(2)}, u32[]{:S(2)}) collective-permute-start(bf16[38,32,128]{2,1,0:T(8,128)(2,1)} %get-tuple-element.22), channel_id=1, source_target_pairs={{0,4},{2,6},{4,0},{6,2},{8,12},{10,14},{12,8},{14,10},{1,5},{3,7},... | collective-permute-start | bytes 933896 | tf_op jit(solution)/shard_map/ppermute | solution.py:410
  5.9 15.6 %collective-permute-start.1 = (bf16[38,32,128]{2,1,0:T(8,128)(2,1)}, bf16[38,32,128]{2,1,0:T(8,128)(2,1)S(1)}, u32[]{:S(2)}, u32[]{:S(2)}) collective-permute-start(bf16[38,32,128]{2,1,0:T(8,128)(2,1)} %get-tuple-element.23), channel_id=1, source_target_pairs={{4,8},{6,10},{8,4},{10,6},{5,9},{7,11},{9,5},{11,7},{20,24},{22,26... | collective-permute-start | bytes 933896 | tf_op jit(solution)/shard_map/ppermute | solution.py:410
  6.6 14.9 %collective-permute-start.2 = (f32[9,4,4,128]{3,2,1,0:T(4,128)}, f32[9,4,4,128]{3,2,1,0:T(4,128)S(1)}, u32[]{:S(2)}, u32[]{:S(2)}) collective-permute-start(f32[9,4,4,128]{3,2,1,0:T(4,128)} %get-tuple-element.24), channel_id=1, source_target_pairs={{0,2},{2,0},{4,6},{6,4},{8,10},{10,8},{12,14},{14,12},{1,3},{3,1},... | collective-permute-start | bytes 221192 | tf_op jit(solution)/shard_map/ppermute | solution.py:410
  8.2 13.3 %collective-permute-start.3 = (bf16[38,4,128]{2,1,0:T(4,128)(2,1)}, bf16[38,4,128]{2,1,0:T(4,128)(2,1)S(1)}, u32[]{:S(2)}, u32[]{:S(2)}) collective-permute-start(bf16[38,4,128]{2,1,0:T(4,128)(2,1)} %get-tuple-element.25), channel_id=1, source_target_pairs={{0,6},{2,4},{4,2},{6,0},{8,14},{10,12},{12,10},{14,8},{1,7},{3,5},... | collective-permute-start | bytes 116744 | tf_op jit(solution)/shard_map/ppermute | solution.py:410
  12.5 8.9 %collective-permute-start.4 = (bf16[38,4,128]{2,1,0:T(4,128)(2,1)}, bf16[38,4,128]{2,1,0:T(4,128)(2,1)S(1)}, u32[]{:S(2)}, u32[]{:S(2)}) collective-permute-start(bf16[38,4,128]{2,1,0:T(4,128)(2,1)} %get-tuple-element.26), channel_id=1, source_target_pairs={{4,10},{6,8},{8,6},{10,4},{5,11},{7,9},{9,7},{11,5},{20,26},{22,24... | collective-permute-start | bytes 116744 | tf_op jit(solution)/shard_map/ppermute | solution.py:410
  16.3 5.1 %copy-start = (f32[1,3,4,32,128]{4,3,2,1,0:T(8,128)S(1)}, f32[1,3,4,32,128]{4,3,2,1,0:T(8,128)}, u32[]{:S(2)}) copy-start(f32[1,3,4,32,128]{4,3,2,1,0:T(8,128)} %refs_0_.3) | copy-start | bytes 589828
  16.3 5.1 %copy-start.1 = (f32[1,3,4,32,128]{4,3,2,1,0:T(8,128)S(1)}, f32[1,3,4,32,128]{4,3,2,1,0:T(8,128)}, u32[]{:S(2)}) copy-start(f32[1,3,4,32,128]{4,3,2,1,0:T(8,128)} %refs_1_.3) | copy-start | bytes 589828
  16.4 5.2 %copy-start.2 = (f32[4,32,128]{2,1,0:T(8,128)S(1)}, f32[4,32,128]{2,1,0:T(8,128)}, u32[]{:S(2)}) copy-start(f32[4,32,128]{2,1,0:T(8,128)} %refs_2_.3) | copy-start | bytes 196612
  16.4 5.2 %copy-start.3 = (f32[4,32,128]{2,1,0:T(8,128)S(1)}, f32[4,32,128]{2,1,0:T(8,128)}, u32[]{:S(2)}) copy-start(f32[4,32,128]{2,1,0:T(8,128)} %refs_3_.3) | copy-start | bytes 196612
  16.4 5.2 %copy-start.4 = (f32[4,32,128]{2,1,0:T(8,128)S(1)}, f32[4,32,128]{2,1,0:T(8,128)}, u32[]{:S(2)}) copy-start(f32[4,32,128]{2,1,0:T(8,128)} %refs_4_.3) | copy-start | bytes 196612
  16.4 16.0 %all-to-all-start = ((bf16[8,200,128]{2,1,0:T(8,128)(2,1)}), bf16[8,200,128]{2,1,0:T(8,128)(2,1)S(1)}, u32[]{:S(2)}, u32[]{:S(2)}) async-start(bf16[8,200,128]{2,1,0:T(8,128)(2,1)} %pack.1), calls=%async_computation | async-start | bytes 819200 | tf_op jit(solution)/shard_map/all_to_all | solution.py:433
  32.3 1.8 %copy-start.5 = (s32[128]{0:T(128)S(1)}, s32[128]{0:T(128)}, u32[]{:S(2)}) copy-start(s32[128]{0:T(128)} %param.14) | copy-start | bytes 1540
  32.3 1.7 %collective-permute-start.5 = (bf16[8,200,128]{2,1,0:T(8,128)(2,1)S(1)}, bf16[8,200,128]{2,1,0:T(8,128)(2,1)S(1)}, u32[]{:S(2)}, u32[]{:S(2)}) collective-permute-start(bf16[8,200,128]{2,1,0:T(8,128)(2,1)S(1)} %all-to-all-done.refs_0_), channel_id=1, source_target_pairs={{0,1},{1,0},{2,3},{3,2},{4,5},{5,4},{6,7},{7,6},{8,9},{9,8},{10,11... | collective-permute-start | bytes 1228808 | tf_op jit(solution)/shard_map/ppermute | solution.py:437

commit v7 on v6

--- a/solution.py
+++ b/solution.py
@@ -50,8 +50,9 @@
     select = (iota((sent, entries), 0) == place).astype(jnp.bfloat16)
     blocks = out_ref.shape[0]
     length = sent // blocks
-    for i in range(panels_ref.shape[0]):
-        part = jnp.dot(select, panels_ref[i], preferred_element_type=jnp.float32).astype(jnp.bfloat16)
+    components = panels_ref.shape[1]
+    for i in range(components):
+        part = jnp.dot(select, panels_ref[:, i].reshape(entries, LANES), preferred_element_type=jnp.float32).astype(jnp.bfloat16)
         out_ref[:, i * length : (i + 1) * length, :] = part.reshape(blocks, length, LANES)
     group = LANES // ranks
     lane = jnp.where(mine, rank + ranks * (me % group), -1)
@@ -62,7 +63,7 @@
         meta.append(lax.dot_general(table, marks, NT, preferred_element_type=jnp.float32).astype(jnp.bfloat16))
     if meta_ref is None:
         tail = jnp.concatenate([m.reshape(owners, 1, LANES) for m in meta] * 4, axis=1)
-        out_ref[:, panels_ref.shape[0] * length :, :] = tail
+        out_ref[:, components * length :, :] = tail
     else:
         for k in range(2):
             meta_ref[k] = meta[k]
@@ -72,7 +73,7 @@
 
 
 def pack(owners, slots, ranks, tiles, offsets, panels):
-    components = panels.shape[0]
+    components = panels.shape[1]
     vmem = pl.BlockSpec(memory_space=pltpu.VMEM)
     kernel = functools.partial(pack_kernel, owners, slots, ranks)
     if ranks % 16 == 0:
@@ -329,60 +330,59 @@
     sent = owners * ranks
     group = LANES // ranks
     columns = strain_ref.shape[0] // STEPS
-    total, out_ref = None, refs[-1]
+    pan, out_ref = refs[0], refs[-1]
     friendly = ranks % 16 == 0
-    for half in range(2):
-        pan = refs[half if friendly else 2 * half]
-        length = sent // pan.shape[0]
-        rows = []
-        for k in range(2):
-            table = pan[:, 6 * length + k, :] if friendly else refs[2 * half + 1][k]
-            table = table.astype(jnp.float32)
-            parts = [
-                jnp.sum(table[g * group : (g + 1) * group], axis=0, keepdims=True) for g in range(owners // group)
-            ]
-            rows.append(jnp.concatenate(parts, axis=1))
-        slot, record = rows
-        owner = iota((1, sent), 1) // ranks
-        spread = (iota((points, sent), 0) == slot.astype(jnp.int32)).astype(jnp.bfloat16)
-        table = jnp.broadcast_to(column_ref[...].astype(jnp.float32), (8, points)).astype(jnp.bfloat16)
-        column = jnp.dot(table, spread, preferred_element_type=jnp.float32)[:1].astype(jnp.int32)
-        grid = None
-        for i in range(3):
-            right = jnp.concatenate(
-                [pan[:, (2 * i + k) * length : (2 * i + k + 1) * length, :].reshape(sent, LANES) for k in range(2)],
-                axis=1,
-            )
-            left = strain_ref[:, 2 * i * LANES : (2 * i + 2) * LANES]
-            term = lax.dot_general(left, right, NT, preferred_element_type=jnp.float32)
-            grid = term if grid is None else grid + term
-        mark = iota((columns, sent), 0) == column
-        reply = [
-            jnp.sum(jnp.where(mark, grid[m * columns : (m + 1) * columns], 0.0), axis=0, keepdims=True)
-            for m in range(STEPS)
+    earlier = refs[-2] if len(refs) > (2 if friendly else 3) else None
+    length = sent // pan.shape[0]
+    rows = []
+    for k in range(2):
+        table = pan[:, 6 * length + k, :] if friendly else refs[1][k]
+        table = table.astype(jnp.float32)
+        parts = [
+            jnp.sum(table[g * group : (g + 1) * group], axis=0, keepdims=True) for g in range(owners // group)
         ]
-        record = record.astype(jnp.int32)
-        offset = record % STEPS
-        delayed = []
-        for n in range(STEPS):
-            value = jnp.where(offset == n, reply[0], 0.0)
-            for m in range(1, n + 1):
-                value = value + jnp.where(offset == n - m, reply[m], 0.0)
-            delayed.append(value)
-        delayed = jnp.concatenate(delayed + [jnp.zeros((8 - STEPS, sent), jnp.float32)], axis=0)
-        key = owner * records + record // STEPS
-        gather = (iota((owners * records, sent), 0) == key).astype(jnp.float32)
-        part = lax.dot_general(
-            delayed, gather, NT, preferred_element_type=jnp.float32, precision=lax.Precision.HIGHEST
+        rows.append(jnp.concatenate(parts, axis=1))
+    slot, record = rows
+    owner = iota((1, sent), 1) // ranks
+    spread = (iota((points, sent), 0) == slot.astype(jnp.int32)).astype(jnp.bfloat16)
+    table = jnp.broadcast_to(column_ref[...].astype(jnp.float32), (8, points)).astype(jnp.bfloat16)
+    column = jnp.dot(table, spread, preferred_element_type=jnp.float32)[:1].astype(jnp.int32)
+    grid = None
+    for i in range(3):
+        right = jnp.concatenate(
+            [pan[:, (2 * i + k) * length : (2 * i + k + 1) * length, :].reshape(sent, LANES) for k in range(2)],
+            axis=1,
         )
-        total = part if total is None else total + part
+        left = strain_ref[:, 2 * i * LANES : (2 * i + 2) * LANES]
+        term = lax.dot_general(left, right, NT, preferred_element_type=jnp.float32)
+        grid = term if grid is None else grid + term
+    mark = iota((columns, sent), 0) == column
+    reply = [
+        jnp.sum(jnp.where(mark, grid[m * columns : (m + 1) * columns], 0.0), axis=0, keepdims=True)
+        for m in range(STEPS)
+    ]
+    record = record.astype(jnp.int32)
+    offset = record % STEPS
+    delayed = []
+    for n in range(STEPS):
+        value = jnp.where(offset == n, reply[0], 0.0)
+        for m in range(1, n + 1):
+            value = value + jnp.where(offset == n - m, reply[m], 0.0)
+        delayed.append(value)
+    delayed = jnp.concatenate(delayed + [jnp.zeros((8 - STEPS, sent), jnp.float32)], axis=0)
+    key = owner * records + record // STEPS
+    gather = (iota((owners * records, sent), 0) == key).astype(jnp.float32)
+    part = lax.dot_general(
+        delayed, gather, NT, preferred_element_type=jnp.float32, precision=lax.Precision.HIGHEST
+    )
     for s in range(owners):
-        out_ref[s] = total[:STEPS, s * records : (s + 1) * records]
-
-
-def respond(owners, ranks, records, strain, columns, halves):
+        share = part[:STEPS, s * records : (s + 1) * records]
+        out_ref[s] = share if earlier is None else share + earlier[s]
+
+
+def respond(owners, ranks, records, strain, columns, half, *earlier):
     vmem = pl.BlockSpec(memory_space=pltpu.VMEM)
-    operands = (strain, columns, *halves[0], *halves[1])
+    operands = (strain, columns, *half, *earlier)
     return pl.pallas_call(
         functools.partial(response_kernel, owners, ranks, records),
         out_shape=jax.ShapeDtypeStruct((owners, STEPS, records), jnp.float32),
@@ -428,15 +428,16 @@
     slip_panels, sent = lax.optimization_barrier((slip_panels, sent))
     halos = [exchange(value, gxs, gys, *way) for value, way in zip(sent, ways)]
 
-    panels = slip_panels.reshape(entries, components, nz).transpose(1, 0, 2)
+    panels = slip_panels.transpose(0, 2, 1, 3)
     payload = pack(owners, slots, ranks, rupture_tiles, slip_offsets, panels)
     arrived = lax.all_to_all(payload, OWNERS_AXES, split_axis=0, concat_axis=0, tiled=True)
 
     final, strain = stencil(halo, *waves, halos)
     arrived, strain = lax.optimization_barrier((arrived, strain))
     other = lax.ppermute(arrived, "comp", [(0, 1), (1, 0)])
-    halves = [unpack(owners, ranks, components, v) for v in (arrived, other)]
-    partial = respond(owners, ranks, records, strain, tile_column.reshape(1, slots), halves)
+    columns = tile_column.reshape(1, slots)
+    partial = respond(owners, ranks, records, strain, columns, unpack(owners, ranks, components, arrived))
+    partial = respond(owners, ranks, records, strain, columns, unpack(owners, ranks, components, other), partial)
     shares = lax.all_to_all(partial, OWNERS_AXES, split_axis=0, concat_axis=0, tiled=True)
     return final, jnp.sum(shares, axis=0).T[None]
 

time: 46.5 us -> 45.1 us (0.970)
  waiting for transfers between devices: 6.73 us -> 5.26 us
    ppermute x1, waiting for transfers between devices: 1.74 us -> 0.28 us  [body(): other = lax.ppermute(arrived, 'comp', [(0, 1), (1, 0)])]
    optimization_barrier x1 -> x0, local copies, waits for them, and re-layouts: 0.78 us -> none  [body(): slip_panels, sent = lax.optimization_barrier((slip_panels, sent))]
    unnamed x14 -> x12, local copies, waits for them, and re-layouts: 0.03 us -> 0.67 us
    pallas_call x1 -> x2, Pallas kernels: 1.37 us -> 1.63 us  [respond(): pl.pallas_call(functools.partial(response_kernel, owners, ranks, records)...]
  transfers between devices with their start and end apart: 7 -> 7, of which waited for: 2 -> 2; matrix products, arithmetic and copies ran while one was open for 2% -> 0% of each run, Pallas kernels for 18% -> 20%
where the time goes in v7:
time: 45.1 us; the launch traced here: 44.8 us
  starting transfers between devices  15.4 us (34%)
  Pallas kernels  12 us (27%)
  blocking collectives  10.1 us (22%)
  waiting for transfers between devices  5.26 us (12%)
  between operations  0.75 us (2%)
  local copies, waits for them, and re-layouts  0.67 us (1%)
  other arithmetic  0.6 us (1%)
    ppermute x5, starting transfers between devices, exchange(): return lax.ppermute(value, OWNERS_AXES, pairs)  10.3 us
    all_to_all x1, blocking collectives, body(): lax.all_to_all(partial, OWNERS_AXES, split_axis=0, concat_axis=0, tiled=T...  10.1 us
    pallas_call x1, Pallas kernels, stencil(): pl.pallas_call(functools.partial(stencil_kernel, halo), out_shape=(jax.Sh...  5.84 us
    all_to_all x1, starting transfers between devices, body(): lax.all_to_all(payload, OWNERS_AXES, split_axis=0, concat_axis=0, tiled=T...  5.06 us
    all_to_all x1, waiting for transfers between devices, body(): lax.all_to_all(payload, OWNERS_AXES, split_axis=0, concat_axis=0, tiled=T...  4.98 us
    pallas_call x1, Pallas kernels, pack(): pl.pallas_call(kernel, out_shape=jax.ShapeDtypeStruct((owners, components...  2.4 us
    pallas_call x1, Pallas kernels, prepare(): pl.pallas_call(functools.partial(prepare_kernel, halo), out_shape=shapes,...  2.15 us
    pallas_call x2, Pallas kernels, respond(): pl.pallas_call(functools.partial(response_kernel, owners, ranks, records)...  1.63 us
  transfers between devices with their start and end apart: 7, of which 2 were waited for; matrix products, arithmetic and copies ran while one was open for 0% of the time, Pallas kernels for 20%

profile of v7, /device:TPU:0, one launch (start us, length us, event | category | flops | bytes accessed | tf_op | source)
XLA Modules:
  0.0 44.8 jit_solution(146482023032532363)
XLA Ops:
  0.6 2.1 %prepare.1 = (bf16[38,32,128]{2,1,0:T(8,128)(2,1)}, bf16[38,32,128]{2,1,0:T(8,128)(2,1)}, f32[9,4,4,128]{3,2,1,0:T(4,128)}, bf16[38,4,128]{2,1,0:T(4,128)(2,1)}, bf16[38,4,128]{2,1,0:T(4,128)(2,1)}) custom-call(f32[1,3,4,32,128]{4,3,2,1,0:T(8,128)} %refs_0_.3, f32[1,3,4,32,128]{4,3,2,1,0:T(8,128)} %refs_1_.3, f32[4,32,128]{2,1,0:T(8,128)} %refs_2_.3, ...), custom_call_target="tpu_custom_call" | custom-call | tf_op jit(solution)/shard_map/prepare/pallas_call | solution.py:202
  2.8 3.1 %collective-permute-start = (bf16[38,32,128]{2,1,0:T(8,128)(2,1)}, bf16[38,32,128]{2,1,0:T(8,128)(2,1)S(1)}, u32[]{:S(2)}, u32[]{:S(2)}) collective-permute-start(bf16[38,32,128]{2,1,0:T(8,128)(2,1)} %get-tuple-element.22), channel_id=1, source_target_pairs={{0,4},{2,6},{4,0},{6,2},{8,12},{10,14},{12,8},{14,10},{1,5},{3,7},... | collective-permute-start | bytes 933896 | tf_op jit(solution)/shard_map/ppermute | solution.py:410
  5.9 0.7 %collective-permute-start.1 = (bf16[38,32,128]{2,1,0:T(8,128)(2,1)}, bf16[38,32,128]{2,1,0:T(8,128)(2,1)S(1)}, u32[]{:S(2)}, u32[]{:S(2)}) collective-permute-start(bf16[38,32,128]{2,1,0:T(8,128)(2,1)} %get-tuple-element.23), channel_id=1, source_target_pairs={{4,8},{6,10},{8,4},{10,6},{5,9},{7,11},{9,5},{11,7},{20,24},{22,26... | collective-permute-start | bytes 933896 | tf_op jit(solution)/shard_map/ppermute | solution.py:410
  6.6 1.6 %collective-permute-start.2 = (f32[9,4,4,128]{3,2,1,0:T(4,128)}, f32[9,4,4,128]{3,2,1,0:T(4,128)S(1)}, u32[]{:S(2)}, u32[]{:S(2)}) collective-permute-start(f32[9,4,4,128]{3,2,1,0:T(4,128)} %get-tuple-element.24), channel_id=1, source_target_pairs={{0,2},{2,0},{4,6},{6,4},{8,10},{10,8},{12,14},{14,12},{1,3},{3,1},... | collective-permute-start | bytes 221192 | tf_op jit(solution)/shard_map/ppermute | solution.py:410
  8.1 4.3 %collective-permute-start.3 = (bf16[38,4,128]{2,1,0:T(4,128)(2,1)}, bf16[38,4,128]{2,1,0:T(4,128)(2,1)S(1)}, u32[]{:S(2)}, u32[]{:S(2)}) collective-permute-start(bf16[38,4,128]{2,1,0:T(4,128)(2,1)} %get-tuple-element.25), channel_id=1, source_target_pairs={{0,6},{2,4},{4,2},{6,0},{8,14},{10,12},{12,10},{14,8},{1,7},{3,5},... | collective-permute-start | bytes 116744 | tf_op jit(solution)/shard_map/ppermute | solution.py:410
  12.5 0.7 %collective-permute-start.4 = (bf16[38,4,128]{2,1,0:T(4,128)(2,1)}, bf16[38,4,128]{2,1,0:T(4,128)(2,1)S(1)}, u32[]{:S(2)}, u32[]{:S(2)}) collective-permute-start(bf16[38,4,128]{2,1,0:T(4,128)(2,1)} %get-tuple-element.26), channel_id=1, source_target_pairs={{4,10},{6,8},{8,6},{10,4},{5,11},{7,9},{9,7},{11,5},{20,26},{22,24... | collective-permute-start | bytes 116744 | tf_op jit(solution)/shard_map/ppermute | solution.py:410
  13.1 2.4 %pack.1 = bf16[8,200,128]{2,1,0:T(8,128)(2,1)} custom-call(s32[16,16]{1,0:T(8,128)} %tiles_ref.1, s32[16,16]{1,0:T(8,128)} %offsets_ref.1, bf16[16,6,16,128]{3,2,1,0:T(8,128)(2,1)} %bitcast.7), custom_call_target="tpu_custom_call" | custom-call | tf_op jit(solution)/shard_map/pack/pallas_call | solution.py:80
  15.5 0.0 copy-start
  15.5 0.0 copy-start.1
  15.5 0.0 copy-start.2
  15.5 0.0 copy-start.3
  15.5 0.0 copy-start.4
  15.5 5.1 %all-to-all-start = ((bf16[8,200,128]{2,1,0:T(8,128)(2,1)}), bf16[8,200,128]{2,1,0:T(8,128)(2,1)S(1)}, u32[]{:S(2)}, u32[]{:S(2)}) async-start(bf16[8,200,128]{2,1,0:T(8,128)(2,1)} %pack.1), calls=%async_computation | async-start | bytes 819200 | tf_op jit(solution)/shard_map/all_to_all | solution.py:433
  20.6 0.0 collective-permute-done.3.refs_8_
  20.6 0.0 collective-permute-done.4.refs_9_
  20.6 0.0 collective-permute-done.2.refs_7_
  20.6 0.0 collective-permute-done.refs_5_
  20.6 0.0 collective-permute-done.1.refs_6_
  20.7 0.0 copy-done
  20.7 0.0 copy-done.1
  20.7 0.0 copy-done.2
  20.7 0.0 copy-done.3
  20.7 0.0 copy-done.4
  20.7 5.8 %stencil.1 = (f32[1,3,4,32,128]{4,3,2,1,0:T(8,128)}, bf16[512,768]{1,0:T(8,128)(2,1)S(1)}) custom-call(f32[1,3,4,32,128]{4,3,2,1,0:T(8,128)S(1)} %copy-done, f32[1,3,4,32,128]{4,3,2,1,0:T(8,128)S(1)} %copy-done.1, f32[4,32,128]{2,1,0:T(8,128)S(1)} %copy-done.2, f32[4,32,128]{2,1,0:T(8,128)S(1)} %copy-done.3, f32[4,32,128]{2,1,0:T(8,128)S(1)} %copy-done.4, ...), custom_call_target="tpu_custom_call" | custom-call | flops 10000000000 | bytes 100000000 | tf_op jit(solution)/shard_map/stencil/pallas_call | solution.py:311
  26.5 5.0 %all-to-all-done.refs_0_ = bf16[8,200,128]{2,1,0:T(8,128)(2,1)S(1)} async-done(((bf16[8,200,128]{2,1,0:T(8,128)(2,1)}), bf16[8,200,128]{2,1,0:T(8,128)(2,1)S(1)}, u32[]{:S(2)}, u32[]{:S(2)}) %all-to-all-start) | async-done | bytes 409632 | tf_op jit(solution)/shard_map/all_to_all | solution.py:433
  31.5 0.0 copy-start.5
  31.5 0.0 collective-permute-start.5
  31.5 0.7 %copy-done.5 = s32[128]{0:T(128)S(1)} copy-done((s32[128]{0:T(128)S(1)}, s32[128]{0:T(128)}, u32[]{:S(2)}) %copy-start.5) | copy-done | bytes 536
  32.2 0.8 %respond.2.refs_1_ = f32[8,4,16]{2,1,0:T(4,128)S(1)} custom-call(bf16[512,768]{1,0:T(8,128)(2,1)S(1)} %get-tuple-element.30.strain_ref, s32[1,128]{1,0:T(1,128)S(1)} %bitcast.5, bf16[8,200,128]{2,1,0:T(8,128)(2,1)S(1)} %all-to-all-done.refs_0_), custom_call_target="tpu_custom_call" | custom-call | tf_op jit(solution)/shard_map/respond/pallas_call | solution.py:386
  33.0 0.3 collective-permute-done.5.refs_0_
  33.3 0.8 %respond.3 = f32[8,4,16]{2,1,0:T(4,128)S(1)} custom-call(bf16[512,768]{1,0:T(8,128)(2,1)S(1)} %get-tuple-element.30.strain_ref, s32[1,128]{1,0:T(1,128)S(1)} %bitcast.6, bf16[8,200,128]{2,1,0:T(8,128)(2,1)S(1)} %collective-permute-done.5.refs_0_, f32[8,4,16]{2,1,0:T(4,128)S(1)} %respond.2.refs_1_), custom_call_target="tpu_custom_call" | custom-call | tf_op jit(solution)/shard_map/respond/pallas_call | solution.py:386
  34.1 10.1 %all_to_all.10 = f32[8,4,16]{2,1,0:T(4,128)S(1)} all-to-all(f32[8,4,16]{2,1,0:T(4,128)S(1)} %respond.3), channel_id=1, replica_groups=mesh['site'=2,'gx'=4,'gy'=2,'comp'=2] {'gx','gy'}, dimensions={0} | all-to-all | bytes 4096 | tf_op jit(solution)/shard_map/all_to_all | solution.py:441
  44.2 0.6 %reduce_sum.9 = f32[4,16]{1,0:T(4,128)} reduce(f32[8,4,16]{2,1,0:T(4,128)S(1)} %all_to_all.10, f32[]{:T(128)} %constant.0.clone.1), dimensions={0}, to_apply=%region_0.0 | reduce | flops 448 | bytes 2308 | tf_op jit(solution)/shard_map/reduce_sum | solution.py:442
Async XLA Ops:
  2.8 17.8 %collective-permute-start = (bf16[38,32,128]{2,1,0:T(8,128)(2,1)}, bf16[38,32,128]{2,1,0:T(8,128)(2,1)S(1)}, u32[]{:S(2)}, u32[]{:S(2)}) collective-permute-start(bf16[38,32,128]{2,1,0:T(8,128)(2,1)} %get-tuple-element.22), channel_id=1, source_target_pairs={{0,4},{2,6},{4,0},{6,2},{8,12},{10,14},{12,8},{14,10},{1,5},{3,7},... | collective-permute-start | bytes 933896 | tf_op jit(solution)/shard_map/ppermute | solution.py:410
  5.9 14.8 %collective-permute-start.1 = (bf16[38,32,128]{2,1,0:T(8,128)(2,1)}, bf16[38,32,128]{2,1,0:T(8,128)(2,1)S(1)}, u32[]{:S(2)}, u32[]{:S(2)}) collective-permute-start(bf16[38,32,128]{2,1,0:T(8,128)(2,1)} %get-tuple-element.23), channel_id=1, source_target_pairs={{4,8},{6,10},{8,4},{10,6},{5,9},{7,11},{9,5},{11,7},{20,24},{22,26... | collective-permute-start | bytes 933896 | tf_op jit(solution)/shard_map/ppermute | solution.py:410
  6.6 14.1 %collective-permute-start.2 = (f32[9,4,4,128]{3,2,1,0:T(4,128)}, f32[9,4,4,128]{3,2,1,0:T(4,128)S(1)}, u32[]{:S(2)}, u32[]{:S(2)}) collective-permute-start(f32[9,4,4,128]{3,2,1,0:T(4,128)} %get-tuple-element.24), channel_id=1, source_target_pairs={{0,2},{2,0},{4,6},{6,4},{8,10},{10,8},{12,14},{14,12},{1,3},{3,1},... | collective-permute-start | bytes 221192 | tf_op jit(solution)/shard_map/ppermute | solution.py:410
  8.1 12.5 %collective-permute-start.3 = (bf16[38,4,128]{2,1,0:T(4,128)(2,1)}, bf16[38,4,128]{2,1,0:T(4,128)(2,1)S(1)}, u32[]{:S(2)}, u32[]{:S(2)}) collective-permute-start(bf16[38,4,128]{2,1,0:T(4,128)(2,1)} %get-tuple-element.25), channel_id=1, source_target_pairs={{0,6},{2,4},{4,2},{6,0},{8,14},{10,12},{12,10},{14,8},{1,7},{3,5},... | collective-permute-start | bytes 116744 | tf_op jit(solution)/shard_map/ppermute | solution.py:410
  12.5 8.2 %collective-permute-start.4 = (bf16[38,4,128]{2,1,0:T(4,128)(2,1)}, bf16[38,4,128]{2,1,0:T(4,128)(2,1)S(1)}, u32[]{:S(2)}, u32[]{:S(2)}) collective-permute-start(bf16[38,4,128]{2,1,0:T(4,128)(2,1)} %get-tuple-element.26), channel_id=1, source_target_pairs={{4,10},{6,8},{8,6},{10,4},{5,11},{7,9},{9,7},{11,5},{20,26},{22,24... | collective-permute-start | bytes 116744 | tf_op jit(solution)/shard_map/ppermute | solution.py:410
  15.5 5.1 %copy-start = (f32[1,3,4,32,128]{4,3,2,1,0:T(8,128)S(1)}, f32[1,3,4,32,128]{4,3,2,1,0:T(8,128)}, u32[]{:S(2)}) copy-start(f32[1,3,4,32,128]{4,3,2,1,0:T(8,128)} %refs_0_.3) | copy-start | bytes 589828
  15.5 5.1 %copy-start.1 = (f32[1,3,4,32,128]{4,3,2,1,0:T(8,128)S(1)}, f32[1,3,4,32,128]{4,3,2,1,0:T(8,128)}, u32[]{:S(2)}) copy-start(f32[1,3,4,32,128]{4,3,2,1,0:T(8,128)} %refs_1_.3) | copy-start | bytes 589828
  15.5 5.2 %copy-start.2 = (f32[4,32,128]{2,1,0:T(8,128)S(1)}, f32[4,32,128]{2,1,0:T(8,128)}, u32[]{:S(2)}) copy-start(f32[4,32,128]{2,1,0:T(8,128)} %refs_2_.3) | copy-start | bytes 196612
  15.5 5.2 %copy-start.3 = (f32[4,32,128]{2,1,0:T(8,128)S(1)}, f32[4,32,128]{2,1,0:T(8,128)}, u32[]{:S(2)}) copy-start(f32[4,32,128]{2,1,0:T(8,128)} %refs_3_.3) | copy-start | bytes 196612
  15.5 5.2 %copy-start.4 = (f32[4,32,128]{2,1,0:T(8,128)S(1)}, f32[4,32,128]{2,1,0:T(8,128)}, u32[]{:S(2)}) copy-start(f32[4,32,128]{2,1,0:T(8,128)} %refs_4_.3) | copy-start | bytes 196612
  15.5 16.0 %all-to-all-start = ((bf16[8,200,128]{2,1,0:T(8,128)(2,1)}), bf16[8,200,128]{2,1,0:T(8,128)(2,1)S(1)}, u32[]{:S(2)}, u32[]{:S(2)}) async-start(bf16[8,200,128]{2,1,0:T(8,128)(2,1)} %pack.1), calls=%async_computation | async-start | bytes 819200 | tf_op jit(solution)/shard_map/all_to_all | solution.py:433
  31.5 0.7 %copy-start.5 = (s32[128]{0:T(128)S(1)}, s32[128]{0:T(128)}, u32[]{:S(2)}) copy-start(s32[128]{0:T(128)} %param.14) | copy-start | bytes 1540
  31.5 1.7 %collective-permute-start.5 = (bf16[8,200,128]{2,1,0:T(8,128)(2,1)S(1)}, bf16[8,200,128]{2,1,0:T(8,128)(2,1)S(1)}, u32[]{:S(2)}, u32[]{:S(2)}) collective-permute-start(bf16[8,200,128]{2,1,0:T(8,128)(2,1)S(1)} %all-to-all-done.refs_0_), channel_id=1, source_target_pairs={{0,1},{1,0},{2,3},{3,2},{4,5},{5,4},{6,7},{7,6},{8,9},{9,8},{10,11... | collective-permute-start | bytes 1228808 | tf_op jit(solution)/shard_map/ppermute | solution.py:437

commit v8 on v7

--- a/solution.py
+++ b/solution.py
@@ -24,7 +24,7 @@
     return lax.axis_index("gx") * lax.axis_size("gy") + lax.axis_index("gy")
 
 
-def pack_kernel(owners, slots, ranks, tiles_ref, offsets_ref, panels_ref, out_ref, meta_ref=None):
+def pack_kernel(owners, slots, ranks, tiles_ref, offsets_ref, panels_ref, arrive, out_ref, meta_ref=None):
     rows, cols = tiles_ref.shape
     entries = rows * cols
     core = lax.axis_index("comp")
@@ -51,6 +51,7 @@
     blocks = out_ref.shape[0]
     length = sent // blocks
     components = panels_ref.shape[1]
+    arrive()
     for i in range(components):
         part = jnp.dot(select, panels_ref[:, i].reshape(entries, LANES), preferred_element_type=jnp.float32).astype(jnp.bfloat16)
         out_ref[:, i * length : (i + 1) * length, :] = part.reshape(blocks, length, LANES)
@@ -70,33 +71,6 @@
 
 
 META_ROWS = 8
-
-
-def pack(owners, slots, ranks, tiles, offsets, panels):
-    components = panels.shape[1]
-    vmem = pl.BlockSpec(memory_space=pltpu.VMEM)
-    kernel = functools.partial(pack_kernel, owners, slots, ranks)
-    if ranks % 16 == 0:
-        return pl.pallas_call(
-            kernel,
-            out_shape=jax.ShapeDtypeStruct((owners, components * ranks + META_ROWS, LANES), jnp.bfloat16),
-            in_specs=[vmem] * 3,
-            out_specs=vmem,
-            name="pack",
-        )(tiles, offsets, panels)
-    body, meta = pl.pallas_call(
-        kernel,
-        out_shape=(
-            jax.ShapeDtypeStruct((1, components * owners * ranks, LANES), jnp.bfloat16),
-            jax.ShapeDtypeStruct((2, owners, LANES), jnp.bfloat16),
-        ),
-        in_specs=[vmem] * 3,
-        out_specs=(vmem, vmem),
-        name="pack",
-    )(tiles, offsets, panels)
-    body = body.reshape(components, owners, ranks, LANES).transpose(1, 0, 2, 3)
-    body = body.reshape(owners, components * ranks, LANES)
-    return jnp.concatenate([body, meta.transpose(1, 0, 2)], axis=1)
 
 
 def unpack(owners, ranks, components, arrived):
@@ -155,21 +129,8 @@
             write(field, k, value)
 
 
-def prepare_kernel(halo, *refs):
-    disp, prev, lam, mu, buoy = refs[:5]
-    outs, fields, sem = refs[5:-2], refs[-2], refs[-1]
-    nx, ny, nz = lam.shape
-    copies = [
-        pltpu.make_async_copy(disp.at[0], fields.at[pl.ds(0, 3)], sem.at[0]),
-        pltpu.make_async_copy(prev.at[0], fields.at[pl.ds(3, 3)], sem.at[1]),
-        pltpu.make_async_copy(lam, fields.at[6], sem.at[2]),
-        pltpu.make_async_copy(mu, fields.at[7], sem.at[3]),
-        pltpu.make_async_copy(buoy, fields.at[8], sem.at[4]),
-    ]
-    for copy in copies:
-        copy.start()
-    for copy in copies:
-        copy.wait()
+def prepare_kernel(halo, fields, *outs):
+    _, nx, ny, nz = fields.shape
     odd_x, odd_y = lax.axis_index("gx") % 2, lax.axis_index("gy") % 2
 
     def coded(p, rows, target):
@@ -192,21 +153,64 @@
             pl.when(odd_y != q)(functools.partial(edge, pl.ds(0, halo), targets))
 
 
-def prepare(halo, ways, disp, prev, lam, mu, buoy):
-    nx, ny, nz = lam.shape
-    vmem, anywhere = pl.BlockSpec(memory_space=pltpu.VMEM), pl.BlockSpec(memory_space=pl.ANY)
-    count = coded_planes(halo)
+def opening_kernel(halo, owners, slots, ranks, sides, *refs):
+    disp, prev, lam, mu, buoy, tiles, offsets, panels = refs[:8]
+    fields, own_tiles, own_offsets, own_panels, sem = refs[-5:]
+    outs = refs[8:-5]
+    pairs = (
+        (tiles, own_tiles),
+        (offsets, own_offsets),
+        (panels, own_panels),
+        (disp.at[0], fields.at[pl.ds(0, 3)]),
+        (prev.at[0], fields.at[pl.ds(3, 3)]),
+        (lam, fields.at[6]),
+        (mu, fields.at[7]),
+        (buoy, fields.at[8]),
+    )
+    copies = [pltpu.make_async_copy(source, target, sem.at[i]) for i, (source, target) in enumerate(pairs)]
+    for copy in copies:
+        copy.start()
+    copies[0].wait()
+    copies[1].wait()
+    pack_kernel(owners, slots, ranks, own_tiles, own_offsets, own_panels, copies[2].wait, *outs[sides:])
+    for copy in copies[3:]:
+        copy.wait()
+    prepare_kernel(halo, fields, *outs[:sides])
+
+
+def opening(halo, ways, owners, slots, ranks, waves, tiles, offsets, panels):
+    nx, ny, nz = waves[2].shape
+    vmem, anywhere = pl.BlockSpec(memory_space=pltpu.VMEM), pl.BlockSpec(memory_space=pltpu.HBM)
+    count, components, sent = coded_planes(halo), panels.shape[1], owners * ranks
     edge = [jax.ShapeDtypeStruct((FIELDS, nx, halo, nz), jnp.float32)]
     edge += [jax.ShapeDtypeStruct((count, halo, nz), jnp.bfloat16)] * 2
     shapes = [jax.ShapeDtypeStruct((count, ny, nz), jnp.bfloat16)] * 2 + edge * ways
-    return pl.pallas_call(
-        functools.partial(prepare_kernel, halo),
+    sides = len(shapes)
+    if ranks % 16 == 0:
+        shapes.append(jax.ShapeDtypeStruct((owners, components * ranks + META_ROWS, LANES), jnp.bfloat16))
+    else:
+        shapes.append(jax.ShapeDtypeStruct((1, components * sent, LANES), jnp.bfloat16))
+        shapes.append(jax.ShapeDtypeStruct((2, owners, LANES), jnp.bfloat16))
+    outs = pl.pallas_call(
+        functools.partial(opening_kernel, halo, owners, slots, ranks, sides),
         out_shape=shapes,
-        in_specs=[anywhere] * 5,
+        in_specs=[anywhere] * 8,
         out_specs=[vmem] * len(shapes),
-        scratch_shapes=[pltpu.VMEM((FIELDS, nx, ny, nz), jnp.float32), pltpu.SemaphoreType.DMA((5,))],
-        name="prepare",
-    )(disp, prev, lam, mu, buoy)
+        scratch_shapes=[
+            pltpu.VMEM((FIELDS, nx, ny, nz), jnp.float32),
+            pltpu.VMEM(tiles.shape, jnp.int32),
+            pltpu.VMEM(offsets.shape, jnp.int32),
+            pltpu.VMEM(panels.shape, jnp.bfloat16),
+            pltpu.SemaphoreType.DMA((8,)),
+        ],
+        name="opening",
+    )(*waves, tiles, offsets, panels)
+    if ranks % 16 == 0:
+        return outs[:sides], outs[sides]
+    body, meta = outs[sides:]
+    body = body.reshape(components, owners, ranks, LANES).transpose(1, 0, 2, 3)
+    body = body.reshape(owners, components * ranks, LANES)
+    return outs[:sides], jnp.concatenate([body, meta.transpose(1, 0, 2)], axis=1)
 
 
 def shifted_up(value, dim):
@@ -423,13 +427,13 @@
 
     waves = (displacement, previous, first_lame, shear_modulus, buoyancy)
     turns_y = range(1 if gys == 2 else 2)
-    sent = prepare(halo, len(turns_y), *waves)
+    panels = slip_panels.transpose(0, 2, 1, 3)
+    sent, payload = opening(
+        halo, len(turns_y), owners, slots, ranks, waves, rupture_tiles, slip_offsets, panels
+    )
     ways = [(0, None), (1, None)] + [(x, q) for q in turns_y for x in (None, 0, 1)]
-    slip_panels, sent = lax.optimization_barrier((slip_panels, sent))
     halos = [exchange(value, gxs, gys, *way) for value, way in zip(sent, ways)]
 
-    panels = slip_panels.transpose(0, 2, 1, 3)
-    payload = pack(owners, slots, ranks, rupture_tiles, slip_offsets, panels)
     arrived = lax.all_to_all(payload, OWNERS_AXES, split_axis=0, concat_axis=0, tiled=True)
 
     final, strain = stencil(halo, *waves, halos)

time: 45.1 us -> 43.2 us (0.958)
  Pallas kernels: 12 us -> 10.1 us
    pallas_call x2 -> x1, Pallas kernels: 4.55 us -> 2.63 us  [opening(): pl.pallas_call(functools.partial(opening_kernel, halo, owners, slots, ran...]
  transfers between devices with their start and end apart: 7 -> 7, of which waited for: 2 -> 2; matrix products, arithmetic and copies ran while one was open for 0% -> 0% of each run, Pallas kernels for 20% -> 16%
where the time goes in v8:
time: 43.2 us; the launch traced here: 42.9 us
  starting transfers between devices  15.4 us (36%)
  Pallas kernels  10.1 us (23%)
  blocking collectives  10.1 us (23%)
  waiting for transfers between devices  5.26 us (12%)
  between operations  0.77 us (2%)
  local copies, waits for them, and re-layouts  0.68 us (2%)
  other arithmetic  0.6 us (1%)
    ppermute x5, starting transfers between devices, exchange(): return lax.ppermute(value, OWNERS_AXES, pairs)  10.3 us
    all_to_all x1, blocking collectives, body(): lax.all_to_all(partial, OWNERS_AXES, split_axis=0, concat_axis=0, tiled=T...  10.1 us
    pallas_call x1, Pallas kernels, stencil(): pl.pallas_call(functools.partial(stencil_kernel, halo), out_shape=(jax.Sh...  5.84 us
    all_to_all x1, starting transfers between devices, body(): lax.all_to_all(payload, OWNERS_AXES, split_axis=0, concat_axis=0, tiled=T...  5.06 us
    all_to_all x1, waiting for transfers between devices, body(): lax.all_to_all(payload, OWNERS_AXES, split_axis=0, concat_axis=0, tiled=T...  4.97 us
    pallas_call x1, Pallas kernels, opening(): pl.pallas_call(functools.partial(opening_kernel, halo, owners, slots, ran...  2.63 us
    pallas_call x2, Pallas kernels, respond(): pl.pallas_call(functools.partial(response_kernel, owners, ranks, records)...  1.63 us
  transfers between devices with their start and end apart: 7, of which 2 were waited for; matrix products, arithmetic and copies ran while one was open for 0% of the time, Pallas kernels for 16%

profile of v8, /device:TPU:0, one launch (start us, length us, event | category | flops | bytes accessed | tf_op | source)
XLA Modules:
  0.0 42.9 jit_solution(7879277085852209646)
XLA Ops:
  0.6 2.6 %opening.1 = (bf16[38,32,128]{2,1,0:T(8,128)(2,1)}, bf16[38,32,128]{2,1,0:T(8,128)(2,1)}, f32[9,4,4,128]{3,2,1,0:T(4,128)}, bf16[38,4,128]{2,1,0:T(4,128)(2,1)},...) custom-call(f32[1,3,4,32,128]{4,3,2,1,0:T(8,128)} %refs_0_.3, f32[1,3,4,32,128]{4,3,2,1,0:T(8,128)} %refs_1_.3, ...), custom_call_target="tpu_custom_call" | custom-call | tf_op jit(solution)/shard_map/opening/pallas_call | solution.py:194
  3.3 3.1 %collective-permute-start = (bf16[38,32,128]{2,1,0:T(8,128)(2,1)}, bf16[38,32,128]{2,1,0:T(8,128)(2,1)S(1)}, u32[]{:S(2)}, u32[]{:S(2)}) collective-permute-start(bf16[38,32,128]{2,1,0:T(8,128)(2,1)} %get-tuple-element.12), channel_id=1, source_target_pairs={{0,4},{2,6},{4,0},{6,2},{8,12},{10,14},{12,8},{14,10},{1,5},{3,7},... | collective-permute-start | bytes 933896 | tf_op jit(solution)/shard_map/ppermute | solution.py:414
  6.4 0.7 %collective-permute-start.1 = (bf16[38,32,128]{2,1,0:T(8,128)(2,1)}, bf16[38,32,128]{2,1,0:T(8,128)(2,1)S(1)}, u32[]{:S(2)}, u32[]{:S(2)}) collective-permute-start(bf16[38,32,128]{2,1,0:T(8,128)(2,1)} %get-tuple-element.13), channel_id=1, source_target_pairs={{4,8},{6,10},{8,4},{10,6},{5,9},{7,11},{9,5},{11,7},{20,24},{22,26... | collective-permute-start | bytes 933896 | tf_op jit(solution)/shard_map/ppermute | solution.py:414
  7.0 1.6 %collective-permute-start.2 = (f32[9,4,4,128]{3,2,1,0:T(4,128)}, f32[9,4,4,128]{3,2,1,0:T(4,128)S(1)}, u32[]{:S(2)}, u32[]{:S(2)}) collective-permute-start(f32[9,4,4,128]{3,2,1,0:T(4,128)} %get-tuple-element.14), channel_id=1, source_target_pairs={{0,2},{2,0},{4,6},{6,4},{8,10},{10,8},{12,14},{14,12},{1,3},{3,1},... | collective-permute-start | bytes 221192 | tf_op jit(solution)/shard_map/ppermute | solution.py:414
  8.6 4.4 %collective-permute-start.3 = (bf16[38,4,128]{2,1,0:T(4,128)(2,1)}, bf16[38,4,128]{2,1,0:T(4,128)(2,1)S(1)}, u32[]{:S(2)}, u32[]{:S(2)}) collective-permute-start(bf16[38,4,128]{2,1,0:T(4,128)(2,1)} %get-tuple-element.15), channel_id=1, source_target_pairs={{0,6},{2,4},{4,2},{6,0},{8,14},{10,12},{12,10},{14,8},{1,7},{3,5},... | collective-permute-start | bytes 116744 | tf_op jit(solution)/shard_map/ppermute | solution.py:414
  12.9 0.7 %collective-permute-start.4 = (bf16[38,4,128]{2,1,0:T(4,128)(2,1)}, bf16[38,4,128]{2,1,0:T(4,128)(2,1)S(1)}, u32[]{:S(2)}, u32[]{:S(2)}) collective-permute-start(bf16[38,4,128]{2,1,0:T(4,128)(2,1)} %get-tuple-element.16), channel_id=1, source_target_pairs={{4,10},{6,8},{8,6},{10,4},{5,11},{7,9},{9,7},{11,5},{20,26},{22,24... | collective-permute-start | bytes 116744 | tf_op jit(solution)/shard_map/ppermute | solution.py:414
  13.6 0.0 copy-start
  13.6 0.0 copy-start.1
  13.6 0.0 copy-start.2
  13.6 0.0 copy-start.3
  13.7 0.0 copy-start.4
  13.7 5.1 %all-to-all-start = ((bf16[8,200,128]{2,1,0:T(8,128)(2,1)}), bf16[8,200,128]{2,1,0:T(8,128)(2,1)S(1)}, u32[]{:S(2)}, u32[]{:S(2)}) async-start(bf16[8,200,128]{2,1,0:T(8,128)(2,1)} %get-tuple-element.18), calls=%async_computation | async-start | bytes 819200 | tf_op jit(solution)/shard_map/all_to_all | solution.py:437
  18.7 0.0 collective-permute-done.3.refs_8_
  18.7 0.0 collective-permute-done.4.refs_9_
  18.7 0.0 collective-permute-done.2.refs_7_
  18.8 0.0 collective-permute-done.refs_5_
  18.8 0.0 collective-permute-done.1.refs_6_
  18.8 0.0 copy-done
  18.8 0.0 copy-done.1
  18.8 0.0 copy-done.2
  18.8 0.0 copy-done.3
  18.8 0.0 copy-done.4
  18.8 5.8 %stencil.1 = (f32[1,3,4,32,128]{4,3,2,1,0:T(8,128)}, bf16[512,768]{1,0:T(8,128)(2,1)S(1)}) custom-call(f32[1,3,4,32,128]{4,3,2,1,0:T(8,128)S(1)} %copy-done, f32[1,3,4,32,128]{4,3,2,1,0:T(8,128)S(1)} %copy-done.1, f32[4,32,128]{2,1,0:T(8,128)S(1)} %copy-done.2, f32[4,32,128]{2,1,0:T(8,128)S(1)} %copy-done.3, f32[4,32,128]{2,1,0:T(8,128)S(1)} %copy-done.4, ...), custom_call_target="tpu_custom_call" | custom-call | flops 10000000000 | bytes 100000000 | tf_op jit(solution)/shard_map/stencil/pallas_call | solution.py:315
  24.7 5.0 %all-to-all-done.refs_0_ = bf16[8,200,128]{2,1,0:T(8,128)(2,1)S(1)} async-done(((bf16[8,200,128]{2,1,0:T(8,128)(2,1)}), bf16[8,200,128]{2,1,0:T(8,128)(2,1)S(1)}, u32[]{:S(2)}, u32[]{:S(2)}) %all-to-all-start) | async-done | bytes 409632 | tf_op jit(solution)/shard_map/all_to_all | solution.py:437
  29.6 0.0 copy-start.5
  29.6 0.0 collective-permute-start.5
  29.6 0.7 %copy-done.5 = s32[128]{0:T(128)S(1)} copy-done((s32[128]{0:T(128)S(1)}, s32[128]{0:T(128)}, u32[]{:S(2)}) %copy-start.5) | copy-done | bytes 536
  30.3 0.8 %respond.2.refs_1_ = f32[8,4,16]{2,1,0:T(4,128)S(1)} custom-call(bf16[512,768]{1,0:T(8,128)(2,1)S(1)} %get-tuple-element.20.strain_ref, s32[1,128]{1,0:T(1,128)S(1)} %bitcast.5, bf16[8,200,128]{2,1,0:T(8,128)(2,1)S(1)} %all-to-all-done.refs_0_), custom_call_target="tpu_custom_call" | custom-call | tf_op jit(solution)/shard_map/respond/pallas_call | solution.py:390
  31.1 0.3 collective-permute-done.5.refs_0_
  31.4 0.8 %respond.3 = f32[8,4,16]{2,1,0:T(4,128)S(1)} custom-call(bf16[512,768]{1,0:T(8,128)(2,1)S(1)} %get-tuple-element.20.strain_ref, s32[1,128]{1,0:T(1,128)S(1)} %bitcast.6, bf16[8,200,128]{2,1,0:T(8,128)(2,1)S(1)} %collective-permute-done.5.refs_0_, f32[8,4,16]{2,1,0:T(4,128)S(1)} %respond.2.refs_1_), custom_call_target="tpu_custom_call" | custom-call | tf_op jit(solution)/shard_map/respond/pallas_call | solution.py:390
  32.2 10.1 %all_to_all.10 = f32[8,4,16]{2,1,0:T(4,128)S(1)} all-to-all(f32[8,4,16]{2,1,0:T(4,128)S(1)} %respond.3), channel_id=1, replica_groups=mesh['site'=2,'gx'=4,'gy'=2,'comp'=2] {'gx','gy'}, dimensions={0} | all-to-all | bytes 4096 | tf_op jit(solution)/shard_map/all_to_all | solution.py:445
  42.3 0.6 %reduce_sum.9 = f32[4,16]{1,0:T(4,128)} reduce(f32[8,4,16]{2,1,0:T(4,128)S(1)} %all_to_all.10, f32[]{:T(128)} %constant.0.clone.1), dimensions={0}, to_apply=%region_0.0 | reduce | flops 448 | bytes 2308 | tf_op jit(solution)/shard_map/reduce_sum | solution.py:446
Async XLA Ops:
  3.3 15.5 %collective-permute-start = (bf16[38,32,128]{2,1,0:T(8,128)(2,1)}, bf16[38,32,128]{2,1,0:T(8,128)(2,1)S(1)}, u32[]{:S(2)}, u32[]{:S(2)}) collective-permute-start(bf16[38,32,128]{2,1,0:T(8,128)(2,1)} %get-tuple-element.12), channel_id=1, source_target_pairs={{0,4},{2,6},{4,0},{6,2},{8,12},{10,14},{12,8},{14,10},{1,5},{3,7},... | collective-permute-start | bytes 933896 | tf_op jit(solution)/shard_map/ppermute | solution.py:414
  6.4 12.4 %collective-permute-start.1 = (bf16[38,32,128]{2,1,0:T(8,128)(2,1)}, bf16[38,32,128]{2,1,0:T(8,128)(2,1)S(1)}, u32[]{:S(2)}, u32[]{:S(2)}) collective-permute-start(bf16[38,32,128]{2,1,0:T(8,128)(2,1)} %get-tuple-element.13), channel_id=1, source_target_pairs={{4,8},{6,10},{8,4},{10,6},{5,9},{7,11},{9,5},{11,7},{20,24},{22,26... | collective-permute-start | bytes 933896 | tf_op jit(solution)/shard_map/ppermute | solution.py:414
  7.0 11.7 %collective-permute-start.2 = (f32[9,4,4,128]{3,2,1,0:T(4,128)}, f32[9,4,4,128]{3,2,1,0:T(4,128)S(1)}, u32[]{:S(2)}, u32[]{:S(2)}) collective-permute-start(f32[9,4,4,128]{3,2,1,0:T(4,128)} %get-tuple-element.14), channel_id=1, source_target_pairs={{0,2},{2,0},{4,6},{6,4},{8,10},{10,8},{12,14},{14,12},{1,3},{3,1},... | collective-permute-start | bytes 221192 | tf_op jit(solution)/shard_map/ppermute | solution.py:414
  8.6 10.1 %collective-permute-start.3 = (bf16[38,4,128]{2,1,0:T(4,128)(2,1)}, bf16[38,4,128]{2,1,0:T(4,128)(2,1)S(1)}, u32[]{:S(2)}, u32[]{:S(2)}) collective-permute-start(bf16[38,4,128]{2,1,0:T(4,128)(2,1)} %get-tuple-element.15), channel_id=1, source_target_pairs={{0,6},{2,4},{4,2},{6,0},{8,14},{10,12},{12,10},{14,8},{1,7},{3,5},... | collective-permute-start | bytes 116744 | tf_op jit(solution)/shard_map/ppermute | solution.py:414
  12.9 5.8 %collective-permute-start.4 = (bf16[38,4,128]{2,1,0:T(4,128)(2,1)}, bf16[38,4,128]{2,1,0:T(4,128)(2,1)S(1)}, u32[]{:S(2)}, u32[]{:S(2)}) collective-permute-start(bf16[38,4,128]{2,1,0:T(4,128)(2,1)} %get-tuple-element.16), channel_id=1, source_target_pairs={{4,10},{6,8},{8,6},{10,4},{5,11},{7,9},{9,7},{11,5},{20,26},{22,24... | collective-permute-start | bytes 116744 | tf_op jit(solution)/shard_map/ppermute | solution.py:414
  13.6 5.2 %copy-start = (f32[1,3,4,32,128]{4,3,2,1,0:T(8,128)S(1)}, f32[1,3,4,32,128]{4,3,2,1,0:T(8,128)}, u32[]{:S(2)}) copy-start(f32[1,3,4,32,128]{4,3,2,1,0:T(8,128)} %refs_0_.3) | copy-start | bytes 589828
  13.6 5.2 %copy-start.1 = (f32[1,3,4,32,128]{4,3,2,1,0:T(8,128)S(1)}, f32[1,3,4,32,128]{4,3,2,1,0:T(8,128)}, u32[]{:S(2)}) copy-start(f32[1,3,4,32,128]{4,3,2,1,0:T(8,128)} %refs_1_.3) | copy-start | bytes 589828
  13.6 5.2 %copy-start.2 = (f32[4,32,128]{2,1,0:T(8,128)S(1)}, f32[4,32,128]{2,1,0:T(8,128)}, u32[]{:S(2)}) copy-start(f32[4,32,128]{2,1,0:T(8,128)} %refs_2_.3) | copy-start | bytes 196612
  13.6 5.2 %copy-start.3 = (f32[4,32,128]{2,1,0:T(8,128)S(1)}, f32[4,32,128]{2,1,0:T(8,128)}, u32[]{:S(2)}) copy-start(f32[4,32,128]{2,1,0:T(8,128)} %refs_3_.3) | copy-start | bytes 196612
  13.7 5.2 %copy-start.4 = (f32[4,32,128]{2,1,0:T(8,128)S(1)}, f32[4,32,128]{2,1,0:T(8,128)}, u32[]{:S(2)}) copy-start(f32[4,32,128]{2,1,0:T(8,128)} %refs_4_.3) | copy-start | bytes 196612
  13.7 16.0 %all-to-all-start = ((bf16[8,200,128]{2,1,0:T(8,128)(2,1)}), bf16[8,200,128]{2,1,0:T(8,128)(2,1)S(1)}, u32[]{:S(2)}, u32[]{:S(2)}) async-start(bf16[8,200,128]{2,1,0:T(8,128)(2,1)} %get-tuple-element.18), calls=%async_computation | async-start | bytes 819200 | tf_op jit(solution)/shard_map/all_to_all | solution.py:437
  29.6 0.7 %copy-start.5 = (s32[128]{0:T(128)S(1)}, s32[128]{0:T(128)}, u32[]{:S(2)}) copy-start(s32[128]{0:T(128)} %param.14) | copy-start | bytes 1540
  29.6 1.7 %collective-permute-start.5 = (bf16[8,200,128]{2,1,0:T(8,128)(2,1)S(1)}, bf16[8,200,128]{2,1,0:T(8,128)(2,1)S(1)}, u32[]{:S(2)}, u32[]{:S(2)}) collective-permute-start(bf16[8,200,128]{2,1,0:T(8,128)(2,1)S(1)} %all-to-all-done.refs_0_), channel_id=1, source_target_pairs={{0,1},{1,0},{2,3},{3,2},{4,5},{5,4},{6,7},{7,6},{8,9},{9,8},{10,11... | collective-permute-start | bytes 1228808 | tf_op jit(solution)/shard_map/ppermute | solution.py:441
